TPU v7x, 32 devices: a whole 2x2x4 slice. The times are simulated.
32 devices in a mesh: rep: 2 (over y), gx: 4 (over z), gy: 4 (over x, core).
Axes of the slice: x: 2, y: 2, z: 4, core: 2. Of those that a mesh axis runs over, the one named last changes fastest.
Arguments:
- positions: float32 [3, 8, 4, 1024], P(None, ('rep', 'gx'), 'gy'), parts along dimension 1, may hold values from 0 to 256, as said below
- charges: float32 [8, 4, 1024], P(('rep', 'gx'), 'gy'), parts along dimension 0, may hold values from -2 to 2
- pair_lists: int32 [8, 4, 4, 4], P(('rep', 'gx'), 'gy'), parts along dimension 0, may hold values from 0 to 35, as said below
- slab_dest: int32 [8, 4, 8], P(('rep', 'gx'), 'gy'), parts along dimension 0, may hold values from 0 to 3, as said below
- atom_counts: int32 [8, 4], P(('rep', 'gx'), 'gy'), parts along dimension 0, may hold values from 512 to 1024, as said below
Outputs:
- short_forces: float32 [3, 8, 4, 1024], P(None, ('rep', 'gx'), 'gy'), parts along dimension 1
- long_forces: float32 [3, 8, 4, 1024], P(None, ('rep', 'gx'), 'gy'), parts along dimension 1
There are 2 independent parts, one for each index of `rep`. A program takes and returns all parts, laid end to end along the dimension named above; each array names one. Nothing has to cross between parts.
Inputs may be any that keep to these rules, and one draw needn't show every extreme that they name: `positions`: the first coordinate lies in [0, 64), the second in [0, 64), and the third in the slab of the atom's block, [s * 32, (s + 1) * 32). `pair_lists`: each list names 4 different clusters of the neighbourhood, the cluster's own, 16 + c for cluster c, first; the others are clusters whose blocks' slabs lie nearest to those of the cluster's own blocks. `slab_dest`: the blocks of a cell name slabs in non-decreasing order; at most 4 blocks of one cell name one slab, and in every cell some slab is named by exactly 4. `atom_counts`: some cell holds 1024 atoms in every draw.
All inputs are finite; a program needn't handle non-finite values.
Results may differ from a plain program's by a relative error of at most 0.0003.
Values sent between devices are 32-bit elements; how exact they have to be, the bound alone decides.
A program may use at most 128 MiB of HBM per device.

v0:
```python
import functools
import math

import jax
import jax.numpy as jnp
import numpy as np
from jax import lax
from jax.experimental import pallas as pl
from jax.experimental.pallas import tpu as pltpu
from jax.sharding import PartitionSpec as P

GRID_X = 256
GRID_Y = 256
GRID_Z = 128


spacing = 0.16
ewald_split = 3.47
cutoff = 0.9
soft_core = 0.09
root_factor = 1.1283791670955126
rows_group = 8


def moved(value, step_x, step_y):
    count_x = lax.axis_size("gx")
    count_y = lax.axis_size("gy")
    pairs = [
        (i * count_y + j, (i + step_x) % count_x * count_y + (j + step_y) % count_y)
        for i in range(count_x)
        for j in range(count_y)
    ]
    return lax.ppermute(value, ("gx", "gy"), pairs)


def round_up(value, multiple):
    return -(-value // multiple) * multiple


def hartley(period):
    turns = np.outer(np.arange(period), np.arange(period)) % period
    phases = turns * (2.0 * np.pi / period)
    return (np.cos(phases) + np.sin(phases)).astype(np.float32)


def halves(value):
    high = value.astype(jnp.bfloat16)
    low = (value - high.astype(jnp.float32)).astype(jnp.bfloat16)
    return (high, low)


def dot(left_side, right_side):
    return jnp.dot(left_side, right_side, preferred_element_type=jnp.float32)


def spline_weights(fraction):
    remain = 1.0 - fraction
    square = fraction * fraction
    cube_part = square * fraction
    values = [
        remain * remain * remain / 6.0,
        (3.0 * cube_part - 6.0 * square + 4.0) / 6.0,
        (-3.0 * cube_part + 3.0 * square + 3.0 * fraction + 1.0) / 6.0,
        cube_part / 6.0,
    ]
    slopes = [
        -0.5 * remain * remain,
        0.5 * (3.0 * square - 4.0 * fraction),
        0.5 * (-3.0 * square + 2.0 * fraction + 1.0),
        0.5 * square,
    ]
    return (values, slopes)


def split_cells(coordinate, offset, cell_count):
    inside = coordinate - offset
    lowest = jnp.clip(jnp.floor(inside).astype(jnp.int32), 0, cell_count - 1)
    return (lowest, inside - lowest.astype(inside.dtype))


def spline_table(lowest, values, table_size, period=None):
    points = lax.broadcasted_iota(jnp.int32, (table_size, lowest.shape[1]), 0)
    lookup = jnp.zeros(points.shape, jnp.float32)
    for spline_term in range(4):
        at = lowest + spline_term
        if period is not None:
            at = jnp.where(at >= period, at - period, at)
        lookup = jnp.where(points == at, values[spline_term], lookup)
    return lookup


def spread_kernel(cells, pad, atoms_ref, base_ref, turn_ref, out_ref, wx_ref, wy_ref, wz_ref, hi_ref, lo_ref):
    cells_x, cells_y, cells_z = cells
    pad_x, pad_y = pad
    atom_total = atoms_ref.shape[1]
    low_x, frac_x = split_cells(atoms_ref[0:1, :], 0.0, cells_x)
    low_y, frac_y = split_cells(atoms_ref[1:2, :], 0.0, cells_y)
    base = base_ref[...]
    low_z, frac_z = split_cells(atoms_ref[2:3, :], base.astype(jnp.float32), cells_z)
    wx_ref[...] = spline_table(low_x, spline_weights(frac_x)[0], pad_x) * atoms_ref[3:4, :]
    wy_ref[...] = spline_table(low_y, spline_weights(frac_y)[0], pad_y)
    turn = turn_ref[...]
    size_z = turn.shape[0]
    table_z = spline_table(base + low_z, spline_weights(frac_z)[0], size_z, size_z)
    waves = jnp.dot(
        turn, table_z, precision=lax.Precision.HIGHEST, preferred_element_type=jnp.float32
    ).T
    high, low = halves(waves)
    wz_ref[:, :size_z] = high
    wz_ref[:, size_z:] = low

    @pl.loop(0, pad_x // rows_group)
    def _(chunk):
        for inner in range(rows_group):
            row = wx_ref[pl.ds(chunk * rows_group + inner, 1), :]
            high, low = halves(row * wy_ref[...])
            hi_ref[pl.ds(inner * pad_y, pad_y), :] = high
            lo_ref[pl.ds(inner * pad_y, pad_y), :] = low
        both = dot(hi_ref[...], wz_ref[...])
        rest = dot(lo_ref[...], wz_ref[:, :size_z])
        total = both[:, :size_z] + both[:, size_z:] + rest
        out_ref[pl.ds(chunk * rows_group, rows_group)] = total.reshape(rows_group, pad_y, size_z)


def gather_kernel(cells, pad, atoms_ref, base_ref, turn_ref, mesh_ref, out_ref, wx_ref, vx_ref, wy_ref, vy_ref, wz_ref, level_ref):
    cells_x, cells_y, cells_z = cells
    pad_x, pad_y = pad
    atom_total = atoms_ref.shape[1]
    low_x, frac_x = split_cells(atoms_ref[0:1, :], 0.0, cells_x)
    low_y, frac_y = split_cells(atoms_ref[1:2, :], 0.0, cells_y)
    base = base_ref[...]
    low_z, frac_z = split_cells(atoms_ref[2:3, :], base.astype(jnp.float32), cells_z)
    values, slopes = spline_weights(frac_x)
    wx_ref[...] = spline_table(low_x, values, pad_x)
    vx_ref[...] = spline_table(low_x, slopes, pad_x)
    values, slopes = spline_weights(frac_y)
    wy_ref[...] = spline_table(low_y, values, pad_y)
    vy_ref[...] = spline_table(low_y, slopes, pad_y)
    values, slopes = spline_weights(frac_z)
    turn = turn_ref[...]
    size_z = turn.shape[0]
    for place, terms in enumerate((values, slopes)):
        table_z = spline_table(base + low_z, terms, size_z, size_z)
        waves = jnp.dot(
            turn, table_z, precision=lax.Precision.HIGHEST, preferred_element_type=jnp.float32
        )
        high, low = halves(waves)
        wz_ref[:size_z, pl.ds(place * atom_total, atom_total)] = high
        wz_ref[size_z:, pl.ds(place * atom_total, atom_total)] = low
    groups = pad_y // 8

    def one_chunk(chunk, sums):
        rows = mesh_ref[pl.ds(chunk * rows_group, rows_group)].reshape(rows_group * pad_y, size_z)
        high, low = halves(rows)
        level_ref[...] = dot(jnp.concatenate([high, high], axis=1), wz_ref[...]) + dot(
            low, wz_ref[:size_z, :]
        )
        first, second, third = sums
        for inner in range(rows_group):
            flat = level_ref[pl.ds(inner * pad_y, pad_y), :atom_total]
            tilt = level_ref[pl.ds(inner * pad_y, pad_y), atom_total:]
            across = wy_ref[...]
            part_x = jnp.sum((across * flat).reshape(groups, 8, atom_total), axis=0)
            part_y = jnp.sum((vy_ref[...] * flat).reshape(groups, 8, atom_total), axis=0)
            part_z = jnp.sum((across * tilt).reshape(groups, 8, atom_total), axis=0)
            weight = wx_ref[pl.ds(chunk * rows_group + inner, 1), :]
            slope = vx_ref[pl.ds(chunk * rows_group + inner, 1), :]
            first = first + slope * part_x
            second = second + weight * part_y
            third = third + weight * part_z
        return (first, second, third)

    zero = jnp.zeros((8, atom_total), jnp.float32)
    sums = lax.fori_loop(0, pad_x // rows_group, one_chunk, (zero, zero, zero))
    factor = -atoms_ref[3:4, :] / spacing
    for place in range(3):
        out_ref[pl.ds(place, 1), :] = factor * jnp.sum(sums[place], axis=0, keepdims=True)


def share_kernel(sizes, atoms_ref, out_ref, send_sem, recv_sem):
    count_x, count_y = sizes
    place_x, place_y = (lax.axis_index("gx"), lax.axis_index("gy"))
    me = place_x * count_y + place_y
    peers = []
    for order in range(1, count_x * count_y):
        peer_x = lax.rem(place_x + order // count_y, count_x)
        peer_y = lax.rem(place_y + order % count_y, count_y)
        peers.append({"gx": peer_x, "gy": peer_y})
    barrier = pltpu.get_barrier_semaphore()
    for peer in peers:
        pl.semaphore_signal(
            barrier, inc=1, device_id=peer, device_id_type=pl.DeviceIdType.MESH
        )
    pl.semaphore_wait(barrier, len(peers))
    copies = [
        pltpu.make_async_remote_copy(
            src_ref=atoms_ref,
            dst_ref=out_ref.at[me],
            send_sem=send_sem.at[order],
            recv_sem=recv_sem.at[order],
            device_id=peer,
            device_id_type=pl.DeviceIdType.MESH,
        )
        for order, peer in enumerate(peers)
    ]
    for copy in copies:
        copy.start()
    out_ref[me] = atoms_ref[...]
    for copy in copies:
        copy.wait()


def shared(atoms, count_x, count_y):
    devices = count_x * count_y
    vmem = pl.BlockSpec(memory_space=pltpu.VMEM)
    flags = pltpu.SemaphoreType.DMA((devices - 1,))
    return pl.pallas_call(
        functools.partial(share_kernel, (count_x, count_y)),
        in_specs=[vmem],
        out_specs=vmem,
        out_shape=jax.ShapeDtypeStruct((devices, *atoms.shape), jnp.float32),
        scratch_shapes=[flags, flags],
        compiler_params=pltpu.CompilerParams(collective_id=0, has_side_effects=True),
        name="share",
    )(atoms)


def depth_rows(table, height, fraction, terms):
    turns = height * table[:, 0:1]
    quarter = GRID_Z // 4
    nearest = jnp.floor(turns * (1.0 / quarter) + 0.5)
    angle = (turns - nearest * quarter) * (2.0 * math.pi / GRID_Z)
    quadrant = nearest - 4.0 * jnp.floor(nearest * 0.25)
    square = angle * angle
    near_cos = 1.0 + square * (
        -0.5 + square * (1.0 / 24.0 + square * (-1.0 / 720.0 + square * (1.0 / 40320.0)))
    )
    near_sin = angle * (
        1.0
        + square
        * (-1.0 / 6.0 + square * (1.0 / 120.0 + square * (-1.0 / 5040.0 + square / 362880.0)))
    )
    odd_turn = (quadrant == 1.0) | (quadrant == 3.0)
    cosine = jnp.where(odd_turn, near_sin, near_cos)
    cosine = jnp.where((quadrant == 1.0) | (quadrant == 2.0), -cosine, cosine)
    sine = jnp.where(odd_turn, near_cos, near_sin)
    sine = jnp.where(quadrant >= 2.0, -sine, sine)
    results = []
    for weights in terms:
        even = sum(table[:, 1 + t : 2 + t] * weights[t] for t in range(4))
        odd = sum(table[:, 5 + t : 6 + t] * weights[t] for t in range(4))
        results.append(cosine * even + sine * odd)
    return results


def mesh_kernel(sizes, cells, pad, atoms_ref, xh_ref, xl_ref, yh_ref, yl_ref, column_ref, row_ref, table_ref, out_ref, mesh_ref, turned_ref, *scratch):
    count_x, count_y = sizes
    cells_x, cells_y = cells
    pad_x, pad_y = pad
    atom_total = atoms_ref.shape[2]
    depth = table_ref.shape[0]
    window = 2 * cells_y
    windows = GRID_Y // window
    lane = lax.broadcasted_iota(jnp.int32, (depth * pad_x, window), 1)
    mesh_ref[...] = jnp.zeros_like(mesh_ref)
    table = table_ref[...]
    per_side = len(scratch) // 2
    banks = (scratch[:per_side], scratch[per_side:])
    for _, _, wy_ref, _, _, _, _, side_ref in banks:
        wy_ref[...] = jnp.zeros_like(wy_ref)
        side_ref[...] = jnp.zeros_like(side_ref)

    def atoms_of(cell, row):
        return atoms_ref[cell, row : row + 1, :]

    def spread_cell(cell, i, j):
        wx_ref, vx_ref, wy_ref, hi_ref, lo_ref, level_ref, stack_ref, side_ref = banks[j % 2]
        low_x, frac_x = split_cells(atoms_of(cell, 0), 0.0, cells_x)
        low_y, frac_y = split_cells(atoms_of(cell, 1), 0.0, cells_y)
        wx_ref[...] = spline_table(low_x, spline_weights(frac_x)[0], pad_x)
        high, low = halves(spline_table(low_y, spline_weights(frac_y)[0], pad_y))
        wy_ref[:pad_y, :] = high
        wy_ref[pl.ds(window, pad_y), :] = low
        height = jnp.floor(atoms_of(cell, 2))
        frac_z = atoms_of(cell, 2) - height
        (deep,) = depth_rows(table, height, frac_z, [spline_weights(frac_z)[0]])
        deep = deep * atoms_of(cell, 3)
        for k in range(depth):
            high, low = halves(deep[k : k + 1, :] * wx_ref[...])
            hi_ref[pl.ds(k * pad_x, pad_x), :] = high
            lo_ref[pl.ds(k * pad_x, pad_x), :] = low
        numbers = (((1,), (1,)), ((), ()))
        both = lax.dot_general(
            hi_ref[...], wy_ref[...], numbers, preferred_element_type=jnp.float32
        )
        rest = lax.dot_general(
            lo_ref[...], wy_ref[:window, :], numbers, preferred_element_type=jnp.float32
        )
        total = both[:, :window] + both[:, window:] + rest
        rows = pl.ds(pl.multiple_of(i * cells_x, 8), pad_x)
        m = j // 2
        if j % 2 == 0:
            mesh_ref[:, rows, pl.ds(m * window, window)] += total.reshape(depth, pad_x, window)
        else:
            total = pltpu.roll(total, cells_y, 1)
            kept = jnp.where(lane >= cells_y, total, 0.0)
            carried = jnp.where(lane < cells_y, total, 0.0)
            after = (m + 1) % windows
            mesh_ref[:, rows, pl.ds(m * window, window)] += kept.reshape(depth, pad_x, window)
            mesh_ref[:, rows, pl.ds(after * window, window)] += carried.reshape(
                depth, pad_x, window
            )

    @pl.loop(0, count_x)
    def _(i):
        for j in range(count_y):
            spread_cell(i * count_y + j, i, j)

    def across(value):
        high, low = halves(value)
        return dot(xh_ref[...], high) + dot(xl_ref[...], high) + dot(xh_ref[...], low)

    def along(value):
        high, low = halves(value)
        return dot(high, yh_ref[...]) + dot(high, yl_ref[...]) + dot(low, yh_ref[...])

    extra = mesh_ref.shape[1] - GRID_X

    @pl.loop(0, depth)
    def _(k):
        mesh_ref[k, :extra, :] += mesh_ref[k, GRID_X:, :]
        waves = along(across(mesh_ref[k, :GRID_X, :]))
        square = column_ref[:, 0:1] + row_ref[0:1, :] + table_ref[pl.ds(k, 1), 9:10]
        scale = column_ref[:, 1:2] * row_ref[1:2, :] * table_ref[pl.ds(k, 1), 10:11]
        green = jnp.where(square > 0.0, scale / jnp.where(square > 0.0, square, 1.0), 0.0)
        plane = across(along(waves * green))
        mesh_ref[k, :GRID_X, :] = plane
        mesh_ref[k, GRID_X:, :] = plane[:extra]
        rolled = pltpu.roll(plane, GRID_Y - cells_y, 1)
        turned_ref[k, :GRID_X, :] = rolled
        turned_ref[k, GRID_X:, :] = rolled[:extra]

    stride = round_up(pad_y, 16)
    groups = pad_x // 8

    def gather_cell(cell, i, j):
        wx_ref, vx_ref, wy_ref, hi_ref, lo_ref, level_ref, stack_ref, side_ref = banks[j % 2]
        low_x, frac_x = split_cells(atoms_of(cell, 0), 0.0, cells_x)
        low_y, frac_y = split_cells(atoms_of(cell, 1), 0.0, cells_y)
        values, slopes = spline_weights(frac_x)
        wx_ref[...] = spline_table(low_x, values, pad_x)
        vx_ref[...] = spline_table(low_x, slopes, pad_x)
        for place, terms in enumerate(spline_weights(frac_y)):
            high, low = halves(spline_table(low_y, terms, stride))
            span = pl.ds(place * atom_total, atom_total)
            side_ref[:stride, span] = high
            side_ref[pl.ds(stride, stride), span] = low
            side_ref[pl.ds(2 * stride, stride), span] = high
        height = jnp.floor(atoms_of(cell, 2))
        frac_z = atoms_of(cell, 2) - height
        deep, steep = depth_rows(table, height, frac_z, spline_weights(frac_z))
        source = mesh_ref if j % 2 == 0 else turned_ref
        rows = pl.ds(pl.multiple_of(i * cells_x, 8), pad_x)
        block = source[:, rows, pl.ds(j // 2 * window, window)].reshape(depth * pad_x, window)
        high = block.astype(jnp.bfloat16).astype(jnp.float32)
        low = block - high
        shifted = pltpu.roll(high, stride, 1)
        stack_ref[:, :window] = jnp.where(lane < stride, high, shifted).astype(jnp.bfloat16)
        stack_ref[:, window:] = jnp.where(
            lane < 2 * stride - window, shifted, pltpu.roll(low, 2 * stride - window, 1)
        ).astype(jnp.bfloat16)
        level_ref[...] = dot(stack_ref[...], side_ref[...])
        zero = jnp.zeros((8, atom_total), jnp.float32)
        first, second, third = (zero, zero, zero)
        for k in range(depth):
            flat = level_ref[pl.ds(k * pad_x, pad_x), :atom_total]
            tilt = level_ref[pl.ds(k * pad_x, pad_x), atom_total:]
            weight = wx_ref[...]
            part_x = jnp.sum((vx_ref[...] * flat).reshape(groups, 8, atom_total), axis=0)
            part_y = jnp.sum((weight * tilt).reshape(groups, 8, atom_total), axis=0)
            part_z = jnp.sum((weight * flat).reshape(groups, 8, atom_total), axis=0)
            first = first + deep[k : k + 1, :] * part_x
            second = second + deep[k : k + 1, :] * part_y
            third = third + steep[k : k + 1, :] * part_z
        for place, value in enumerate((first, second, third)):
            out_ref[cell, pl.ds(place, 1), :] = jnp.sum(value, axis=0, keepdims=True)
        out_ref[cell, 3:4, :] = jnp.zeros((1, atom_total), jnp.float32)

    @pl.loop(0, count_x)
    def _(i):
        for j in range(count_y):
            gather_cell(i * count_y + j, i, j)


def green_table(period):
    index = np.arange(period)
    signed = np.where(index <= period // 2, index, index - period) / (period * spacing)
    modulus = ((2.0 + np.cos(index * (2.0 * np.pi / period))) / 3.0) ** 2
    square = signed * signed
    return np.stack([square, np.exp(-((np.pi / ewald_split) ** 2) * square) / modulus]).astype(
        np.float32
    )


def green_factors(index, period):
    signed = jnp.where(index <= period // 2, index, index - period).astype(jnp.float32) / (
        period * spacing
    )
    modulus = ((2.0 + jnp.cos(index.astype(jnp.float32) * (2.0 * jnp.pi / period))) / 3.0) ** 2
    square = signed * signed
    return jnp.stack([square, jnp.exp(-((jnp.pi / ewald_split) ** 2) * square) / modulus])


def one_cluster(own_rows, partner):
    offsets = (own_rows[:3, :, None] - partner[:3, None, :]) * spacing
    dist_square = jnp.sum(offsets * offsets, axis=0)
    soft_square = dist_square + soft_core
    soft_dist = jnp.sqrt(soft_square)
    scaled = ewald_split * soft_dist
    strength = (
        jax.scipy.special.erfc(scaled) / soft_dist
        + ewald_split * root_factor * jnp.exp(-scaled * scaled)
    ) / soft_square
    cutoff_taper = jnp.where(
        dist_square < cutoff * cutoff, (1.0 - dist_square / (cutoff * cutoff)) ** 2, 0.0
    )
    weight = partner[3][None, :] * strength * cutoff_taper
    return own_rows[3] * jnp.sum(weight[None] * offsets, axis=2)


def far_by_planes(gathered, own_charge, count_x, count_y, cells_x, cells_y):
    devices = count_x * count_y
    place = lax.axis_index("gx") * count_y + lax.axis_index("gy")
    depth = GRID_Z // devices
    atom_total = gathered.shape[2]
    pad_x = round_up(cells_x + 3, 8)
    pad_y = round_up(cells_y + 3, 8)
    window = 2 * cells_y
    turn_x = halves(jnp.asarray(hartley(GRID_X)))
    turn_y = halves(jnp.asarray(hartley(GRID_Y)))
    volume = GRID_X * GRID_Y * GRID_Z * spacing**3
    column = jnp.asarray(green_table(GRID_X).T)
    row = jnp.asarray(green_table(GRID_Y))
    every_k = np.arange(GRID_Z)
    taps = np.outer(every_k, np.arange(4)) * (2.0 * np.pi / GRID_Z)
    square, scale = green_table(GRID_Z)
    table = np.concatenate(
        [
            every_k[:, None],
            np.cos(taps) + np.sin(taps),
            np.cos(taps) - np.sin(taps),
            square[:, None],
            scale[:, None] / (np.pi * volume),
        ],
        axis=1,
    ).astype(np.float32)
    table = lax.dynamic_slice_in_dim(jnp.asarray(table), place * depth, depth, axis=0)
    vmem = pl.BlockSpec(memory_space=pltpu.VMEM)
    rows = GRID_X + pad_x - cells_x
    bank = [
        pltpu.VMEM((pad_x, atom_total), jnp.float32),
        pltpu.VMEM((pad_x, atom_total), jnp.float32),
        pltpu.VMEM((2 * window, atom_total), jnp.bfloat16),
        pltpu.VMEM((depth * pad_x, atom_total), jnp.bfloat16),
        pltpu.VMEM((depth * pad_x, atom_total), jnp.bfloat16),
        pltpu.VMEM((depth * pad_x, 2 * atom_total), jnp.float32),
        pltpu.VMEM((depth * pad_x, 2 * window), jnp.bfloat16),
        pltpu.VMEM((2 * window, 2 * atom_total), jnp.bfloat16),
    ]
    partial = pl.pallas_call(
        functools.partial(mesh_kernel, (count_x, count_y), (cells_x, cells_y), (pad_x, pad_y)),
        in_specs=[vmem] * 8,
        out_specs=vmem,
        out_shape=jax.ShapeDtypeStruct((devices, 4, atom_total), jnp.float32),
        scratch_shapes=[pltpu.VMEM((depth, rows, GRID_Y), jnp.float32)] * 2 + 2 * bank,
        name="mesh",
    )(gathered, *turn_x, *turn_y, column, row, table)
    parts = lax.all_to_all(partial, ("gx", "gy"), split_axis=0, concat_axis=0, tiled=True)
    total = jnp.sum(parts, axis=0)[:3]
    return total * (-own_charge / spacing)


def convolved_by_lines(charge_mesh, count_x, count_y):
    turn_x = jnp.asarray(hartley(GRID_X))
    turn_y = jnp.asarray(hartley(GRID_Y))
    product = functools.partial(
        jnp.einsum, precision=lax.Precision.HIGHEST, preferred_element_type=jnp.float32
    )
    exchange = functools.partial(lax.all_to_all, tiled=True)
    lines = exchange(charge_mesh, "gx", split_axis=2, concat_axis=0)
    lines = product("xyk,xu->uyk", lines, turn_x)
    lines = exchange(lines, "gy", split_axis=0, concat_axis=1)
    lines = product("uyk,yv->uvk", lines, turn_y)
    wide, _, depth = lines.shape
    start_x = lax.axis_index("gy") * wide
    start_z = lax.axis_index("gx") * depth
    volume = GRID_X * GRID_Y * GRID_Z * spacing**3
    fx = green_factors(start_x + jnp.arange(wide, dtype=jnp.int32), GRID_X)
    fy = green_factors(jnp.arange(GRID_Y, dtype=jnp.int32), GRID_Y)
    fz = green_factors(start_z + jnp.arange(depth, dtype=jnp.int32), GRID_Z)
    square = fx[0][:, None, None] + fy[0][:, None] + fz[0]
    scale = fx[1][:, None, None] * fy[1][:, None] * fz[1] / (math.pi * volume)
    lines = lines * jnp.where(square > 0.0, scale / jnp.where(square > 0.0, square, 1.0), 0.0)
    lines = product("uvk,vy->uyk", lines, turn_y)
    lines = exchange(lines, "gy", split_axis=1, concat_axis=0)
    lines = product("uyk,ux->xyk", lines, turn_x)
    return exchange(lines, "gx", split_axis=0, concat_axis=2)


def far_by_lines(atoms, base, count_x, count_y, cells_x, cells_y, cells_z):
    atom_total = atoms.shape[1]
    cells = (cells_x, cells_y, cells_z)
    pad = (round_up(cells_x + 3, rows_group), round_up(cells_y + 3, 8))
    pad_x, pad_y = pad
    turn_z = jnp.asarray(hartley(GRID_Z))
    spread = pl.pallas_call(
        functools.partial(spread_kernel, cells, pad),
        out_shape=jax.ShapeDtypeStruct((pad_x, pad_y, GRID_Z), jnp.float32),
        scratch_shapes=[
            pltpu.VMEM((pad_x, atom_total), jnp.float32),
            pltpu.VMEM((pad_y, atom_total), jnp.float32),
            pltpu.VMEM((atom_total, 2 * GRID_Z), jnp.bfloat16),
            pltpu.VMEM((rows_group * pad_y, atom_total), jnp.bfloat16),
            pltpu.VMEM((rows_group * pad_y, atom_total), jnp.bfloat16),
        ],
        name="spread",
    )(atoms, base, turn_z)

    from_x = moved(spread[cells_x : cells_x + 3, :cells_y], 1, 0)
    from_y = moved(spread[:cells_x, cells_y : cells_y + 3], 0, 1)
    from_both = moved(spread[cells_x : cells_x + 3, cells_y : cells_y + 3], 1, 1)
    charge_mesh = (
        spread[:cells_x, :cells_y]
        .at[:3]
        .add(from_x)
        .at[:, :3]
        .add(from_y)
        .at[:3, :3]
        .add(from_both)
    )
    potential = convolved_by_lines(charge_mesh, count_x, count_y)
    upper_x = moved(potential[:3], -1, 0)
    upper_y = moved(potential[:, :3], 0, -1)
    upper_both = moved(potential[:3, :3], -1, -1)
    wider = jnp.concatenate(
        [
            jnp.concatenate([potential, upper_x], axis=0),
            jnp.concatenate([upper_y, upper_both], axis=0),
        ],
        axis=1,
    )
    wider = jnp.pad(wider, ((0, pad_x - cells_x - 3), (0, pad_y - cells_y - 3), (0, 0)))
    return pl.pallas_call(
        functools.partial(gather_kernel, cells, pad),
        out_shape=jax.ShapeDtypeStruct((3, atom_total), jnp.float32),
        scratch_shapes=[
            pltpu.VMEM((pad_x, atom_total), jnp.float32),
            pltpu.VMEM((pad_x, atom_total), jnp.float32),
            pltpu.VMEM((pad_y, atom_total), jnp.float32),
            pltpu.VMEM((pad_y, atom_total), jnp.float32),
            pltpu.VMEM((2 * GRID_Z, 2 * atom_total), jnp.bfloat16),
            pltpu.VMEM((rows_group * pad_y, 2 * atom_total), jnp.float32),
        ],
        name="gather",
    )(atoms, base, turn_z, wider)


def local(positions, charges, pair_lists, slab_dest, atom_counts):
    count_x = lax.axis_size("gx")
    count_y = lax.axis_size("gy")
    devices = count_x * count_y
    atom_total = positions.shape[3]
    clusters = pair_lists.shape[2]
    cluster_size = atom_total // clusters
    blocks = slab_dest.shape[2]
    block_size = atom_total // blocks
    cells_x = GRID_X // count_x
    cells_y = GRID_Y // count_y
    cells_z = GRID_Z // count_y
    living = jnp.arange(atom_total, dtype=jnp.int32) < atom_counts[0, 0]
    charge = jnp.where(living, charges[0, 0], 0.0)
    packed = jnp.concatenate([positions, charge[None, None, None, :]], axis=0)
    atoms = packed.reshape(4, atom_total)

    base = jnp.broadcast_to(
        (slab_dest[0, 0] * cells_z)[:, None], (blocks, block_size)
    ).reshape(1, atom_total)
    by_planes = GRID_Z % devices == 0 and cells_y == 64 and cells_x % 8 == 0
    if by_planes:
        gathered = shared(atoms, count_x, count_y)
    else:
        gathered = lax.all_gather(atoms, ("gx", "gy"), axis=0, tiled=False)
    if by_planes:
        far_part = far_by_planes(gathered, charge, count_x, count_y, cells_x, cells_y)
    else:
        far_part = far_by_lines(atoms, base, count_x, count_y, cells_x, cells_y, cells_z)

    chosen = pair_lists[0, 0]
    beside = chosen // clusters
    step_x, step_y = (beside // 3 - 1, beside % 3 - 1)
    at_x = (lax.axis_index("gx") + step_x + count_x) % count_x
    at_y = (lax.axis_index("gy") + step_y + count_y) % count_y
    number = (at_x * count_y + at_y) * clusters + chosen % clusters
    pick = (number[:, :, None] == jnp.arange(devices * clusters, dtype=jnp.int32)).astype(
        jnp.float32
    )
    pool = gathered[:, :4].reshape(devices, 4, clusters, cluster_size)
    pool = jnp.transpose(pool, (1, 0, 2, 3)).reshape(4, devices * clusters, cluster_size)
    partners = jnp.einsum(
        "cln,fnk->cflk",
        pick,
        pool,
        precision=lax.Precision.HIGHEST,
        preferred_element_type=jnp.float32,
    )
    shift_x = (step_x * cells_x).astype(jnp.float32)
    shift_y = (step_y * cells_y).astype(jnp.float32)
    flat = jnp.zeros_like(shift_x)
    shift = jnp.stack([shift_x, shift_y, flat, flat], axis=1)
    partners = (partners + shift[:, :, :, None]).reshape(clusters, 4, -1)
    own = packed.reshape(4, clusters, cluster_size)
    pair_part = jnp.stack(
        [one_cluster(own[:, c], partners[c]) for c in range(clusters)], axis=1
    )
    short_forces = pair_part.reshape(3, 1, 1, atom_total)
    return (short_forces, far_part.reshape(3, 1, 1, atom_total))


def solution(mesh):
    return jax.shard_map(
        local,
        mesh=mesh,
        in_specs=(
            P(None, ("rep", "gx"), "gy", None),
            P(("rep", "gx"), "gy", None),
            P(("rep", "gx"), "gy", None, None),
            P(("rep", "gx"), "gy", None),
            P(("rep", "gx"), "gy"),
        ),
        out_specs=(P(None, ("rep", "gx"), "gy", None), P(None, ("rep", "gx"), "gy", None)),
        check_vma=False,
    )
```

profile of v0, /device:TPU:0, one launch (start us, length us, event | category | flops | bytes accessed | tf_op | source)
XLA Modules:
  0.0 96.2 jit_solution(10155256270435562340)
XLA Ops:
  0.6 0.0 copy-start.3
  1.3 0.7 copy.15
  2.0 0.7 compare_select_fusion
  2.7 0.6 maximum_bitcast_fusion.atoms_ref
  3.3 13.4 %share.1.atoms_ref = f32[16,4,1024]{2,1,0:T(4,128)} custom-call(f32[4,1024]{1,0:T(4,128)} %maximum_bitcast_fusion.atoms_ref), custom_call_target="tpu_custom_call" | custom-call | tf_op jit(solution)/shard_map/share/pallas_call | solution.py:217
  16.7 0.0 copy-start
  16.7 1.3 %constant_dynamic-slice_fusion.table_ref = f32[8,11]{1,0:T(8,128)} fusion(f32[128,11]{1,0:T(8,128)} %constant.156.clone, s32[]{:T(128)S(6)} %select_n.155), kind=kLoop, calls=%fused_computation.169 | loop fusion | bytes 708 | tf_op jit(solution)/shard_map/dynamic_slice | solution.py:457
  18.0 52.3 %mesh.1 = f32[16,4,1024]{2,1,0:T(4,128)} custom-call(f32[16,4,1024]{2,1,0:T(4,128)} %share.1.atoms_ref, bf16[256,256]{1,0:T(8,128)(2,1)} %constant.161.xh_ref.yh_ref, bf16[256,256]{1,0:T(8,128)(2,1)} %constant.164.xl_ref.yl_ref, bf16[256,256]{1,0:T(8,128)(2,1)} %constant.161.xh_ref.yh_ref, bf16[256,256]{1,0:T(8,128)(2,1)} %constant.164.xl_ref.yl_ref, ...), custom_call_target="tpu_custom_call" | custom-call | tf_op jit(solution)/shard_map/mesh/pallas_call | solution.py:470
  70.3 6.0 %all-to-all-start = ((f32[16,4,1024]{2,1,0:T(4,128)}), f32[16,4,1024]{2,1,0:T(4,128)S(1)}, u32[]{:S(2)}, u32[]{:S(2)}) async-start(f32[16,4,1024]{2,1,0:T(4,128)} %mesh.1), calls=%async_computation | async-start | bytes 524288 | tf_op jit(solution)/shard_map/all_to_all | solution.py:478
  76.3 0.0 copy-done.3
  76.3 0.0 copy-start.1
  76.4 0.0 copy-done
  76.4 0.0 copy-start.2
  76.4 0.2 reshape.884
  76.6 0.1 reshape.888
  76.7 0.1 pad.6.clone
  76.8 0.1 maximum_maximum_fusion
  76.9 0.3 fusion.12
  77.2 0.0 copy-done.1
  77.2 0.5 broadcast.1440
  77.7 0.0 copy-done.2
  77.7 0.7 reduce.4
  78.6 0.4 fusion.4
  79.0 3.1 %multiply_multiply_fusion.4 = f32[256,1024]{1,0:T(8,128)S(1)} fusion(f32[256,1024]{1,0:T(8,128)S(1)} %fusion.4, f32[1024]{0:T(1024)S(1)} %bitcast.129), kind=kLoop, calls=%fused_computation.74 | loop fusion | flops 19922944 | bytes 2101248 | tf_op jit(solution)/shard_map/mul | solution.py:428
  82.1 0.5 fusion.5
  82.6 0.4 fusion.7
  83.1 3.1 %multiply_multiply_fusion.2 = f32[256,1024]{1,0:T(8,128)S(1)} fusion(f32[256,1024]{1,0:T(8,128)S(1)} %fusion.7, f32[1024]{0:T(1024)S(1)} %bitcast.128), kind=kLoop, calls=%fused_computation.64 | loop fusion | flops 19922944 | bytes 2101248 | tf_op jit(solution)/shard_map/mul | solution.py:428
  86.2 0.5 fusion.8
  86.7 0.4 fusion.10
  87.2 3.1 %multiply_multiply_fusion = f32[256,1024]{1,0:T(8,128)S(1)} fusion(f32[256,1024]{1,0:T(8,128)S(1)} %fusion.10, f32[1024]{0:T(1024)S(1)} %bitcast.127), kind=kLoop, calls=%fused_computation.54 | loop fusion | flops 19922944 | bytes 2101248 | tf_op jit(solution)/shard_map/mul | solution.py:428
  90.2 0.5 fusion.11
  90.7 0.4 fusion.1
  91.2 3.1 %multiply_multiply_fusion.6 = f32[256,1024]{1,0:T(8,128)S(1)} fusion(f32[256,1024]{1,0:T(8,128)S(1)} %fusion.1, f32[1024]{0:T(1024)S(1)} %bitcast.126), kind=kLoop, calls=%fused_computation.84 | loop fusion | flops 19922944 | bytes 2101248 | tf_op jit(solution)/shard_map/mul | solution.py:428
  94.3 0.5 fusion.2
  94.9 0.6 copy.17
  95.5 0.0 all-to-all-done
  95.5 0.1 reduce_sum.101
  95.5 0.6 reshape.887
  (29 shorter events, 0.3 us)
Async XLA Ops:
  0.6 75.7 %copy-start.3 = (s32[1,1,4,4]{3,2,1,0:T(4,128)S(1)}, s32[1,1,4,4]{3,2,1,0:T(4,128)}, u32[]{:S(2)}) copy-start(s32[1,1,4,4]{3,2,1,0:T(4,128)} %param.12) | copy-start | bytes 196
  16.7 59.7 %copy-start = (f32[16,4,1024]{2,1,0:T(4,128)S(1)}, f32[16,4,1024]{2,1,0:T(4,128)}, u32[]{:S(2)}) copy-start(f32[16,4,1024]{2,1,0:T(4,128)} %share.1.atoms_ref) | copy-start | bytes 786436
  70.3 25.2 %all-to-all-start = ((f32[16,4,1024]{2,1,0:T(4,128)}), f32[16,4,1024]{2,1,0:T(4,128)S(1)}, u32[]{:S(2)}, u32[]{:S(2)}) async-start(f32[16,4,1024]{2,1,0:T(4,128)} %mesh.1), calls=%async_computation | async-start | bytes 524288 | tf_op jit(solution)/shard_map/all_to_all | solution.py:478
  76.3 0.9 copy-start.1
  76.4 1.3 %copy-start.2 = (f32[1,1,1024]{2,1,0:T(1,128)S(1)}, f32[1,1,1024]{2,1,0:T(1,128)}, u32[]{:S(2)}) copy-start(f32[1,1,1024]{2,1,0:T(1,128)} %param.11) | copy-start | bytes 12292
where the time goes:
time: 96.7 us; the launch traced here: 96.2 us
  Pallas kernels  65.6 us (68%)
  other arithmetic  18.4 us (19%)
  starting transfers between devices  5.97 us (6%)
  local copies, waits for them, and re-layouts  4.27 us (4%)
  between operations  1.64 us (2%)
    pallas_call x1, Pallas kernels, far_by_planes(): pl.pallas_call(functools.partial(mesh_kernel, (count_x, count_y), (cells_...  52.3 us
    pallas_call x1, Pallas kernels, shared(): pl.pallas_call(functools.partial(share_kernel, (count_x, count_y)), in_sp...  13.4 us
    mul x8, other arithmetic, one_cluster(): return own_rows[3] * jnp.sum(weight[None] * offsets, axis=2)  12.3 us
    all_to_all x1, starting transfers between devices, far_by_planes(): lax.all_to_all(partial, ('gx', 'gy'), split_axis=0, concat_axis=0, tiled=...  5.97 us
    reduce_sum x4, other arithmetic, one_cluster(): return own_rows[3] * jnp.sum(weight[None] * offsets, axis=2)  2.04 us
  transfers between devices with their start and end apart: 1, of which 0 were waited for; matrix products, arithmetic and copies ran while one was open for 20% of the time, Pallas kernels for 0%

commit v1 on v0

--- a/solution.py
+++ b/solution.py
@@ -392,6 +392,167 @@
             gather_cell(i * count_y + j, i, j)
 
 
+root_terms = (
+    3.9164407301418542,
+    -0.0037127819564810594,
+    0.16802528315459195,
+    -0.003061234121505335,
+    -0.0076524954798020545,
+    0.002268454833542123,
+    -0.0003056487922112269,
+    1.686888935413571e-05,
+)
+
+
+def pair_weight(square):
+    soft_square = square * (spacing * spacing) + soft_core
+    inverse = lax.rsqrt(soft_square)
+    series = jnp.full_like(inverse, root_terms[-1])
+    for term in root_terms[-2::-1]:
+        series = series * inverse + term
+    decay = jnp.exp(soft_square * (-ewald_split * ewald_split))
+    taper = jnp.maximum(1.0 - square * (spacing * spacing / (cutoff * cutoff)), 0.0)
+    return (decay * series) * (inverse * taper) ** 2
+
+
+def row_sums(values):
+    total = None
+    ones = jnp.ones((16, values.shape[1]), jnp.bfloat16)
+    for _ in range(3):
+        part = values.astype(jnp.bfloat16)
+        values = values - part.astype(jnp.float32)
+        summed = lax.dot_general(
+            ones, part, (((1,), (1,)), ((), ())), preferred_element_type=jnp.float32
+        )
+        total = summed if total is None else total + summed
+    return total[0:1, :]
+
+
+def peers_of(count_x, count_y):
+    place_x, place_y = (lax.axis_index("gx"), lax.axis_index("gy"))
+    peers = []
+    for order in range(1, count_x * count_y):
+        peer_x = lax.rem(place_x + order // count_y, count_x)
+        peer_y = lax.rem(place_y + order % count_y, count_y)
+        peers.append((peer_x, peer_y))
+    return peers
+
+
+def finish_kernel(sizes, cells, pairs_ref, partial_ref, atoms_ref, short_ref, long_ref, land_ref, column_ref, partner_ref, sum_ref, send_sem, recv_sem):
+    count_x, count_y = sizes
+    cells_x, cells_y = cells
+    place_x, place_y = (lax.axis_index("gx"), lax.axis_index("gy"))
+    me = place_x * count_y + place_y
+    peers = peers_of(count_x, count_y)
+    barrier = pltpu.get_barrier_semaphore()
+    for peer_x, peer_y in peers:
+        pl.semaphore_signal(
+            barrier,
+            inc=1,
+            device_id={"gx": peer_x, "gy": peer_y},
+            device_id_type=pl.DeviceIdType.MESH,
+        )
+    clusters, listed = pairs_ref.shape[2:]
+    atom_total = atoms_ref.shape[2]
+    size = atom_total // clusters
+    lanes = 128
+    for axis in range(3):
+        for chunk in range(atom_total // lanes):
+            row = atoms_ref[me, pl.ds(axis, 1), pl.ds(chunk * lanes, lanes)]
+            column_ref[axis, pl.ds(chunk * lanes, lanes), :] = jnp.broadcast_to(
+                row, (lanes, lanes)
+            ).T
+    for c in range(clusters):
+        for n in range(listed):
+            chosen = pairs_ref[0, 0, c, n]
+            beside = lax.div(chosen, clusters)
+            which = chosen - beside * clusters
+            row_x = lax.div(beside, 3)
+            step_x = row_x - 1
+            step_y = beside - row_x * 3 - 1
+            from_x = lax.rem(place_x + step_x + count_x, count_x)
+            from_y = lax.rem(place_y + step_y + count_y, count_y)
+            block = atoms_ref[from_x * count_y + from_y]
+            part = block[:, :size]
+            for k in range(1, clusters):
+                part = jnp.where(which == k, block[:, k * size : (k + 1) * size], part)
+            shifts = (
+                (step_x * cells_x).astype(jnp.float32),
+                (step_y * cells_y).astype(jnp.float32),
+            )
+            for axis in range(4):
+                row = part[axis : axis + 1, :]
+                if axis < 2:
+                    row = row + shifts[axis]
+                partner_ref[c, axis, :, n * size : (n + 1) * size] = jnp.broadcast_to(
+                    row, (8, size)
+                )
+
+    pl.semaphore_wait(barrier, len(peers))
+    copies = []
+    for order, (peer_x, peer_y) in enumerate(peers):
+        copy = pltpu.make_async_remote_copy(
+            src_ref=partial_ref.at[peer_x * count_y + peer_y],
+            dst_ref=land_ref.at[order],
+            send_sem=send_sem.at[order],
+            recv_sem=recv_sem.at[order],
+            device_id={"gx": peer_x, "gy": peer_y},
+            device_id_type=pl.DeviceIdType.MESH,
+        )
+        copy.start()
+        copies.append(copy)
+
+    @pl.loop(0, clusters)
+    def _(c):
+        @pl.loop(0, size // 8)
+        def _(step):
+            rows = pl.ds(pl.multiple_of(c * size + step * 8, 8), 8)
+            own = [column_ref[axis, rows, :] for axis in range(3)]
+            sums = [jnp.zeros((8, lanes), jnp.float32) for _ in range(3)]
+            for tile in range(listed * size // lanes):
+                span = pl.ds(tile * lanes, lanes)
+                offsets = [own[axis] - partner_ref[c, axis, :, span] for axis in range(3)]
+                square = sum(offset * offset for offset in offsets)
+                weight = pair_weight(square) * partner_ref[c, 3, :, span]
+                sums = [total + weight * offset for total, offset in zip(sums, offsets)]
+            for axis in range(3):
+                sum_ref[axis, rows, :] = sums[axis]
+
+    own_charge = atoms_ref[me, 3:4, :]
+    for axis in range(3):
+        short_ref[axis, 0, :, :] = row_sums(sum_ref[axis]) * (own_charge * spacing)
+    for copy in copies:
+        copy.wait()
+    total = partial_ref[me]
+    for order in range(len(peers)):
+        total = total + land_ref[order]
+    for axis in range(3):
+        long_ref[axis, 0, :, :] = total[axis : axis + 1, :] * (own_charge * (-1.0 / spacing))
+
+
+def finished(pair_lists, partial, gathered, count_x, count_y, cells_x, cells_y):
+    devices, _, atom_total = gathered.shape
+    clusters, listed = pair_lists.shape[2:]
+    vmem = pl.BlockSpec(memory_space=pltpu.VMEM)
+    flags = pltpu.SemaphoreType.DMA((devices - 1,))
+    return pl.pallas_call(
+        functools.partial(finish_kernel, (count_x, count_y), (cells_x, cells_y)),
+        in_specs=[pl.BlockSpec(memory_space=pltpu.SMEM), vmem, vmem],
+        out_specs=[vmem, vmem],
+        out_shape=[jax.ShapeDtypeStruct((3, 1, 1, atom_total), jnp.float32)] * 2,
+        scratch_shapes=[
+            pltpu.VMEM((devices - 1, *partial.shape[1:]), jnp.float32),
+            pltpu.VMEM((3, atom_total, 128), jnp.float32),
+            pltpu.VMEM((clusters, 4, 8, listed * atom_total // clusters), jnp.float32),
+            pltpu.VMEM((3, atom_total, 128), jnp.float32),
+            flags,
+            flags,
+        ],
+        compiler_params=pltpu.CompilerParams(collective_id=1, has_side_effects=True),
+        name="finish",
+    )(pair_lists, partial, gathered)
+
+
 def green_table(period):
     index = np.arange(period)
     signed = np.where(index <= period // 2, index, index - period) / (period * spacing)
@@ -428,7 +589,7 @@
     return own_rows[3] * jnp.sum(weight[None] * offsets, axis=2)
 
 
-def far_by_planes(gathered, own_charge, count_x, count_y, cells_x, cells_y):
+def far_by_planes(gathered, count_x, count_y, cells_x, cells_y):
     devices = count_x * count_y
     place = lax.axis_index("gx") * count_y + lax.axis_index("gy")
     depth = GRID_Z // devices
@@ -475,9 +636,7 @@
         scratch_shapes=[pltpu.VMEM((depth, rows, GRID_Y), jnp.float32)] * 2 + 2 * bank,
         name="mesh",
     )(gathered, *turn_x, *turn_y, column, row, table)
-    parts = lax.all_to_all(partial, ("gx", "gy"), split_axis=0, concat_axis=0, tiled=True)
-    total = jnp.sum(parts, axis=0)[:3]
-    return total * (-own_charge / spacing)
+    return partial
 
 
 def convolved_by_lines(charge_mesh, count_x, count_y):
@@ -588,12 +747,12 @@
     by_planes = GRID_Z % devices == 0 and cells_y == 64 and cells_x % 8 == 0
     if by_planes:
         gathered = shared(atoms, count_x, count_y)
-    else:
-        gathered = lax.all_gather(atoms, ("gx", "gy"), axis=0, tiled=False)
-    if by_planes:
-        far_part = far_by_planes(gathered, charge, count_x, count_y, cells_x, cells_y)
-    else:
-        far_part = far_by_lines(atoms, base, count_x, count_y, cells_x, cells_y, cells_z)
+        partial = far_by_planes(gathered, count_x, count_y, cells_x, cells_y)
+        return tuple(
+            finished(pair_lists, partial, gathered, count_x, count_y, cells_x, cells_y)
+        )
+    gathered = lax.all_gather(atoms, ("gx", "gy"), axis=0, tiled=False)
+    far_part = far_by_lines(atoms, base, count_x, count_y, cells_x, cells_y, cells_z)
 
     chosen = pair_lists[0, 0]
     beside = chosen // clusters

time: 96.7 us -> 86.2 us (0.89)
  other arithmetic: 18.4 us -> 0.62 us
  Pallas kernels: 65.6 us -> 80.7 us
  starting transfers between devices: 5.97 us -> 0 us
  local copies, waits for them, and re-layouts: 4.27 us -> 3.22 us
    pallas_call x0 -> x1, Pallas kernels: none -> 15.1 us  [finished(): pl.pallas_call(functools.partial(finish_kernel, (count_x, count_y), (cell...]
    mul x9 -> x0, other arithmetic: 12.3 us -> none  [the longest x8 12.3 us: one_cluster(): return own_rows[3] * jnp.sum(weight[None] * offsets, axis=2)]
    all_to_all x1 -> x0, starting transfers between devices: 5.97 us -> none  [far_by_planes(): lax.all_to_all(partial, ('gx', 'gy'), split_axis=0, concat_axis=0, tiled=...]
    reduce_sum x9 -> x0, other arithmetic: 3.89 us -> none  [the longest x4 2.04 us: one_cluster(): return own_rows[3] * jnp.sum(weight[None] * offsets, axis=2)]
  transfers between devices with their start and end apart: 1 -> 0, of which waited for: 0 -> 0; matrix products, arithmetic and copies ran while one was open for 20% -> 0% of each run, Pallas kernels for 0% -> 0%
where the time goes in v1:
time: 86.2 us; the launch traced here: 85.9 us
  Pallas kernels  80.7 us (94%)
  local copies, waits for them, and re-layouts  3.22 us (4%)
  between operations  1.36 us (2%)
    pallas_call x1, Pallas kernels, far_by_planes(): pl.pallas_call(functools.partial(mesh_kernel, (count_x, count_y), (cells_...  52.3 us
    pallas_call x1, Pallas kernels, finished(): pl.pallas_call(functools.partial(finish_kernel, (count_x, count_y), (cell...  15.1 us
    pallas_call x1, Pallas kernels, shared(): pl.pallas_call(functools.partial(share_kernel, (count_x, count_y)), in_sp...  13.4 us
    unnamed x9, local copies, waits for them, and re-layouts  1.93 us

profile of v1, /device:TPU:0, one launch (start us, length us, event | category | flops | bytes accessed | tf_op | source)
XLA Modules:
  0.0 85.9 jit_solution(11513973494242383701)
XLA Ops:
  0.6 0.0 copy-start
  1.3 0.0 copy-start.2
  1.3 1.3 %constant_dynamic-slice_fusion.table_ref = f32[8,11]{1,0:T(8,128)} fusion(f32[128,11]{1,0:T(8,128)} %constant.28.clone, s32[]{:T(128)S(6)} %select_n.15), kind=kLoop, calls=%fused_computation.2 | loop fusion | bytes 708 | tf_op jit(solution)/shard_map/dynamic_slice | solution.py:618
  2.6 0.0 copy-done.2
  2.6 0.0 copy-done
  2.6 0.6 maximum_bitcast_fusion.atoms_ref
  3.2 13.4 %share.1.atoms_ref = f32[16,4,1024]{2,1,0:T(4,128)} custom-call(f32[4,1024]{1,0:T(4,128)} %maximum_bitcast_fusion.atoms_ref), custom_call_target="tpu_custom_call" | custom-call | tf_op jit(solution)/shard_map/share/pallas_call | solution.py:217
  16.6 52.3 %mesh.1.partial_ref = f32[16,4,1024]{2,1,0:T(4,128)} custom-call(f32[16,4,1024]{2,1,0:T(4,128)} %share.1.atoms_ref, bf16[256,256]{1,0:T(8,128)(2,1)} %constant.33.xh_ref.yh_ref, bf16[256,256]{1,0:T(8,128)(2,1)} %constant.36.xl_ref.yl_ref, bf16[256,256]{1,0:T(8,128)(2,1)} %constant.33.xh_ref.yh_ref, bf16[256,256]{1,0:T(8,128)(2,1)} %constant.36.xl_ref.yl_ref, ...), custom_call_target="tpu_custom_call" | custom-call | tf_op jit(solution)/shard_map/mesh/pallas_call | solution.py:631
  68.9 15.1 %finish.1 = (f32[3,1,1,1024]{3,2,1,0:T(1,128)}, f32[3,1,1,1024]{3,2,1,0:T(1,128)}) custom-call(s32[1,1,4,4]{3,2,1,0:T(4,128)} %pairs_ref.1, f32[16,4,1024]{2,1,0:T(4,128)} %mesh.1.partial_ref, f32[16,4,1024]{2,1,0:T(4,128)} %share.1.atoms_ref), custom_call_target="tpu_custom_call" | custom-call | tf_op jit(solution)/shard_map/finish/pallas_call | solution.py:538
  84.0 0.0 copy-start.1
  84.0 1.3 %copy.15 = f32[3,1,1,1024]{3,2,1,0:T(1,128)} copy(f32[3,1,1,1024]{3,2,1,0:T(1,128)} %get-tuple-element.4) | data formatting | bytes 24576
  85.3 0.0 copy-done.1
  85.3 0.6 copy.16
  (2 shorter events, 0.0 us)
Async XLA Ops:
  0.6 2.0 %copy-start = (f32[3,1,1,1024]{3,2,1,0:T(1,128)S(1)}, f32[3,1,1,1024]{3,2,1,0:T(1,128)}, u32[]{:S(2)}) copy-start(f32[3,1,1,1024]{3,2,1,0:T(1,128)} %param.10) | copy-start | bytes 36868
  1.3 1.3 %copy-start.2 = (f32[1,1,1024]{2,1,0:T(1,128)S(1)}, f32[1,1,1024]{2,1,0:T(1,128)}, u32[]{:S(2)}) copy-start(f32[1,1,1024]{2,1,0:T(1,128)} %param.11) | copy-start | bytes 12292
  84.0 1.3 %copy-start.1 = (f32[3,1,1,1024]{3,2,1,0:T(1,128)S(1)}, f32[3,1,1,1024]{3,2,1,0:T(1,128)}, u32[]{:S(2)}) copy-start(f32[3,1,1,1024]{3,2,1,0:T(1,128)} %get-tuple-element.5) | copy-start | bytes 36868

commit v2 on v1

--- a/solution.py
+++ b/solution.py
@@ -20,6 +20,10 @@
 soft_core = 0.09
 root_factor = 1.1283791670955126
 rows_group = 8
+lanes = 128
+window_rows = 24
+group_size = 4
+plane_group = 2
 
 
 def moved(value, step_x, step_y):
@@ -177,55 +181,160 @@
         out_ref[pl.ds(place, 1), :] = factor * jnp.sum(sums[place], axis=0, keepdims=True)
 
 
-def share_kernel(sizes, atoms_ref, out_ref, send_sem, recv_sem):
-    count_x, count_y = sizes
+def peers_of(count_x, count_y):
     place_x, place_y = (lax.axis_index("gx"), lax.axis_index("gy"))
-    me = place_x * count_y + place_y
     peers = []
     for order in range(1, count_x * count_y):
         peer_x = lax.rem(place_x + order // count_y, count_x)
         peer_y = lax.rem(place_y + order % count_y, count_y)
-        peers.append({"gx": peer_x, "gy": peer_y})
+        peers.append((peer_x, peer_y))
+    return peers
+
+
+def share_kernel(sizes, cells, count_ref, position_ref, charge_ref, raw_ref, sorted_ref, bounds_ref, rank_ref, key_ref, split_ref, raw_send, raw_recv, sort_send, sort_recv, mark_send, mark_recv):
+    count_x, count_y = sizes
+    cells_x, _ = cells
+    place_x, place_y = (lax.axis_index("gx"), lax.axis_index("gy"))
+    me = place_x * count_y + place_y
+    peers = peers_of(count_x, count_y)
     barrier = pltpu.get_barrier_semaphore()
-    for peer in peers:
+    for peer_x, peer_y in peers:
         pl.semaphore_signal(
-            barrier, inc=1, device_id=peer, device_id_type=pl.DeviceIdType.MESH
+            barrier,
+            inc=1,
+            device_id={"gx": peer_x, "gy": peer_y},
+            device_id_type=pl.DeviceIdType.MESH,
         )
-    pl.semaphore_wait(barrier, len(peers))
-    copies = [
-        pltpu.make_async_remote_copy(
-            src_ref=atoms_ref,
-            dst_ref=out_ref.at[me],
+
+    def sent(source, target, send_sem, recv_sem, order):
+        peer_x, peer_y = peers[order]
+        return pltpu.make_async_remote_copy(
+            src_ref=source.at[me],
+            dst_ref=target.at[me],
             send_sem=send_sem.at[order],
             recv_sem=recv_sem.at[order],
-            device_id=peer,
+            device_id={"gx": peer_x, "gy": peer_y},
             device_id_type=pl.DeviceIdType.MESH,
         )
-        for order, peer in enumerate(peers)
+
+    atom_total = charge_ref.shape[2]
+    tiles = atom_total // lanes
+    slot = lax.broadcasted_iota(jnp.int32, (1, atom_total), 1)
+    living = slot < count_ref[0, 0]
+    charge = jnp.where(living, charge_ref[0], 0.0)
+    rows = [position_ref[axis, 0] for axis in range(3)] + [charge]
+    for axis in range(4):
+        raw_ref[me, pl.ds(axis, 1), :] = rows[axis]
+    column = jnp.clip(jnp.floor(rows[0]), 0.0, cells_x - 1.0)
+    key = jnp.where(living, column, float(cells_x)) * float(atom_total) + slot.astype(jnp.float32)
+    for tile in range(tiles):
+        span = slice(tile * lanes, (tile + 1) * lanes)
+        key_ref[span, :] = jnp.broadcast_to(key[:, span], (lanes, lanes)).T
+    wide = [
+        jnp.broadcast_to(key[:, tile * lanes : (tile + 1) * lanes], (8, lanes))
+        for tile in range(tiles)
     ]
+
+    def count_group(group, totals):
+        for inner in range(8):
+            others = key_ref[pl.ds(pl.multiple_of(group * 64 + inner * 8, 8), 8), :]
+            totals = tuple(
+                total + jnp.where(others < own, 1.0, 0.0) for total, own in zip(totals, wide)
+            )
+        return totals
+
+    zero = jnp.zeros((8, lanes), jnp.float32)
+    totals = lax.fori_loop(0, atom_total // 64, count_group, (zero,) * tiles)
+    for tile, total in enumerate(totals):
+        rank_ref[:, tile * lanes : (tile + 1) * lanes] = jnp.sum(total, axis=0, keepdims=True)
+
+    pl.semaphore_wait(barrier, len(peers))
+    beside = sorted(
+        {
+            step_x % count_x * count_y + step_y % count_y
+            for step_x in (-1, 0, 1)
+            for step_y in (-1, 0, 1)
+        }
+        - {0}
+    )
+    copies = [sent(raw_ref, raw_ref, raw_send, raw_recv, order - 1) for order in beside]
     for copy in copies:
         copy.start()
-    out_ref[me] = atoms_ref[...]
-    for copy in copies:
+
+    split_ref[...] = jnp.zeros_like(split_ref)
+    rest = raw_ref[me]
+    for part in range(3):
+        piece = rest.astype(jnp.bfloat16).astype(jnp.float32)
+        split_ref[4 * part : 4 * part + 4, :] = piece
+        rest = rest - piece
+    split = split_ref[...].astype(jnp.bfloat16)
+    rank = rank_ref[...]
+    block = 2 * lanes
+    for part in range(atom_total // block):
+        place = lax.broadcasted_iota(jnp.int32, (block, atom_total), 0) + part * block
+        chosen = jnp.where(place.astype(jnp.float32) == rank, 1.0, 0.0).astype(jnp.bfloat16)
+        found = lax.dot_general(
+            split, chosen, (((1,), (1,)), ((), ())), preferred_element_type=jnp.float32
+        )
+        found = (found[0:4] + found[4:8]) + found[8:12]
+        for tile in range(block // lanes):
+            row = part * (block // lanes) + tile
+            for axis in range(4):
+                sorted_ref[me, axis, row : row + 1, :] = found[
+                    axis : axis + 1, tile * lanes : (tile + 1) * lanes
+                ]
+    spot = lax.broadcasted_iota(jnp.int32, (tiles, lanes), 0) * lanes
+    spot = spot + lax.broadcasted_iota(jnp.int32, (tiles, lanes), 1)
+    inside = spot < count_ref[0, 0]
+    column = jnp.clip(jnp.floor(sorted_ref[me, 0]), 0.0, cells_x - 1.0)
+    lowest = jnp.min(jnp.where(inside, column, float(cells_x)), axis=1, keepdims=True)
+    highest = jnp.max(jnp.where(inside, column, -1.0), axis=1, keepdims=True)
+    first = jnp.floor(lowest * 0.125)
+    last = jnp.floor((highest + 3.0) * 0.125)
+    windows = jnp.where(
+        highest >= 0.0, jnp.floor((last - first) * (8.0 / window_rows) + 0.01) + 1.0, 0.0
+    )
+    lane = lax.broadcasted_iota(jnp.int32, (tiles, lanes), 1)
+    row = lax.broadcasted_iota(jnp.int32, (tiles, lanes), 0)
+    marks = jnp.where(lane == row, first, jnp.where(lane == row + tiles, windows, 0.0))
+    marks = jnp.sum(marks, axis=0, keepdims=True)
+    bounds_ref[me] = marks.astype(jnp.int32)
+
+    everyone = range(len(peers))
+    later = [sent(sorted_ref, sorted_ref, sort_send, sort_recv, order) for order in everyone]
+    later += [sent(bounds_ref, bounds_ref, mark_send, mark_recv, order) for order in everyone]
+    for copy in later:
+        copy.start()
+    for copy in copies + later:
         copy.wait()
 
 
-def shared(atoms, count_x, count_y):
+def shared(positions, charges, atom_counts, count_x, count_y, cells_x, cells_y):
     devices = count_x * count_y
+    atom_total = charges.shape[2]
     vmem = pl.BlockSpec(memory_space=pltpu.VMEM)
     flags = pltpu.SemaphoreType.DMA((devices - 1,))
     return pl.pallas_call(
-        functools.partial(share_kernel, (count_x, count_y)),
-        in_specs=[vmem],
-        out_specs=vmem,
-        out_shape=jax.ShapeDtypeStruct((devices, *atoms.shape), jnp.float32),
-        scratch_shapes=[flags, flags],
+        functools.partial(share_kernel, (count_x, count_y), (cells_x, cells_y)),
+        in_specs=[pl.BlockSpec(memory_space=pltpu.SMEM), vmem, vmem],
+        out_specs=[vmem] * 4,
+        out_shape=[
+            jax.ShapeDtypeStruct((devices, 4, atom_total), jnp.float32),
+            jax.ShapeDtypeStruct((devices, 4, atom_total // lanes, lanes), jnp.float32),
+            jax.ShapeDtypeStruct((devices, 1, lanes), jnp.int32),
+            jax.ShapeDtypeStruct((1, atom_total), jnp.float32),
+        ],
+        scratch_shapes=[
+            pltpu.VMEM((atom_total, lanes), jnp.float32),
+            pltpu.VMEM((16, atom_total), jnp.float32),
+        ]
+        + [flags] * 6,
         compiler_params=pltpu.CompilerParams(collective_id=0, has_side_effects=True),
         name="share",
-    )(atoms)
-
-
-def depth_rows(table, height, fraction, terms):
+    )(atom_counts, positions, charges)
+
+
+def depth_rows(table, height, terms):
     turns = height * table[:, 0:1]
     quarter = GRID_Z // 4
     nearest = jnp.floor(turns * (1.0 / quarter) + 0.5)
@@ -253,68 +362,156 @@
     return results
 
 
-def mesh_kernel(sizes, cells, pad, atoms_ref, xh_ref, xl_ref, yh_ref, yl_ref, column_ref, row_ref, table_ref, out_ref, mesh_ref, turned_ref, *scratch):
+def mesh_kernel(sizes, cells, pad_y, bounds_ref, atoms_ref, xh_ref, xl_ref, yh_ref, yl_ref, column_ref, row_ref, table_ref, out_ref, mesh_ref, stack_ref, prep_ref, deep_ref, steep_ref, near_ref, wy_ref, side_ref, level_ref, square_ref, scale_ref):
     count_x, count_y = sizes
     cells_x, cells_y = cells
-    pad_x, pad_y = pad
-    atom_total = atoms_ref.shape[2]
-    depth = table_ref.shape[0]
+    devices = count_x * count_y
+    place = lax.axis_index("gx") * count_y + lax.axis_index("gy")
+    tiles = atoms_ref.shape[2]
+    depth = stack_ref.shape[0]
     window = 2 * cells_y
     windows = GRID_Y // window
-    lane = lax.broadcasted_iota(jnp.int32, (depth * pad_x, window), 1)
+    chunks = tiles
+    extra = 8
     mesh_ref[...] = jnp.zeros_like(mesh_ref)
-    table = table_ref[...]
-    per_side = len(scratch) // 2
-    banks = (scratch[:per_side], scratch[per_side:])
-    for _, _, wy_ref, _, _, _, _, side_ref in banks:
-        wy_ref[...] = jnp.zeros_like(wy_ref)
-        side_ref[...] = jnp.zeros_like(side_ref)
-
-    def atoms_of(cell, row):
-        return atoms_ref[cell, row : row + 1, :]
-
-    def spread_cell(cell, i, j):
-        wx_ref, vx_ref, wy_ref, hi_ref, lo_ref, level_ref, stack_ref, side_ref = banks[j % 2]
-        low_x, frac_x = split_cells(atoms_of(cell, 0), 0.0, cells_x)
-        low_y, frac_y = split_cells(atoms_of(cell, 1), 0.0, cells_y)
-        wx_ref[...] = spline_table(low_x, spline_weights(frac_x)[0], pad_x)
-        high, low = halves(spline_table(low_y, spline_weights(frac_y)[0], pad_y))
-        wy_ref[:pad_y, :] = high
-        wy_ref[pl.ds(window, pad_y), :] = low
-        height = jnp.floor(atoms_of(cell, 2))
-        frac_z = atoms_of(cell, 2) - height
-        (deep,) = depth_rows(table, height, frac_z, [spline_weights(frac_z)[0]])
-        deep = deep * atoms_of(cell, 3)
-        for k in range(depth):
-            high, low = halves(deep[k : k + 1, :] * wx_ref[...])
-            hi_ref[pl.ds(k * pad_x, pad_x), :] = high
-            lo_ref[pl.ds(k * pad_x, pad_x), :] = low
-        numbers = (((1,), (1,)), ((), ()))
-        both = lax.dot_general(
-            hi_ref[...], wy_ref[...], numbers, preferred_element_type=jnp.float32
-        )
-        rest = lax.dot_general(
-            lo_ref[...], wy_ref[:window, :], numbers, preferred_element_type=jnp.float32
-        )
-        total = both[:, :window] + both[:, window:] + rest
-        rows = pl.ds(pl.multiple_of(i * cells_x, 8), pad_x)
-        m = j // 2
-        if j % 2 == 0:
-            mesh_ref[:, rows, pl.ds(m * window, window)] += total.reshape(depth, pad_x, window)
-        else:
-            total = pltpu.roll(total, cells_y, 1)
-            kept = jnp.where(lane >= cells_y, total, 0.0)
-            carried = jnp.where(lane < cells_y, total, 0.0)
-            after = (m + 1) % windows
-            mesh_ref[:, rows, pl.ds(m * window, window)] += kept.reshape(depth, pad_x, window)
-            mesh_ref[:, rows, pl.ds(after * window, window)] += carried.reshape(
-                depth, pad_x, window
-            )
-
-    @pl.loop(0, count_x)
-    def _(i):
-        for j in range(count_y):
-            spread_cell(i * count_y + j, i, j)
+    stack_ref[:, GRID_X:, :] = jnp.zeros_like(stack_ref[:, GRID_X:, :])
+    out_ref[...] = jnp.zeros_like(out_ref)
+    wy_ref[...] = jnp.zeros_like(wy_ref)
+    table = table_ref[pl.ds(pl.multiple_of(place * depth, 8), depth), :]
+
+    def prep_row(kind, cell, tile):
+        return prep_ref[pl.ds((kind * devices + cell) * tiles + tile, 8, stride=0), :]
+
+    @pl.loop(0, devices)
+    def _(cell):
+        def keep(kind, value):
+            rows = pl.ds(pl.multiple_of((kind * devices + cell) * tiles, 8), tiles)
+            prep_ref[rows, :] = value
+
+        for axis, count in enumerate((cells_x, cells_y)):
+            value = atoms_ref[cell, axis]
+            lowest = jnp.clip(jnp.floor(value), 0.0, count - 1.0)
+            values, slopes = spline_weights(value - lowest)
+            keep(9 * axis, lowest)
+            for term in range(4):
+                keep(9 * axis + 1 + term, values[term])
+                keep(9 * axis + 5 + term, slopes[term])
+        value = atoms_ref[cell, 2]
+        height = jnp.floor(value)
+        values, slopes = spline_weights(value - height)
+        keep(18, height)
+        for term in range(4):
+            keep(19 + term, values[term])
+            keep(23 + term, slopes[term])
+        keep(27, atoms_ref[cell, 3])
+        for tile in range(tiles):
+            height = prep_row(18, cell, tile)
+            terms = [[prep_row(19 + 4 * s + term, cell, tile) for term in range(4)] for s in range(2)]
+            deep, steep = depth_rows(table, height, terms)
+            rows = pl.ds(pl.multiple_of((cell * tiles + tile) * depth, 8), depth)
+            deep_ref[rows, :] = deep
+            steep_ref[rows, :] = steep
+
+    row_index = lax.broadcasted_iota(jnp.int32, (8, lanes), 0).astype(jnp.float32)
+
+    def looked_up(points, lowest, term_lists):
+        results = [jnp.zeros_like(points) for _ in term_lists]
+        for term in range(4):
+            hit = points == lowest + float(term)
+            results = [
+                jnp.where(hit, terms[term], result)
+                for terms, result in zip(term_lists, results)
+            ]
+        return results
+
+    def kinds(first, cell, tile):
+        return [prep_row(first + term, cell, tile) for term in range(4)]
+
+    stride = round_up(pad_y, 16)
+    far_away = 1.0e6
+
+    def window_of(cell, chunk, step):
+        first = bounds_ref[cell, 0, chunk]
+        count = bounds_ref[cell, 0, chunks + chunk]
+        begin = first * 8 + jnp.minimum(step, jnp.maximum(count - 1, 0)) * window_rows
+        base = jnp.where(step < count, begin.astype(jnp.float32), far_away)
+        return (begin, base)
+
+    def window_count(cell, chunk):
+        counts = [bounds_ref[cell, 0, chunks + chunk + place] for place in range(group_size)]
+        return functools.reduce(jnp.maximum, counts)
+
+    def y_table(cell, chunk, kind):
+        lowest = prep_row(9, cell, chunk)
+        terms = kinds(kind, cell, chunk)
+        for group in range(stride // 16):
+            pieces = [
+                looked_up(row_index + float(group * 16 + half * 8), lowest, [terms])[0]
+                if group * 16 + half * 8 < pad_y
+                else jnp.zeros_like(row_index)
+                for half in range(2)
+            ]
+            yield (slice(group * 16, group * 16 + 16), *halves(jnp.concatenate(pieces, axis=0)))
+
+    steps_x = window_rows // 8
+
+    def spread_group(cell, group, i, m, odd):
+        @pl.loop(0, window_count(cell, group * group_size))
+        def _(step):
+            for place in range(group_size):
+                chunk = group * group_size + place
+                spot = cell * chunks + chunk
+                for rows, high, low in y_table(cell, chunk, 10):
+                    after = slice(window + rows.start, window + rows.stop)
+                    later = slice(stride + rows.start, stride + rows.stop)
+                    wy_ref[place, rows, :lanes] = high
+                    wy_ref[place, rows, lanes:] = high
+                    wy_ref[place, after, :lanes] = low
+                    near_ref[spot, rows, :] = high
+                    near_ref[spot, later, :] = low
+                begin, base = window_of(cell, chunk, step)
+                lowest = prep_row(0, cell, chunk) - base
+                charge = prep_row(27, cell, chunk)
+                terms = [term * charge for term in kinds(1, cell, chunk)]
+                weights = [
+                    looked_up(row_index + float(tile * 8), lowest, [terms])[0]
+                    for tile in range(steps_x)
+                ]
+                modes = [
+                    deep_ref[pl.ds((cell * tiles + chunk) * depth + k, 8, stride=0), :]
+                    for k in range(depth)
+                ]
+                blocks = [weight * mode for mode in modes for weight in weights]
+                for pair in range(len(blocks) // 2):
+                    high, low = halves(
+                        jnp.concatenate(blocks[2 * pair : 2 * pair + 2], axis=0)
+                    )
+                    rows = slice(pair * 16, pair * 16 + 16)
+                    side_ref[place, rows, :lanes] = high
+                    side_ref[place, rows, lanes:] = low
+            totals = []
+            for place in range(group_size):
+                total = lax.dot_general(
+                    side_ref[place],
+                    wy_ref[place],
+                    (((1,), (1,)), ((), ())),
+                    preferred_element_type=jnp.float32,
+                )
+                totals.append(total[:, :window] + total[:, window:])
+            for place, total in enumerate(totals):
+                begin, _ = window_of(cell, group * group_size + place, step)
+                rows = pl.ds(pl.multiple_of(i * cells_x + begin, 8), window_rows)
+                here = pl.ds(pl.multiple_of(m * window, lanes), window)
+                mesh_ref[odd, :, rows, here] += total.reshape(depth, window_rows, window)
+
+    @pl.loop(0, devices)
+    def _(cell):
+        i = lax.div(cell, count_y)
+        j = lax.rem(cell, count_y)
+
+        @pl.loop(0, chunks // group_size)
+        def _(group):
+            spread_group(cell, group, i, lax.div(j, 2), lax.rem(j, 2))
 
     def across(value):
         high, low = halves(value)
@@ -324,72 +521,116 @@
         high, low = halves(value)
         return dot(high, yh_ref[...]) + dot(high, yl_ref[...]) + dot(low, yh_ref[...])
 
-    extra = mesh_ref.shape[1] - GRID_X
-
-    @pl.loop(0, depth)
-    def _(k):
-        mesh_ref[k, :extra, :] += mesh_ref[k, GRID_X:, :]
-        waves = along(across(mesh_ref[k, :GRID_X, :]))
-        square = column_ref[:, 0:1] + row_ref[0:1, :] + table_ref[pl.ds(k, 1), 9:10]
-        scale = column_ref[:, 1:2] * row_ref[1:2, :] * table_ref[pl.ds(k, 1), 10:11]
-        green = jnp.where(square > 0.0, scale / jnp.where(square > 0.0, square, 1.0), 0.0)
+    plane_lane = lax.broadcasted_iota(jnp.int32, (GRID_X, window), 1)
+
+    shape = (GRID_X, GRID_Y)
+    square_ref[...] = jnp.broadcast_to(column_ref[:, 0:1], shape) + row_ref[0:1, :]
+    scale_ref[...] = jnp.broadcast_to(column_ref[:, 1:2], shape) * row_ref[1:2, :]
+
+    def one_plane(k):
+        charge = mesh_ref[0, k, :GRID_X, :] + pltpu.roll(mesh_ref[1, k, :GRID_X, :], cells_y, 1)
+        over = slice(GRID_X, GRID_X + extra)
+        beyond = mesh_ref[0, k, over, :] + pltpu.roll(mesh_ref[1, k, over, :], cells_y, 1)
+        charge = jnp.concatenate([charge[:extra] + beyond, charge[extra:]], axis=0)
+        waves = along(across(charge))
+        mode = pl.ds(place * depth + k, 1)
+        square = square_ref[...] + table_ref[mode, 9:10]
+        scale = scale_ref[...] * table_ref[mode, 10:11]
+        green = jnp.where(square > 0.0, scale / square, 0.0)
         plane = across(along(waves * green))
-        mesh_ref[k, :GRID_X, :] = plane
-        mesh_ref[k, GRID_X:, :] = plane[:extra]
-        rolled = pltpu.roll(plane, GRID_Y - cells_y, 1)
-        turned_ref[k, :GRID_X, :] = rolled
-        turned_ref[k, GRID_X:, :] = rolled[:extra]
-
-    stride = round_up(pad_y, 16)
-    groups = pad_x // 8
-
-    def gather_cell(cell, i, j):
-        wx_ref, vx_ref, wy_ref, hi_ref, lo_ref, level_ref, stack_ref, side_ref = banks[j % 2]
-        low_x, frac_x = split_cells(atoms_of(cell, 0), 0.0, cells_x)
-        low_y, frac_y = split_cells(atoms_of(cell, 1), 0.0, cells_y)
-        values, slopes = spline_weights(frac_x)
-        wx_ref[...] = spline_table(low_x, values, pad_x)
-        vx_ref[...] = spline_table(low_x, slopes, pad_x)
-        for place, terms in enumerate(spline_weights(frac_y)):
-            high, low = halves(spline_table(low_y, terms, stride))
-            span = pl.ds(place * atom_total, atom_total)
-            side_ref[:stride, span] = high
-            side_ref[pl.ds(stride, stride), span] = low
-            side_ref[pl.ds(2 * stride, stride), span] = high
-        height = jnp.floor(atoms_of(cell, 2))
-        frac_z = atoms_of(cell, 2) - height
-        deep, steep = depth_rows(table, height, frac_z, spline_weights(frac_z))
-        source = mesh_ref if j % 2 == 0 else turned_ref
-        rows = pl.ds(pl.multiple_of(i * cells_x, 8), pad_x)
-        block = source[:, rows, pl.ds(j // 2 * window, window)].reshape(depth * pad_x, window)
-        high = block.astype(jnp.bfloat16).astype(jnp.float32)
-        low = block - high
-        shifted = pltpu.roll(high, stride, 1)
-        stack_ref[:, :window] = jnp.where(lane < stride, high, shifted).astype(jnp.bfloat16)
-        stack_ref[:, window:] = jnp.where(
-            lane < 2 * stride - window, shifted, pltpu.roll(low, 2 * stride - window, 1)
-        ).astype(jnp.bfloat16)
-        level_ref[...] = dot(stack_ref[...], side_ref[...])
-        zero = jnp.zeros((8, atom_total), jnp.float32)
-        first, second, third = (zero, zero, zero)
-        for k in range(depth):
-            flat = level_ref[pl.ds(k * pad_x, pad_x), :atom_total]
-            tilt = level_ref[pl.ds(k * pad_x, pad_x), atom_total:]
-            weight = wx_ref[...]
-            part_x = jnp.sum((vx_ref[...] * flat).reshape(groups, 8, atom_total), axis=0)
-            part_y = jnp.sum((weight * tilt).reshape(groups, 8, atom_total), axis=0)
-            part_z = jnp.sum((weight * flat).reshape(groups, 8, atom_total), axis=0)
-            first = first + deep[k : k + 1, :] * part_x
-            second = second + deep[k : k + 1, :] * part_y
-            third = third + steep[k : k + 1, :] * part_z
-        for place, value in enumerate((first, second, third)):
-            out_ref[cell, pl.ds(place, 1), :] = jnp.sum(value, axis=0, keepdims=True)
-        out_ref[cell, 3:4, :] = jnp.zeros((1, atom_total), jnp.float32)
-
-    @pl.loop(0, count_x)
-    def _(i):
-        for j in range(count_y):
-            gather_cell(i * count_y + j, i, j)
+        for odd in range(2):
+            if odd:
+                plane = pltpu.roll(plane, GRID_Y - cells_y, 1)
+            for j_half in range(windows):
+                j = 2 * j_half + odd
+                block = plane[:, j_half * window : (j_half + 1) * window]
+                high = block.astype(jnp.bfloat16).astype(jnp.float32)
+                low = block - high
+                shifted = pltpu.roll(high, stride, 1)
+                left = jnp.where(plane_lane < stride, high, shifted)
+                right = jnp.where(
+                    plane_lane < 2 * stride - window,
+                    shifted,
+                    pltpu.roll(low, 2 * stride - window, 1),
+                )
+                for side, value in enumerate((left, right)):
+                    span = slice((2 * j + side) * window, (2 * j + side + 1) * window)
+                    stack_ref[k, :GRID_X, span] = value
+                    stack_ref[k, GRID_X : GRID_X + extra, span] = value[:extra]
+
+    @pl.loop(0, depth // plane_group)
+    def _(pair):
+        for inner in range(plane_group):
+            one_plane(pair * plane_group + inner)
+
+    def gather_group(cell, group, i, j):
+        @pl.loop(0, window_count(cell, group * group_size))
+        def _(step):
+            blank = jnp.zeros((2 * window - 3 * stride, lanes), jnp.bfloat16)
+            for place in range(group_size):
+                chunk = group * group_size + place
+                near = near_ref[cell * chunks + chunk]
+                highs, lows = [], []
+                for _, high, low in y_table(cell, chunk, 14):
+                    highs.append(high)
+                    lows.append(low)
+                columns = jnp.concatenate(
+                    [
+                        jnp.concatenate([near, near[:stride], blank], axis=0),
+                        jnp.concatenate([*highs, *lows, *highs, blank], axis=0),
+                    ],
+                    axis=1,
+                )
+                begin, _ = window_of(cell, chunk, step)
+                rows = pl.ds(pl.multiple_of(i * cells_x + begin, 8), window_rows)
+                span = pl.ds(pl.multiple_of(j * 2 * window, lanes), 2 * window)
+                block = stack_ref[:, rows, span].reshape(depth * window_rows, 2 * window)
+                level_ref[place] = dot(block.astype(jnp.bfloat16), columns)
+            for place in range(group_size):
+                chunk = group * group_size + place
+                _, base = window_of(cell, chunk, step)
+                lowest = prep_row(0, cell, chunk) - base
+                values = kinds(1, cell, chunk)
+                slopes = kinds(5, cell, chunk)
+                spots = [
+                    pl.ds((cell * tiles + chunk) * depth + k, 8, stride=0) for k in range(depth)
+                ]
+                deep = [deep_ref[spot, :] for spot in spots]
+                steep = [steep_ref[spot, :] for spot in spots]
+                zero = jnp.zeros((8, lanes), jnp.float32)
+                sums = [zero, zero, zero]
+                for tile in range(steps_x):
+                    weight, slope = looked_up(
+                        row_index + float(tile * 8), lowest, [values, slopes]
+                    )
+                    parts = [zero, zero, zero]
+                    for k in range(depth):
+                        at = slice(k * window_rows + tile * 8, k * window_rows + tile * 8 + 8)
+                        flat = level_ref[place, at, :lanes]
+                        tilt = level_ref[place, at, lanes:]
+                        parts = [
+                            parts[0] + deep[k] * flat,
+                            parts[1] + deep[k] * tilt,
+                            parts[2] + steep[k] * flat,
+                        ]
+                    sums = [
+                        sums[0] + slope * parts[0],
+                        sums[1] + weight * parts[1],
+                        sums[2] + weight * parts[2],
+                    ]
+                for axis in range(3):
+                    out_ref[cell, axis, pl.ds(chunk, 1), :] += jnp.sum(
+                        sums[axis], axis=0, keepdims=True
+                    )
+
+    @pl.loop(0, devices)
+    def _(cell):
+        i = lax.div(cell, count_y)
+        j = lax.rem(cell, count_y)
+
+        @pl.loop(0, chunks // group_size)
+        def _(group):
+            gather_group(cell, group, i, j)
 
 
 root_terms = (
@@ -428,17 +669,7 @@
     return total[0:1, :]
 
 
-def peers_of(count_x, count_y):
-    place_x, place_y = (lax.axis_index("gx"), lax.axis_index("gy"))
-    peers = []
-    for order in range(1, count_x * count_y):
-        peer_x = lax.rem(place_x + order // count_y, count_x)
-        peer_y = lax.rem(place_y + order % count_y, count_y)
-        peers.append((peer_x, peer_y))
-    return peers
-
-
-def finish_kernel(sizes, cells, pairs_ref, partial_ref, atoms_ref, short_ref, long_ref, land_ref, column_ref, partner_ref, sum_ref, send_sem, recv_sem):
+def finish_kernel(sizes, cells, pairs_ref, partial_ref, atoms_ref, rank_ref, short_ref, long_ref, land_ref, column_ref, partner_ref, sum_ref, order_ref, force_ref, send_sem, recv_sem):
     count_x, count_y = sizes
     cells_x, cells_y = cells
     place_x, place_y = (lax.axis_index("gx"), lax.axis_index("gy"))
@@ -455,7 +686,6 @@
     clusters, listed = pairs_ref.shape[2:]
     atom_total = atoms_ref.shape[2]
     size = atom_total // clusters
-    lanes = 128
     for axis in range(3):
         for chunk in range(atom_total // lanes):
             row = atoms_ref[me, pl.ds(axis, 1), pl.ds(chunk * lanes, lanes)]
@@ -521,36 +751,58 @@
     own_charge = atoms_ref[me, 3:4, :]
     for axis in range(3):
         short_ref[axis, 0, :, :] = row_sums(sum_ref[axis]) * (own_charge * spacing)
+    rank = rank_ref[...]
+
+    @pl.loop(0, atom_total // size)
+    def _(block):
+        place = lax.broadcasted_iota(jnp.int32, (size, atom_total), 0) + block * size
+        order_ref[pl.ds(pl.multiple_of(block * size, size), size), :] = jnp.where(
+            place.astype(jnp.float32) == rank, 1.0, 0.0
+        ).astype(jnp.bfloat16)
+
+    force_ref[...] = jnp.zeros_like(force_ref)
     for copy in copies:
         copy.wait()
     total = partial_ref[me]
     for order in range(len(peers)):
         total = total + land_ref[order]
+    for part in range(3):
+        piece = total.astype(jnp.bfloat16).astype(jnp.float32)
+        total = total - piece
+        for axis in range(3):
+            for tile in range(atom_total // lanes):
+                span = slice(tile * lanes, (tile + 1) * lanes)
+                row = 4 * part + axis
+                force_ref[row : row + 1, span] = piece[axis, tile : tile + 1, :]
+    placed = dot(force_ref[...].astype(jnp.bfloat16), order_ref[...])
+    placed = (placed[0:4] + placed[4:8]) + placed[8:12]
     for axis in range(3):
-        long_ref[axis, 0, :, :] = total[axis : axis + 1, :] * (own_charge * (-1.0 / spacing))
-
-
-def finished(pair_lists, partial, gathered, count_x, count_y, cells_x, cells_y):
-    devices, _, atom_total = gathered.shape
+        long_ref[axis, 0, :, :] = placed[axis : axis + 1, :] * (own_charge * (-1.0 / spacing))
+
+
+def finished(pair_lists, partial, raw, rank, count_x, count_y, cells_x, cells_y):
+    devices, _, atom_total = raw.shape
     clusters, listed = pair_lists.shape[2:]
     vmem = pl.BlockSpec(memory_space=pltpu.VMEM)
     flags = pltpu.SemaphoreType.DMA((devices - 1,))
     return pl.pallas_call(
         functools.partial(finish_kernel, (count_x, count_y), (cells_x, cells_y)),
-        in_specs=[pl.BlockSpec(memory_space=pltpu.SMEM), vmem, vmem],
+        in_specs=[pl.BlockSpec(memory_space=pltpu.SMEM), vmem, vmem, vmem],
         out_specs=[vmem, vmem],
         out_shape=[jax.ShapeDtypeStruct((3, 1, 1, atom_total), jnp.float32)] * 2,
         scratch_shapes=[
             pltpu.VMEM((devices - 1, *partial.shape[1:]), jnp.float32),
-            pltpu.VMEM((3, atom_total, 128), jnp.float32),
+            pltpu.VMEM((3, atom_total, lanes), jnp.float32),
             pltpu.VMEM((clusters, 4, 8, listed * atom_total // clusters), jnp.float32),
-            pltpu.VMEM((3, atom_total, 128), jnp.float32),
+            pltpu.VMEM((3, atom_total, lanes), jnp.float32),
+            pltpu.VMEM((atom_total, atom_total), jnp.bfloat16),
+            pltpu.VMEM((16, atom_total), jnp.float32),
             flags,
             flags,
         ],
         compiler_params=pltpu.CompilerParams(collective_id=1, has_side_effects=True),
         name="finish",
-    )(pair_lists, partial, gathered)
+    )(pair_lists, partial, raw, rank)
 
 
 def green_table(period):
@@ -589,13 +841,12 @@
     return own_rows[3] * jnp.sum(weight[None] * offsets, axis=2)
 
 
-def far_by_planes(gathered, count_x, count_y, cells_x, cells_y):
+def far_by_planes(bounds, atoms, count_x, count_y, cells_x, cells_y):
     devices = count_x * count_y
-    place = lax.axis_index("gx") * count_y + lax.axis_index("gy")
     depth = GRID_Z // devices
-    atom_total = gathered.shape[2]
-    pad_x = round_up(cells_x + 3, 8)
+    tiles = atoms.shape[2]
     pad_y = round_up(cells_y + 3, 8)
+    stride = round_up(pad_y, 16)
     window = 2 * cells_y
     turn_x = halves(jnp.asarray(hartley(GRID_X)))
     turn_y = halves(jnp.asarray(hartley(GRID_Y)))
@@ -615,28 +866,29 @@
         ],
         axis=1,
     ).astype(np.float32)
-    table = lax.dynamic_slice_in_dim(jnp.asarray(table), place * depth, depth, axis=0)
     vmem = pl.BlockSpec(memory_space=pltpu.VMEM)
-    rows = GRID_X + pad_x - cells_x
-    bank = [
-        pltpu.VMEM((pad_x, atom_total), jnp.float32),
-        pltpu.VMEM((pad_x, atom_total), jnp.float32),
-        pltpu.VMEM((2 * window, atom_total), jnp.bfloat16),
-        pltpu.VMEM((depth * pad_x, atom_total), jnp.bfloat16),
-        pltpu.VMEM((depth * pad_x, atom_total), jnp.bfloat16),
-        pltpu.VMEM((depth * pad_x, 2 * atom_total), jnp.float32),
-        pltpu.VMEM((depth * pad_x, 2 * window), jnp.bfloat16),
-        pltpu.VMEM((2 * window, 2 * atom_total), jnp.bfloat16),
-    ]
-    partial = pl.pallas_call(
-        functools.partial(mesh_kernel, (count_x, count_y), (cells_x, cells_y), (pad_x, pad_y)),
-        in_specs=[vmem] * 8,
+    rows = GRID_X + window_rows
+    batch = depth * window_rows
+    return pl.pallas_call(
+        functools.partial(mesh_kernel, (count_x, count_y), (cells_x, cells_y), pad_y),
+        in_specs=[pl.BlockSpec(memory_space=pltpu.SMEM)] + [vmem] * 8,
         out_specs=vmem,
-        out_shape=jax.ShapeDtypeStruct((devices, 4, atom_total), jnp.float32),
-        scratch_shapes=[pltpu.VMEM((depth, rows, GRID_Y), jnp.float32)] * 2 + 2 * bank,
+        out_shape=jax.ShapeDtypeStruct((devices, 3, tiles, lanes), jnp.float32),
+        scratch_shapes=[
+            pltpu.VMEM((2, depth, rows, GRID_Y), jnp.float32),
+            pltpu.VMEM((depth, rows, 4 * GRID_Y), jnp.float32),
+            pltpu.VMEM((28 * devices * tiles, lanes), jnp.float32),
+            pltpu.VMEM((devices * tiles * depth, lanes), jnp.float32),
+            pltpu.VMEM((devices * tiles * depth, lanes), jnp.float32),
+            pltpu.VMEM((devices * tiles, 2 * stride, lanes), jnp.bfloat16),
+            pltpu.VMEM((group_size, 2 * window, 2 * lanes), jnp.bfloat16),
+            pltpu.VMEM((group_size, batch, 2 * lanes), jnp.bfloat16),
+            pltpu.VMEM((group_size, batch, 2 * lanes), jnp.float32),
+            pltpu.VMEM((GRID_X, GRID_Y), jnp.float32),
+            pltpu.VMEM((GRID_X, GRID_Y), jnp.float32),
+        ],
         name="mesh",
-    )(gathered, *turn_x, *turn_y, column, row, table)
-    return partial
+    )(bounds, atoms, *turn_x, *turn_y, column, row, jnp.asarray(table))
 
 
 def convolved_by_lines(charge_mesh, count_x, count_y):
@@ -736,21 +988,27 @@
     cells_x = GRID_X // count_x
     cells_y = GRID_Y // count_y
     cells_z = GRID_Z // count_y
+    by_planes = (
+        GRID_Z == 8 * devices
+        and cells_y == 64
+        and cells_x % 8 == 0
+        and cells_x <= 64
+        and count_y % 2 == 0
+        and atom_total == 8 * lanes
+        and cluster_size % lanes == 0
+    )
+    if by_planes:
+        sizes = (count_x, count_y, cells_x, cells_y)
+        raw, atoms, bounds, rank = shared(positions, charges, atom_counts, *sizes)
+        partial = far_by_planes(bounds, atoms, *sizes)
+        return tuple(finished(pair_lists, partial, raw, rank, *sizes))
     living = jnp.arange(atom_total, dtype=jnp.int32) < atom_counts[0, 0]
     charge = jnp.where(living, charges[0, 0], 0.0)
     packed = jnp.concatenate([positions, charge[None, None, None, :]], axis=0)
     atoms = packed.reshape(4, atom_total)
-
     base = jnp.broadcast_to(
         (slab_dest[0, 0] * cells_z)[:, None], (blocks, block_size)
     ).reshape(1, atom_total)
-    by_planes = GRID_Z % devices == 0 and cells_y == 64 and cells_x % 8 == 0
-    if by_planes:
-        gathered = shared(atoms, count_x, count_y)
-        partial = far_by_planes(gathered, count_x, count_y, cells_x, cells_y)
-        return tuple(
-            finished(pair_lists, partial, gathered, count_x, count_y, cells_x, cells_y)
-        )
     gathered = lax.all_gather(atoms, ("gx", "gy"), axis=0, tiled=False)
     far_part = far_by_lines(atoms, base, count_x, count_y, cells_x, cells_y, cells_z)
 

time: 86.2 us -> 73.8 us (0.86)
  Pallas kernels: 80.7 us -> 69.9 us
  local copies, waits for them, and re-layouts: 3.22 us -> 1.92 us
    pallas_call x1, Pallas kernels: 52.3 us -> 37.5 us  [far_by_planes(): pl.pallas_call(functools.partial(mesh_kernel, (count_x, count_y), (cells_...]
    pallas_call x1, Pallas kernels: 13.4 us -> 17.8 us  [shared(): pl.pallas_call(functools.partial(share_kernel, (count_x, count_y), (cells...]
    dynamic_slice x1 -> x0, local copies, waits for them, and re-layouts: 1.29 us -> none  [far_by_planes(): lax.dynamic_slice_in_dim(jnp.asarray(table), place * depth, depth, axis=0)]
    unnamed x9 -> x4, local copies, waits for them, and re-layouts: 1.93 us -> 1.92 us
where the time goes in v2:
time: 73.8 us; the launch traced here: 73.1 us
  Pallas kernels  69.9 us (95%)
  local copies, waits for them, and re-layouts  1.92 us (3%)
  between operations  1.3 us (2%)
    pallas_call x1, Pallas kernels, far_by_planes(): pl.pallas_call(functools.partial(mesh_kernel, (count_x, count_y), (cells_...  37.5 us
    pallas_call x1, Pallas kernels, shared(): pl.pallas_call(functools.partial(share_kernel, (count_x, count_y), (cells...  17.8 us
    pallas_call x1, Pallas kernels, finished(): pl.pallas_call(functools.partial(finish_kernel, (count_x, count_y), (cell...  14.7 us
    unnamed x4, local copies, waits for them, and re-layouts  1.92 us

profile of v2, /device:TPU:0, one launch (start us, length us, event | category | flops | bytes accessed | tf_op | source)
XLA Modules:
  0.0 73.1 jit_solution(14694404904586841375)
XLA Ops:
  1.3 17.8 %share.1 = (f32[16,4,1024]{2,1,0:T(4,128)}, f32[16,4,8,128]{3,2,1,0:T(8,128)}, s32[16,1,128]{2,1,0:T(1,128)}, f32[1,1024]{1,0:T(1,128)}) custom-call(s32[1,1]{1,0:T(1,128)S(6)} %copy.13.count_ref, f32[3,1,1,1024]{3,2,1,0:T(1,128)} %position_ref.1, f32[1,1,1024]{2,1,0:T(1,128)} %charge_ref.1), custom_call_target="tpu_custom_call" | custom-call | tf_op jit(solution)/shard_map/share/pallas_call | solution.py:317
  19.0 37.5 %mesh.1.partial_ref = f32[16,3,8,128]{3,2,1,0:T(8,128)} custom-call(s32[16,1,128]{2,1,0:T(1,128)} %get-tuple-element.6.bounds_ref, f32[16,4,8,128]{3,2,1,0:T(8,128)} %get-tuple-element.7.atoms_ref, bf16[256,256]{1,0:T(8,128)(2,1)} %constant.16.xh_ref.yh_ref, bf16[256,256]{1,0:T(8,128)(2,1)} %constant.19.xl_ref.yl_ref, ...), custom_call_target="tpu_custom_call" | custom-call | tf_op jit(solution)/shard_map/mesh/pallas_call | solution.py:872
  56.6 14.7 %finish.1 = (f32[3,1,1,1024]{3,2,1,0:T(1,128)}, f32[3,1,1,1024]{3,2,1,0:T(1,128)}) custom-call(s32[1,1,4,4]{3,2,1,0:T(4,128)} %pairs_ref.1, f32[16,3,8,128]{3,2,1,0:T(8,128)} %mesh.1.partial_ref, f32[16,4,1024]{2,1,0:T(4,128)} %get-tuple-element.8.atoms_ref, f32[1,1024]{1,0:T(1,128)} %get-tuple-element.9.rank_ref), custom_call_target="tpu_custom_call" | custom-call | tf_op jit(solution)/shard_map/finish/pallas_call | solution.py:788
  71.2 0.0 copy-start
  71.2 1.3 %copy.14 = f32[3,1,1,1024]{3,2,1,0:T(1,128)} copy(f32[3,1,1,1024]{3,2,1,0:T(1,128)} %get-tuple-element.12) | data formatting | bytes 24576
  72.5 0.0 copy-done
  72.5 0.6 copy.15
Async XLA Ops:
  71.2 1.3 %copy-start = (f32[3,1,1,1024]{3,2,1,0:T(1,128)S(1)}, f32[3,1,1,1024]{3,2,1,0:T(1,128)}, u32[]{:S(2)}) copy-start(f32[3,1,1,1024]{3,2,1,0:T(1,128)} %get-tuple-element.13) | copy-start | bytes 36868

commit v3 on v2

--- a/solution.py
+++ b/solution.py
@@ -24,6 +24,7 @@
 window_rows = 24
 group_size = 4
 plane_group = 2
+fixed_arrays = 7
 
 
 def moved(value, step_x, step_y):
@@ -191,11 +192,120 @@
     return peers
 
 
-def share_kernel(sizes, cells, count_ref, position_ref, charge_ref, raw_ref, sorted_ref, bounds_ref, rank_ref, key_ref, split_ref, raw_send, raw_recv, sort_send, sort_recv, mark_send, mark_recv):
+root_terms = (
+    3.9164407301418542,
+    -0.0037127819564810594,
+    0.16802528315459195,
+    -0.003061234121505335,
+    -0.0076524954798020545,
+    0.002268454833542123,
+    -0.0003056487922112269,
+    1.686888935413571e-05,
+)
+
+
+def pair_weight(square):
+    soft_square = square * (spacing * spacing) + soft_core
+    inverse = lax.rsqrt(soft_square)
+    series = jnp.full_like(inverse, root_terms[-1])
+    for term in root_terms[-2::-1]:
+        series = series * inverse + term
+    decay = jnp.exp(soft_square * (-ewald_split * ewald_split))
+    taper = jnp.maximum(1.0 - square * (spacing * spacing / (cutoff * cutoff)), 0.0)
+    return (decay * series) * (inverse * taper) ** 2
+
+
+def row_sums(values):
+    total = None
+    ones = jnp.ones((16, values.shape[1]), jnp.bfloat16)
+    for _ in range(3):
+        part = values.astype(jnp.bfloat16)
+        values = values - part.astype(jnp.float32)
+        summed = lax.dot_general(
+            ones, part, (((1,), (1,)), ((), ())), preferred_element_type=jnp.float32
+        )
+        total = summed if total is None else total + summed
+    return total[0:1, :]
+
+
+def place_partners(sizes, cells, pairs_ref, atoms_ref, partner_ref, chosen_clusters):
+    count_x, count_y = sizes
+    cells_x, cells_y = cells
+    place_x, place_y = (lax.axis_index("gx"), lax.axis_index("gy"))
+    clusters, listed = pairs_ref.shape[2:]
+    size = atoms_ref.shape[2] // clusters
+    for slot, c in enumerate(chosen_clusters):
+        for n in range(listed):
+            chosen = pairs_ref[0, 0, c, n]
+            beside = lax.div(chosen, clusters)
+            which = chosen - beside * clusters
+            row_x = lax.div(beside, 3)
+            step_x = row_x - 1
+            step_y = beside - row_x * 3 - 1
+            from_x = lax.rem(place_x + step_x + count_x, count_x)
+            from_y = lax.rem(place_y + step_y + count_y, count_y)
+            block = atoms_ref[from_x * count_y + from_y]
+            part = block[:, :size]
+            for k in range(1, clusters):
+                part = jnp.where(which == k, block[:, k * size : (k + 1) * size], part)
+            shifts = (
+                (step_x * cells_x).astype(jnp.float32),
+                (step_y * cells_y).astype(jnp.float32),
+            )
+            for axis in range(4):
+                row = part[axis : axis + 1, :]
+                if axis < 2:
+                    row = row + shifts[axis]
+                partner_ref[slot, axis, :, n * size : (n + 1) * size] = jnp.broadcast_to(
+                    row, (8, size)
+                )
+
+
+def place_columns(me, atoms_ref, column_ref, start):
+    for axis in range(3):
+        for chunk in range(column_ref.shape[1] // lanes):
+            at = start + chunk * lanes
+            row = atoms_ref[me, axis : axis + 1, at : at + lanes]
+            column_ref[axis, chunk * lanes : (chunk + 1) * lanes, :] = jnp.broadcast_to(
+                row, (lanes, lanes)
+            ).T
+
+
+def pair_sums(slot, size, column_ref, partner_ref, sum_ref, out_ref, out_start):
+    @pl.loop(0, size // 16)
+    def _(step):
+        for half in range(2):
+            own_rows = pl.ds(pl.multiple_of(slot * size + step * 16 + half * 8, 8), 8)
+            own = [column_ref[axis, own_rows, :] for axis in range(3)]
+            sums = [jnp.zeros((8, lanes), jnp.float32) for _ in range(3)]
+            for tile in range(partner_ref.shape[3] // lanes):
+                span = slice(tile * lanes, (tile + 1) * lanes)
+                offsets = [own[axis] - partner_ref[slot, axis, :, span] for axis in range(3)]
+                square = sum(offset * offset for offset in offsets)
+                weight = pair_weight(square) * partner_ref[slot, 3, :, span]
+                sums = [total + weight * offset for total, offset in zip(sums, offsets)]
+            rows = pl.ds(pl.multiple_of(step * 16 + half * 8, 8), 8)
+            for axis in range(3):
+                sum_ref[axis, rows, :] = sums[axis]
+
+    for axis in range(3):
+        out_ref[axis : axis + 1, out_start : out_start + size] = row_sums(sum_ref[axis])
+
+
+def share_kernel(sizes, cells, early, count_ref, pairs_ref, position_ref, charge_ref, raw_ref, sorted_ref, bounds_ref, rank_ref, pair_ref, key_ref, split_ref, column_ref, partner_ref, sum_ref, raw_send, raw_recv, sort_send, sort_recv, mark_send, mark_recv):
     count_x, count_y = sizes
     cells_x, _ = cells
     place_x, place_y = (lax.axis_index("gx"), lax.axis_index("gy"))
     me = place_x * count_y + place_y
+    place_chip, place_core = (place_y // 2, lax.rem(place_y, 2))
+    chips = count_y // 2
+
+    def at(step_x, step_chip, flip):
+        peer_x = lax.rem(place_x + step_x, count_x)
+        peer_chip = lax.rem(place_chip + step_chip, chips)
+        peer_core = 1 - place_core if flip else place_core
+        return (peer_x, peer_chip * 2 + peer_core)
+
     peers = peers_of(count_x, count_y)
     barrier = pltpu.get_barrier_semaphore()
     for peer_x, peer_y in peers:
@@ -206,16 +316,31 @@
             device_id_type=pl.DeviceIdType.MESH,
         )
 
-    def sent(source, target, send_sem, recv_sem, order):
-        peer_x, peer_y = peers[order]
+    def sent(ref, owner, peer, send_sem, recv_sem, order, slot):
         return pltpu.make_async_remote_copy(
-            src_ref=source.at[me],
-            dst_ref=target.at[me],
+            src_ref=ref.at[owner],
+            dst_ref=ref.at[owner],
             send_sem=send_sem.at[order],
-            recv_sem=recv_sem.at[order],
-            device_id={"gx": peer_x, "gy": peer_y},
+            recv_sem=recv_sem.at[slot],
+            device_id={"gx": peer[0], "gy": peer[1]},
             device_id_type=pl.DeviceIdType.MESH,
         )
+
+    passed = []
+
+    def passes(owner, peer):
+        order = len(passed)
+        copies = [
+            sent(sorted_ref, owner, peer, sort_send, sort_recv, order, owner),
+            sent(bounds_ref, owner, peer, mark_send, mark_recv, order, owner),
+        ]
+        for copy in copies:
+            copy.start()
+        passed.append(copies)
+
+    def arrives(owner, peer):
+        sent(sorted_ref, owner, peer, sort_send, sort_recv, 0, owner).wait_recv()
+        sent(bounds_ref, owner, peer, mark_send, mark_recv, 0, owner).wait_recv()
 
     atom_total = charge_ref.shape[2]
     tiles = atom_total // lanes
@@ -257,7 +382,10 @@
         }
         - {0}
     )
-    copies = [sent(raw_ref, raw_ref, raw_send, raw_recv, order - 1) for order in beside]
+    copies = [
+        sent(raw_ref, me, peers[order - 1], raw_send, raw_recv, order - 1, order - 1)
+        for order in beside
+    ]
     for copy in copies:
         copy.start()
 
@@ -300,38 +428,84 @@
     marks = jnp.sum(marks, axis=0, keepdims=True)
     bounds_ref[me] = marks.astype(jnp.int32)
 
-    everyone = range(len(peers))
-    later = [sent(sorted_ref, sorted_ref, sort_send, sort_recv, order) for order in everyone]
-    later += [sent(bounds_ref, bounds_ref, mark_send, mark_recv, order) for order in everyone]
-    for copy in later:
-        copy.start()
-    for copy in copies + later:
-        copy.wait()
-
-
-def shared(positions, charges, atom_counts, count_x, count_y, cells_x, cells_y):
+    others = [(step, at(step, 0, False)) for step in range(1, count_x)]
+    for _, peer in others:
+        passes(me, peer)
+    for step in range(1, chips):
+        passes(me, at(0, step, False))
+    passes(me, at(0, 0, True))
+    place_columns(me, raw_ref, column_ref, 0)
+    for copy in copies:
+        copy.wait_recv()
+    place_partners(sizes, cells, pairs_ref, raw_ref, partner_ref, range(early))
+    size = atom_total // pairs_ref.shape[2]
+    stops = [[] for _ in range(max(early, 2))]
+    stops[0] = [(step, 0) for step in range(1, count_x)]
+    stops[1] = [(step, chip) for chip in range(1, chips) for step in range(count_x)]
+    for stage, stop in enumerate(stops):
+        if stage < early:
+            pair_sums(stage, size, column_ref, partner_ref, sum_ref, pair_ref, stage * size)
+        for step, chip in stop:
+            owner_x, owner_y = at(step, chip, False)
+            owner = owner_x * count_y + owner_y
+            arrives(owner, at(step, 0, False) if chip == 0 else at(0, chip, False))
+            if chip == 0:
+                for far in range(1, chips):
+                    passes(owner, at(0, far, False))
+            passes(owner, at(0, 0, True))
+    for step in range(count_x):
+        for chip in range(chips):
+            owner_x, owner_y = at(step, chip, True)
+            arrives(owner_x * count_y + owner_y, at(0, 0, True))
+    for copy in copies:
+        copy.wait_send()
+    for pair in passed:
+        for copy in pair:
+            copy.wait_send()
+
+
+def shared(positions, charges, pair_lists, atom_counts, count_x, count_y, cells_x, cells_y):
     devices = count_x * count_y
     atom_total = charges.shape[2]
+    clusters, listed = pair_lists.shape[2:]
+    size = atom_total // clusters
+    early = clusters // 2
     vmem = pl.BlockSpec(memory_space=pltpu.VMEM)
-    flags = pltpu.SemaphoreType.DMA((devices - 1,))
+    smem = pl.BlockSpec(memory_space=pltpu.SMEM)
+    fewer = pltpu.SemaphoreType.DMA((devices - 1,))
+    flags = pltpu.SemaphoreType.DMA((devices,))
     return pl.pallas_call(
-        functools.partial(share_kernel, (count_x, count_y), (cells_x, cells_y)),
-        in_specs=[pl.BlockSpec(memory_space=pltpu.SMEM), vmem, vmem],
-        out_specs=[vmem] * 4,
+        functools.partial(share_kernel, (count_x, count_y), (cells_x, cells_y), early),
+        in_specs=[smem, smem, vmem, vmem],
+        out_specs=[vmem] * 5,
         out_shape=[
             jax.ShapeDtypeStruct((devices, 4, atom_total), jnp.float32),
             jax.ShapeDtypeStruct((devices, 4, atom_total // lanes, lanes), jnp.float32),
             jax.ShapeDtypeStruct((devices, 1, lanes), jnp.int32),
             jax.ShapeDtypeStruct((1, atom_total), jnp.float32),
+            jax.ShapeDtypeStruct((3, early * size), jnp.float32),
         ],
         scratch_shapes=[
             pltpu.VMEM((atom_total, lanes), jnp.float32),
             pltpu.VMEM((16, atom_total), jnp.float32),
+            pltpu.VMEM((3, early * size, lanes), jnp.float32),
+            pltpu.VMEM((early, 4, 8, listed * size), jnp.float32),
+            pltpu.VMEM((3, size, lanes), jnp.float32),
+            fewer,
+            fewer,
         ]
-        + [flags] * 6,
-        compiler_params=pltpu.CompilerParams(collective_id=0, has_side_effects=True),
+        + [flags] * 4,
+        compiler_params=pltpu.CompilerParams(
+            collective_id=0, has_side_effects=True, vmem_limit_bytes=12 << 20
+        ),
         name="share",
-    )(atom_counts, positions, charges)
+    )(
+        atom_counts,
+        *[
+            pltpu.with_memory_space_constraint(value, pltpu.HBM)
+            for value in (pair_lists, positions, charges)
+        ],
+    )
 
 
 def depth_rows(table, height, terms):
@@ -362,7 +536,17 @@
     return results
 
 
-def mesh_kernel(sizes, cells, pad_y, bounds_ref, atoms_ref, xh_ref, xl_ref, yh_ref, yl_ref, column_ref, row_ref, table_ref, out_ref, mesh_ref, stack_ref, prep_ref, deep_ref, steep_ref, near_ref, wy_ref, side_ref, level_ref, square_ref, scale_ref):
+def mesh_kernel(sizes, cells, pad_y, bounds_ref, atoms_ref, *refs):
+    constants, (out_ref, *scratch) = refs[:fixed_arrays], refs[fixed_arrays:]
+    held, copy_sem = scratch[-fixed_arrays - 1 : -1], scratch[-1]
+    copies = [
+        pltpu.make_async_copy(source, target, copy_sem.at[place])
+        for place, (source, target) in enumerate(zip(constants, held))
+    ]
+    for copy in copies:
+        copy.start()
+    xh_ref, xl_ref, yh_ref, yl_ref, column_ref, row_ref, table_ref = held
+    mesh_ref, stack_ref, prep_ref, deep_ref, steep_ref, near_ref, wy_ref, side_ref, level_ref, square_ref, scale_ref = scratch[: -fixed_arrays - 1]
     count_x, count_y = sizes
     cells_x, cells_y = cells
     devices = count_x * count_y
@@ -377,6 +561,7 @@
     stack_ref[:, GRID_X:, :] = jnp.zeros_like(stack_ref[:, GRID_X:, :])
     out_ref[...] = jnp.zeros_like(out_ref)
     wy_ref[...] = jnp.zeros_like(wy_ref)
+    copies[-1].wait()
     table = table_ref[pl.ds(pl.multiple_of(place * depth, 8), depth), :]
 
     def prep_row(kind, cell, tile):
@@ -523,6 +708,8 @@
 
     plane_lane = lax.broadcasted_iota(jnp.int32, (GRID_X, window), 1)
 
+    for copy in copies[:-1]:
+        copy.wait()
     shape = (GRID_X, GRID_Y)
     square_ref[...] = jnp.broadcast_to(column_ref[:, 0:1], shape) + row_ref[0:1, :]
     scale_ref[...] = jnp.broadcast_to(column_ref[:, 1:2], shape) * row_ref[1:2, :]
@@ -633,45 +820,8 @@
             gather_group(cell, group, i, j)
 
 
-root_terms = (
-    3.9164407301418542,
-    -0.0037127819564810594,
-    0.16802528315459195,
-    -0.003061234121505335,
-    -0.0076524954798020545,
-    0.002268454833542123,
-    -0.0003056487922112269,
-    1.686888935413571e-05,
-)
-
-
-def pair_weight(square):
-    soft_square = square * (spacing * spacing) + soft_core
-    inverse = lax.rsqrt(soft_square)
-    series = jnp.full_like(inverse, root_terms[-1])
-    for term in root_terms[-2::-1]:
-        series = series * inverse + term
-    decay = jnp.exp(soft_square * (-ewald_split * ewald_split))
-    taper = jnp.maximum(1.0 - square * (spacing * spacing / (cutoff * cutoff)), 0.0)
-    return (decay * series) * (inverse * taper) ** 2
-
-
-def row_sums(values):
-    total = None
-    ones = jnp.ones((16, values.shape[1]), jnp.bfloat16)
-    for _ in range(3):
-        part = values.astype(jnp.bfloat16)
-        values = values - part.astype(jnp.float32)
-        summed = lax.dot_general(
-            ones, part, (((1,), (1,)), ((), ())), preferred_element_type=jnp.float32
-        )
-        total = summed if total is None else total + summed
-    return total[0:1, :]
-
-
-def finish_kernel(sizes, cells, pairs_ref, partial_ref, atoms_ref, rank_ref, short_ref, long_ref, land_ref, column_ref, partner_ref, sum_ref, order_ref, force_ref, send_sem, recv_sem):
+def finish_kernel(sizes, cells, early, pairs_ref, partial_ref, atoms_ref, rank_ref, pair_ref, short_ref, long_ref, land_ref, column_ref, partner_ref, sum_ref, late_ref, order_ref, force_ref, send_sem, recv_sem):
     count_x, count_y = sizes
-    cells_x, cells_y = cells
     place_x, place_y = (lax.axis_index("gx"), lax.axis_index("gy"))
     me = place_x * count_y + place_y
     peers = peers_of(count_x, count_y)
@@ -683,41 +833,11 @@
             device_id={"gx": peer_x, "gy": peer_y},
             device_id_type=pl.DeviceIdType.MESH,
         )
-    clusters, listed = pairs_ref.shape[2:]
+    clusters = pairs_ref.shape[2]
     atom_total = atoms_ref.shape[2]
     size = atom_total // clusters
-    for axis in range(3):
-        for chunk in range(atom_total // lanes):
-            row = atoms_ref[me, pl.ds(axis, 1), pl.ds(chunk * lanes, lanes)]
-            column_ref[axis, pl.ds(chunk * lanes, lanes), :] = jnp.broadcast_to(
-                row, (lanes, lanes)
-            ).T
-    for c in range(clusters):
-        for n in range(listed):
-            chosen = pairs_ref[0, 0, c, n]
-            beside = lax.div(chosen, clusters)
-            which = chosen - beside * clusters
-            row_x = lax.div(beside, 3)
-            step_x = row_x - 1
-            step_y = beside - row_x * 3 - 1
-            from_x = lax.rem(place_x + step_x + count_x, count_x)
-            from_y = lax.rem(place_y + step_y + count_y, count_y)
-            block = atoms_ref[from_x * count_y + from_y]
-            part = block[:, :size]
-            for k in range(1, clusters):
-                part = jnp.where(which == k, block[:, k * size : (k + 1) * size], part)
-            shifts = (
-                (step_x * cells_x).astype(jnp.float32),
-                (step_y * cells_y).astype(jnp.float32),
-            )
-            for axis in range(4):
-                row = part[axis : axis + 1, :]
-                if axis < 2:
-                    row = row + shifts[axis]
-                partner_ref[c, axis, :, n * size : (n + 1) * size] = jnp.broadcast_to(
-                    row, (8, size)
-                )
-
+    place_columns(me, atoms_ref, column_ref, early * size)
+    place_partners(sizes, cells, pairs_ref, atoms_ref, partner_ref, range(early, clusters))
     pl.semaphore_wait(barrier, len(peers))
     copies = []
     for order, (peer_x, peer_y) in enumerate(peers):
@@ -731,26 +851,15 @@
         )
         copy.start()
         copies.append(copy)
-
-    @pl.loop(0, clusters)
-    def _(c):
-        @pl.loop(0, size // 8)
-        def _(step):
-            rows = pl.ds(pl.multiple_of(c * size + step * 8, 8), 8)
-            own = [column_ref[axis, rows, :] for axis in range(3)]
-            sums = [jnp.zeros((8, lanes), jnp.float32) for _ in range(3)]
-            for tile in range(listed * size // lanes):
-                span = pl.ds(tile * lanes, lanes)
-                offsets = [own[axis] - partner_ref[c, axis, :, span] for axis in range(3)]
-                square = sum(offset * offset for offset in offsets)
-                weight = pair_weight(square) * partner_ref[c, 3, :, span]
-                sums = [total + weight * offset for total, offset in zip(sums, offsets)]
-            for axis in range(3):
-                sum_ref[axis, rows, :] = sums[axis]
-
+    for slot in range(clusters - early):
+        pair_sums(slot, size, column_ref, partner_ref, sum_ref, late_ref, slot * size)
     own_charge = atoms_ref[me, 3:4, :]
     for axis in range(3):
-        short_ref[axis, 0, :, :] = row_sums(sum_ref[axis]) * (own_charge * spacing)
+        for half, source in enumerate((pair_ref, late_ref)):
+            span = slice(0, early * size) if half == 0 else slice(early * size, atom_total)
+            short_ref[axis, 0, :, span] = source[axis : axis + 1, :] * (
+                own_charge[:, span] * spacing
+            )
     rank = rank_ref[...]
 
     @pl.loop(0, atom_total // size)
@@ -780,29 +889,35 @@
         long_ref[axis, 0, :, :] = placed[axis : axis + 1, :] * (own_charge * (-1.0 / spacing))
 
 
-def finished(pair_lists, partial, raw, rank, count_x, count_y, cells_x, cells_y):
+def finished(pair_lists, partial, raw, rank, pair_part, count_x, count_y, cells_x, cells_y):
     devices, _, atom_total = raw.shape
     clusters, listed = pair_lists.shape[2:]
+    size = atom_total // clusters
+    early = clusters // 2
+    late = clusters - early
     vmem = pl.BlockSpec(memory_space=pltpu.VMEM)
     flags = pltpu.SemaphoreType.DMA((devices - 1,))
     return pl.pallas_call(
-        functools.partial(finish_kernel, (count_x, count_y), (cells_x, cells_y)),
-        in_specs=[pl.BlockSpec(memory_space=pltpu.SMEM), vmem, vmem, vmem],
+        functools.partial(finish_kernel, (count_x, count_y), (cells_x, cells_y), early),
+        in_specs=[pl.BlockSpec(memory_space=pltpu.SMEM), vmem, vmem, vmem, vmem],
         out_specs=[vmem, vmem],
         out_shape=[jax.ShapeDtypeStruct((3, 1, 1, atom_total), jnp.float32)] * 2,
         scratch_shapes=[
             pltpu.VMEM((devices - 1, *partial.shape[1:]), jnp.float32),
-            pltpu.VMEM((3, atom_total, lanes), jnp.float32),
-            pltpu.VMEM((clusters, 4, 8, listed * atom_total // clusters), jnp.float32),
-            pltpu.VMEM((3, atom_total, lanes), jnp.float32),
+            pltpu.VMEM((3, late * size, lanes), jnp.float32),
+            pltpu.VMEM((late, 4, 8, listed * size), jnp.float32),
+            pltpu.VMEM((3, size, lanes), jnp.float32),
+            pltpu.VMEM((3, late * size), jnp.float32),
             pltpu.VMEM((atom_total, atom_total), jnp.bfloat16),
             pltpu.VMEM((16, atom_total), jnp.float32),
             flags,
             flags,
         ],
-        compiler_params=pltpu.CompilerParams(collective_id=1, has_side_effects=True),
+        compiler_params=pltpu.CompilerParams(
+            collective_id=1, has_side_effects=True, vmem_limit_bytes=16 << 20
+        ),
         name="finish",
-    )(pair_lists, partial, raw, rank)
+    )(pair_lists, partial, raw, rank, pair_part)
 
 
 def green_table(period):
@@ -869,9 +984,11 @@
     vmem = pl.BlockSpec(memory_space=pltpu.VMEM)
     rows = GRID_X + window_rows
     batch = depth * window_rows
+    constants = (*turn_x, *turn_y, column, row, jnp.asarray(table))
+    fixed = pl.BlockSpec(memory_space=pltpu.HBM)
     return pl.pallas_call(
         functools.partial(mesh_kernel, (count_x, count_y), (cells_x, cells_y), pad_y),
-        in_specs=[pl.BlockSpec(memory_space=pltpu.SMEM)] + [vmem] * 8,
+        in_specs=[pl.BlockSpec(memory_space=pltpu.SMEM)] + [vmem] + [fixed] * fixed_arrays,
         out_specs=vmem,
         out_shape=jax.ShapeDtypeStruct((devices, 3, tiles, lanes), jnp.float32),
         scratch_shapes=[
@@ -886,9 +1003,14 @@
             pltpu.VMEM((group_size, batch, 2 * lanes), jnp.float32),
             pltpu.VMEM((GRID_X, GRID_Y), jnp.float32),
             pltpu.VMEM((GRID_X, GRID_Y), jnp.float32),
+            *[pltpu.VMEM(value.shape, value.dtype) for value in constants],
+            pltpu.SemaphoreType.DMA((fixed_arrays,)),
         ],
+        compiler_params=pltpu.CompilerParams(vmem_limit_bytes=36 << 20),
         name="mesh",
-    )(bounds, atoms, *turn_x, *turn_y, column, row, jnp.asarray(table))
+    )(
+        bounds, atoms, *[pltpu.with_memory_space_constraint(value, pltpu.HBM) for value in constants]
+    )
 
 
 def convolved_by_lines(charge_mesh, count_x, count_y):
@@ -994,14 +1116,17 @@
         and cells_x % 8 == 0
         and cells_x <= 64
         and count_y % 2 == 0
+        and clusters % 2 == 0
         and atom_total == 8 * lanes
         and cluster_size % lanes == 0
     )
     if by_planes:
         sizes = (count_x, count_y, cells_x, cells_y)
-        raw, atoms, bounds, rank = shared(positions, charges, atom_counts, *sizes)
+        raw, atoms, bounds, rank, pair_part = shared(
+            positions, charges, pair_lists, atom_counts, *sizes
+        )
         partial = far_by_planes(bounds, atoms, *sizes)
-        return tuple(finished(pair_lists, partial, raw, rank, *sizes))
+        return tuple(finished(pair_lists, partial, raw, rank, pair_part, *sizes))
     living = jnp.arange(atom_total, dtype=jnp.int32) < atom_counts[0, 0]
     charge = jnp.where(living, charges[0, 0], 0.0)
     packed = jnp.concatenate([positions, charge[None, None, None, :]], axis=0)

time: 73.8 us -> 69 us (0.935); the launches traced: 73.1 us -> 69.4 us
  Pallas kernels: 69.9 us -> 66.9 us
    pallas_call x1, Pallas kernels: 14.7 us -> 9.68 us  [finished(): pl.pallas_call(functools.partial(finish_kernel, (count_x, count_y), (cell...]
    pallas_call x1, Pallas kernels: 37.5 us -> 39.1 us  [far_by_planes(): pl.pallas_call(functools.partial(mesh_kernel, (count_x, count_y), (cells_...]
where the time goes in v3:
time: 69 us; the launch traced here: 69.4 us
  Pallas kernels  66.9 us (97%)
  between operations  1.32 us (2%)
  local copies, waits for them, and re-layouts  1.21 us (2%)
    pallas_call x1, Pallas kernels, far_by_planes(): pl.pallas_call(functools.partial(mesh_kernel, (count_x, count_y), (cells_...  39.1 us
    pallas_call x1, Pallas kernels, shared(): pl.pallas_call(functools.partial(share_kernel, (count_x, count_y), (cells...  18.1 us
    pallas_call x1, Pallas kernels, finished(): pl.pallas_call(functools.partial(finish_kernel, (count_x, count_y), (cell...  9.68 us

profile of v3, /device:TPU:0, one launch (start us, length us, event | category | flops | bytes accessed | tf_op | source)
XLA Modules:
  0.0 69.4 jit_solution(8299573671838375842)
XLA Ops:
  1.3 18.1 %share.1 = (f32[16,4,1024]{2,1,0:T(4,128)S(1)}, f32[16,4,8,128]{3,2,1,0:T(8,128)S(1)}, s32[16,1,128]{2,1,0:T(1,128)S(1)}, f32[1,1024]{1,0:T(1,128)S(1)}, f32[3,512]{1,0:T(4,128)S(1)}) custom-call(s32[1,1]{1,0:T(1,128)S(6)} %copy.13.count_ref, s32[1,1,4,4]{3,2,1,0:T(4,128)} %pairs_ref.3, f32[3,1,1,1024]{3,2,1,0:T(1,128)} %position_ref.1, f32[1,1,1024]{2,1,0:T(1,128)} %charge_ref.1), custom_call_target="tpu_custom_call" | custom-call | tf_op jit(solution)/shard_map/share/pallas_call | solution.py:477
  19.4 0.0 copy-start
  19.4 39.1 %mesh.1.partial_ref = f32[16,3,8,128]{3,2,1,0:T(8,128)S(1)} custom-call(s32[16,1,128]{2,1,0:T(1,128)S(1)} %get-tuple-element.7.bounds_ref, f32[16,4,8,128]{3,2,1,0:T(8,128)S(1)} %get-tuple-element.8.atoms_ref, bf16[256,256]{1,0:T(8,128)(2,1)} %constant.16.refs_0_.refs_2_, bf16[256,256]{1,0:T(8,128)(2,1)} %constant.19.refs_1_.refs_3_, ...), custom_call_target="tpu_custom_call" | custom-call | tf_op jit(solution)/shard_map/mesh/pallas_call | solution.py:989
  58.5 0.0 copy-done
  58.5 9.7 %finish.1 = (f32[3,1,1,1024]{3,2,1,0:T(1,128)S(1)}, f32[3,1,1,1024]{3,2,1,0:T(1,128)S(1)}) custom-call(s32[1,1,4,4]{3,2,1,0:T(4,128)S(1)} %copy-done, f32[16,3,8,128]{3,2,1,0:T(8,128)S(1)} %mesh.1.partial_ref, f32[16,4,1024]{2,1,0:T(4,128)S(1)} %get-tuple-element.9.atoms_ref, f32[1,1024]{1,0:T(1,128)S(1)} %get-tuple-element.10.rank_ref, ...), custom_call_target="tpu_custom_call" | custom-call | tf_op jit(solution)/shard_map/finish/pallas_call | solution.py:900
  68.2 0.6 copy.14
  68.8 0.6 copy.15
Async XLA Ops:
  19.4 39.1 %copy-start = (s32[1,1,4,4]{3,2,1,0:T(4,128)S(1)}, s32[1,1,4,4]{3,2,1,0:T(4,128)}, u32[]{:S(2)}) copy-start(s32[1,1,4,4]{3,2,1,0:T(4,128)} %pairs_ref.3) | copy-start | bytes 196

commit v4 on v3

--- a/solution.py
+++ b/solution.py
@@ -22,7 +22,7 @@
 rows_group = 8
 lanes = 128
 window_rows = 24
-group_size = 4
+group_size = 8
 plane_group = 2
 fixed_arrays = 7
 
@@ -546,7 +546,7 @@
     for copy in copies:
         copy.start()
     xh_ref, xl_ref, yh_ref, yl_ref, column_ref, row_ref, table_ref = held
-    mesh_ref, stack_ref, prep_ref, deep_ref, steep_ref, near_ref, wy_ref, side_ref, level_ref, square_ref, scale_ref = scratch[: -fixed_arrays - 1]
+    mesh_ref, stack_ref, prep_ref, deep_ref, steep_ref, near_ref, wy_ref, side_ref, level_ref, square_ref, scale_ref, work_ref = scratch[: -fixed_arrays - 1]
     count_x, count_y = sizes
     cells_x, cells_y = cells
     devices = count_x * count_y
@@ -555,7 +555,6 @@
     depth = stack_ref.shape[0]
     window = 2 * cells_y
     windows = GRID_Y // window
-    chunks = tiles
     extra = 8
     mesh_ref[...] = jnp.zeros_like(mesh_ref)
     stack_ref[:, GRID_X:, :] = jnp.zeros_like(stack_ref[:, GRID_X:, :])
@@ -564,11 +563,18 @@
     copies[-1].wait()
     table = table_ref[pl.ds(pl.multiple_of(place * depth, 8), depth), :]
 
-    def prep_row(kind, cell, tile):
-        return prep_ref[pl.ds((kind * devices + cell) * tiles + tile, 8, stride=0), :]
-
-    @pl.loop(0, devices)
-    def _(cell):
+    steps_x = window_rows // 8
+    most = (cells_x + 2) // 8 // steps_x + 1
+
+    def prep_row(kind, spot):
+        return prep_ref[pl.ds(kind * devices * tiles + spot, 8, stride=0), :]
+
+    def prepare(cell, total):
+        for tile in range(tiles):
+            for step in range(most):
+                work_ref[total + step] = (cell * tiles + tile) * most + step
+            total = total + bounds_ref[cell, 0, tiles + tile]
+
         def keep(kind, value):
             rows = pl.ds(pl.multiple_of((kind * devices + cell) * tiles, 8), tiles)
             prep_ref[rows, :] = value
@@ -590,12 +596,17 @@
             keep(23 + term, slopes[term])
         keep(27, atoms_ref[cell, 3])
         for tile in range(tiles):
-            height = prep_row(18, cell, tile)
-            terms = [[prep_row(19 + 4 * s + term, cell, tile) for term in range(4)] for s in range(2)]
+            spot = cell * tiles + tile
+            height = prep_row(18, spot)
+            terms = [[prep_row(19 + 4 * s + term, spot) for term in range(4)] for s in range(2)]
             deep, steep = depth_rows(table, height, terms)
-            rows = pl.ds(pl.multiple_of((cell * tiles + tile) * depth, 8), depth)
+            rows = pl.ds(pl.multiple_of(spot * depth, 8), depth)
             deep_ref[rows, :] = deep
             steep_ref[rows, :] = steep
+        return total
+
+    total = lax.fori_loop(0, devices, prepare, jnp.int32(0))
+    rounds = lax.div(total + group_size - 1, group_size)
 
     row_index = lax.broadcasted_iota(jnp.int32, (8, lanes), 0).astype(jnp.float32)
 
@@ -609,26 +620,26 @@
             ]
         return results
 
-    def kinds(first, cell, tile):
-        return [prep_row(first + term, cell, tile) for term in range(4)]
+    def kinds(first, spot):
+        return [prep_row(first + term, spot) for term in range(4)]
 
     stride = round_up(pad_y, 16)
     far_away = 1.0e6
 
-    def window_of(cell, chunk, step):
-        first = bounds_ref[cell, 0, chunk]
-        count = bounds_ref[cell, 0, chunks + chunk]
-        begin = first * 8 + jnp.minimum(step, jnp.maximum(count - 1, 0)) * window_rows
-        base = jnp.where(step < count, begin.astype(jnp.float32), far_away)
-        return (begin, base)
-
-    def window_count(cell, chunk):
-        counts = [bounds_ref[cell, 0, chunks + chunk + place] for place in range(group_size)]
-        return functools.reduce(jnp.maximum, counts)
-
-    def y_table(cell, chunk, kind):
-        lowest = prep_row(9, cell, chunk)
-        terms = kinds(kind, cell, chunk)
+    def task(index):
+        entry = jnp.where(index < total, work_ref[index], 0)
+        spot = lax.div(entry, most)
+        cell = lax.div(spot, tiles)
+        chunk = spot - cell * tiles
+        begin = bounds_ref[cell, 0, chunk] * 8 + (entry - spot * most) * window_rows
+        base = jnp.where(index < total, begin.astype(jnp.float32), far_away)
+        i = lax.div(cell, count_y)
+        rows = pl.ds(pl.multiple_of(i * cells_x + begin, 8), window_rows)
+        return (spot, cell, chunk, cell - i * count_y, rows, base)
+
+    def y_table(spot, kind):
+        lowest = prep_row(9, spot)
+        terms = kinds(kind, spot)
         for group in range(stride // 16):
             pieces = [
                 looked_up(row_index + float(group * 16 + half * 8), lowest, [terms])[0]
@@ -638,65 +649,45 @@
             ]
             yield (slice(group * 16, group * 16 + 16), *halves(jnp.concatenate(pieces, axis=0)))
 
-    steps_x = window_rows // 8
-
-    def spread_group(cell, group, i, m, odd):
-        @pl.loop(0, window_count(cell, group * group_size))
-        def _(step):
-            for place in range(group_size):
-                chunk = group * group_size + place
-                spot = cell * chunks + chunk
-                for rows, high, low in y_table(cell, chunk, 10):
-                    after = slice(window + rows.start, window + rows.stop)
-                    later = slice(stride + rows.start, stride + rows.stop)
-                    wy_ref[place, rows, :lanes] = high
-                    wy_ref[place, rows, lanes:] = high
-                    wy_ref[place, after, :lanes] = low
-                    near_ref[spot, rows, :] = high
-                    near_ref[spot, later, :] = low
-                begin, base = window_of(cell, chunk, step)
-                lowest = prep_row(0, cell, chunk) - base
-                charge = prep_row(27, cell, chunk)
-                terms = [term * charge for term in kinds(1, cell, chunk)]
-                weights = [
-                    looked_up(row_index + float(tile * 8), lowest, [terms])[0]
-                    for tile in range(steps_x)
-                ]
-                modes = [
-                    deep_ref[pl.ds((cell * tiles + chunk) * depth + k, 8, stride=0), :]
-                    for k in range(depth)
-                ]
-                blocks = [weight * mode for mode in modes for weight in weights]
-                for pair in range(len(blocks) // 2):
-                    high, low = halves(
-                        jnp.concatenate(blocks[2 * pair : 2 * pair + 2], axis=0)
-                    )
-                    rows = slice(pair * 16, pair * 16 + 16)
-                    side_ref[place, rows, :lanes] = high
-                    side_ref[place, rows, lanes:] = low
-            totals = []
-            for place in range(group_size):
-                total = lax.dot_general(
-                    side_ref[place],
-                    wy_ref[place],
-                    (((1,), (1,)), ((), ())),
-                    preferred_element_type=jnp.float32,
-                )
-                totals.append(total[:, :window] + total[:, window:])
-            for place, total in enumerate(totals):
-                begin, _ = window_of(cell, group * group_size + place, step)
-                rows = pl.ds(pl.multiple_of(i * cells_x + begin, 8), window_rows)
-                here = pl.ds(pl.multiple_of(m * window, lanes), window)
-                mesh_ref[odd, :, rows, here] += total.reshape(depth, window_rows, window)
-
-    @pl.loop(0, devices)
-    def _(cell):
-        i = lax.div(cell, count_y)
-        j = lax.rem(cell, count_y)
-
-        @pl.loop(0, chunks // group_size)
-        def _(group):
-            spread_group(cell, group, i, lax.div(j, 2), lax.rem(j, 2))
+    @pl.loop(0, rounds)
+    def _(turn):
+        tasks = [task(turn * group_size + place) for place in range(group_size)]
+        for place, (spot, _, _, _, _, base) in enumerate(tasks):
+            for rows, high, low in y_table(spot, 10):
+                after = slice(window + rows.start, window + rows.stop)
+                later = slice(stride + rows.start, stride + rows.stop)
+                wy_ref[place, rows, :lanes] = high
+                wy_ref[place, rows, lanes:] = high
+                wy_ref[place, after, :lanes] = low
+                near_ref[spot, rows, :] = high
+                near_ref[spot, later, :] = low
+            lowest = prep_row(0, spot) - base
+            charge = prep_row(27, spot)
+            terms = [term * charge for term in kinds(1, spot)]
+            weights = [
+                looked_up(row_index + float(tile * 8), lowest, [terms])[0]
+                for tile in range(steps_x)
+            ]
+            modes = [
+                deep_ref[pl.ds(spot * depth + k, 8, stride=0), :] for k in range(depth)
+            ]
+            blocks = [weight * mode for mode in modes for weight in weights]
+            for pair in range(len(blocks) // 2):
+                high, low = halves(jnp.concatenate(blocks[2 * pair : 2 * pair + 2], axis=0))
+                rows = slice(pair * 16, pair * 16 + 16)
+                side_ref[place, rows, :lanes] = high
+                side_ref[place, rows, lanes:] = low
+        for place, (_, _, _, j, rows, _) in enumerate(tasks):
+            product = lax.dot_general(
+                side_ref[place],
+                wy_ref[place],
+                (((1,), (1,)), ((), ())),
+                preferred_element_type=jnp.float32,
+            )
+            product = product[:, :window] + product[:, window:]
+            m = lax.div(j, 2)
+            here = pl.ds(pl.multiple_of(m * window, lanes), window)
+            mesh_ref[j - 2 * m, :, rows, here] += product.reshape(depth, window_rows, window)
 
     def across(value):
         high, low = halves(value)
@@ -750,74 +741,56 @@
         for inner in range(plane_group):
             one_plane(pair * plane_group + inner)
 
-    def gather_group(cell, group, i, j):
-        @pl.loop(0, window_count(cell, group * group_size))
-        def _(step):
-            blank = jnp.zeros((2 * window - 3 * stride, lanes), jnp.bfloat16)
-            for place in range(group_size):
-                chunk = group * group_size + place
-                near = near_ref[cell * chunks + chunk]
-                highs, lows = [], []
-                for _, high, low in y_table(cell, chunk, 14):
-                    highs.append(high)
-                    lows.append(low)
-                columns = jnp.concatenate(
-                    [
-                        jnp.concatenate([near, near[:stride], blank], axis=0),
-                        jnp.concatenate([*highs, *lows, *highs, blank], axis=0),
-                    ],
-                    axis=1,
+    @pl.loop(0, rounds)
+    def _(turn):
+        tasks = [task(turn * group_size + place) for place in range(group_size)]
+        blank = jnp.zeros((2 * window - 3 * stride, lanes), jnp.bfloat16)
+        for place, (spot, _, _, j, rows, _) in enumerate(tasks):
+            near = near_ref[spot]
+            highs, lows = [], []
+            for _, high, low in y_table(spot, 14):
+                highs.append(high)
+                lows.append(low)
+            columns = jnp.concatenate(
+                [
+                    jnp.concatenate([near, near[:stride], blank], axis=0),
+                    jnp.concatenate([*highs, *lows, *highs, blank], axis=0),
+                ],
+                axis=1,
+            )
+            span = pl.ds(pl.multiple_of(j * 2 * window, lanes), 2 * window)
+            block = stack_ref[:, rows, span].reshape(depth * window_rows, 2 * window)
+            level_ref[place] = dot(block.astype(jnp.bfloat16), columns)
+        for place, (spot, cell, chunk, _, _, base) in enumerate(tasks):
+            lowest = prep_row(0, spot) - base
+            values = kinds(1, spot)
+            slopes = kinds(5, spot)
+            modes = [pl.ds(spot * depth + k, 8, stride=0) for k in range(depth)]
+            deep = [deep_ref[mode, :] for mode in modes]
+            steep = [steep_ref[mode, :] for mode in modes]
+            zero = jnp.zeros((8, lanes), jnp.float32)
+            sums = [zero, zero, zero]
+            for tile in range(steps_x):
+                weight, slope = looked_up(row_index + float(tile * 8), lowest, [values, slopes])
+                parts = [zero, zero, zero]
+                for k in range(depth):
+                    at = slice(k * window_rows + tile * 8, k * window_rows + tile * 8 + 8)
+                    flat = level_ref[place, at, :lanes]
+                    tilt = level_ref[place, at, lanes:]
+                    parts = [
+                        parts[0] + deep[k] * flat,
+                        parts[1] + deep[k] * tilt,
+                        parts[2] + steep[k] * flat,
+                    ]
+                sums = [
+                    sums[0] + slope * parts[0],
+                    sums[1] + weight * parts[1],
+                    sums[2] + weight * parts[2],
+                ]
+            for axis in range(3):
+                out_ref[cell, axis, pl.ds(chunk, 1), :] += jnp.sum(
+                    sums[axis], axis=0, keepdims=True
                 )
-                begin, _ = window_of(cell, chunk, step)
-                rows = pl.ds(pl.multiple_of(i * cells_x + begin, 8), window_rows)
-                span = pl.ds(pl.multiple_of(j * 2 * window, lanes), 2 * window)
-                block = stack_ref[:, rows, span].reshape(depth * window_rows, 2 * window)
-                level_ref[place] = dot(block.astype(jnp.bfloat16), columns)
-            for place in range(group_size):
-                chunk = group * group_size + place
-                _, base = window_of(cell, chunk, step)
-                lowest = prep_row(0, cell, chunk) - base
-                values = kinds(1, cell, chunk)
-                slopes = kinds(5, cell, chunk)
-                spots = [
-                    pl.ds((cell * tiles + chunk) * depth + k, 8, stride=0) for k in range(depth)
-                ]
-                deep = [deep_ref[spot, :] for spot in spots]
-                steep = [steep_ref[spot, :] for spot in spots]
-                zero = jnp.zeros((8, lanes), jnp.float32)
-                sums = [zero, zero, zero]
-                for tile in range(steps_x):
-                    weight, slope = looked_up(
-                        row_index + float(tile * 8), lowest, [values, slopes]
-                    )
-                    parts = [zero, zero, zero]
-                    for k in range(depth):
-                        at = slice(k * window_rows + tile * 8, k * window_rows + tile * 8 + 8)
-                        flat = level_ref[place, at, :lanes]
-                        tilt = level_ref[place, at, lanes:]
-                        parts = [
-                            parts[0] + deep[k] * flat,
-                            parts[1] + deep[k] * tilt,
-                            parts[2] + steep[k] * flat,
-                        ]
-                    sums = [
-                        sums[0] + slope * parts[0],
-                        sums[1] + weight * parts[1],
-                        sums[2] + weight * parts[2],
-                    ]
-                for axis in range(3):
-                    out_ref[cell, axis, pl.ds(chunk, 1), :] += jnp.sum(
-                        sums[axis], axis=0, keepdims=True
-                    )
-
-    @pl.loop(0, devices)
-    def _(cell):
-        i = lax.div(cell, count_y)
-        j = lax.rem(cell, count_y)
-
-        @pl.loop(0, chunks // group_size)
-        def _(group):
-            gather_group(cell, group, i, j)
 
 
 def finish_kernel(sizes, cells, early, pairs_ref, partial_ref, atoms_ref, rank_ref, pair_ref, short_ref, long_ref, land_ref, column_ref, partner_ref, sum_ref, late_ref, order_ref, force_ref, send_sem, recv_sem):
@@ -1003,6 +976,7 @@
             pltpu.VMEM((group_size, batch, 2 * lanes), jnp.float32),
             pltpu.VMEM((GRID_X, GRID_Y), jnp.float32),
             pltpu.VMEM((GRID_X, GRID_Y), jnp.float32),
+            pltpu.SMEM((4 * devices * tiles,), jnp.int32),
             *[pltpu.VMEM(value.shape, value.dtype) for value in constants],
             pltpu.SemaphoreType.DMA((fixed_arrays,)),
         ],

time: 69 us -> 59.6 us (0.86); the launches traced: 69.4 us -> 58.8 us
  Pallas kernels: 66.9 us -> 56.3 us
    pallas_call x1, Pallas kernels: 39.1 us -> 28.5 us  [far_by_planes(): pl.pallas_call(functools.partial(mesh_kernel, (count_x, count_y), (cells_...]
where the time goes in v4:
time: 59.6 us; the launch traced here: 58.8 us
  Pallas kernels  56.3 us (94%)
  between operations  1.32 us (2%)
  local copies, waits for them, and re-layouts  1.21 us (2%)
    pallas_call x1, Pallas kernels, far_by_planes(): pl.pallas_call(functools.partial(mesh_kernel, (count_x, count_y), (cells_...  28.5 us
    pallas_call x1, Pallas kernels, shared(): pl.pallas_call(functools.partial(share_kernel, (count_x, count_y), (cells...  18.1 us
    pallas_call x1, Pallas kernels, finished(): pl.pallas_call(functools.partial(finish_kernel, (count_x, count_y), (cell...  9.69 us
    unnamed x4, local copies, waits for them, and re-layouts  1.21 us

profile of v4, /device:TPU:0, one launch (start us, length us, event | category | flops | bytes accessed | tf_op | source)
XLA Modules:
  0.0 58.8 jit_solution(16673918816045361523)
XLA Ops:
  1.3 18.1 %share.1 = (f32[16,4,1024]{2,1,0:T(4,128)S(1)}, f32[16,4,8,128]{3,2,1,0:T(8,128)S(1)}, s32[16,1,128]{2,1,0:T(1,128)S(1)}, f32[1,1024]{1,0:T(1,128)S(1)}, f32[3,512]{1,0:T(4,128)S(1)}) custom-call(s32[1,1]{1,0:T(1,128)S(6)} %copy.13.count_ref, s32[1,1,4,4]{3,2,1,0:T(4,128)} %pairs_ref.3, f32[3,1,1,1024]{3,2,1,0:T(1,128)} %position_ref.1, f32[1,1,1024]{2,1,0:T(1,128)} %charge_ref.1), custom_call_target="tpu_custom_call" | custom-call | tf_op jit(solution)/shard_map/share/pallas_call | solution.py:477
  19.4 0.0 copy-start
  19.4 28.5 %mesh.1.partial_ref = f32[16,3,8,128]{3,2,1,0:T(8,128)S(1)} custom-call(s32[16,1,128]{2,1,0:T(1,128)S(1)} %get-tuple-element.7.bounds_ref, f32[16,4,8,128]{3,2,1,0:T(8,128)S(1)} %get-tuple-element.8.atoms_ref, bf16[256,256]{1,0:T(8,128)(2,1)} %constant.16.refs_0_.refs_2_, bf16[256,256]{1,0:T(8,128)(2,1)} %constant.19.refs_1_.refs_3_, ...), custom_call_target="tpu_custom_call" | custom-call | tf_op jit(solution)/shard_map/mesh/pallas_call | solution.py:962
  47.9 0.0 copy-done
  47.9 9.7 %finish.1 = (f32[3,1,1,1024]{3,2,1,0:T(1,128)S(1)}, f32[3,1,1,1024]{3,2,1,0:T(1,128)S(1)}) custom-call(s32[1,1,4,4]{3,2,1,0:T(4,128)S(1)} %copy-done, f32[16,3,8,128]{3,2,1,0:T(8,128)S(1)} %mesh.1.partial_ref, f32[16,4,1024]{2,1,0:T(4,128)S(1)} %get-tuple-element.9.atoms_ref, f32[1,1024]{1,0:T(1,128)S(1)} %get-tuple-element.10.rank_ref, ...), custom_call_target="tpu_custom_call" | custom-call | tf_op jit(solution)/shard_map/finish/pallas_call | solution.py:873
  57.6 0.6 %copy.14 = f32[3,1,1,1024]{3,2,1,0:T(1,128)} copy(f32[3,1,1,1024]{3,2,1,0:T(1,128)S(1)} %get-tuple-element.14) | data formatting | bytes 24576
  58.2 0.6 %copy.15 = f32[3,1,1,1024]{3,2,1,0:T(1,128)} copy(f32[3,1,1,1024]{3,2,1,0:T(1,128)S(1)} %get-tuple-element.15) | data formatting | bytes 24576
Async XLA Ops:
  19.4 28.6 %copy-start = (s32[1,1,4,4]{3,2,1,0:T(4,128)S(1)}, s32[1,1,4,4]{3,2,1,0:T(4,128)}, u32[]{:S(2)}) copy-start(s32[1,1,4,4]{3,2,1,0:T(4,128)} %pairs_ref.3) | copy-start | bytes 196

commit v5 on v4

--- a/solution.py
+++ b/solution.py
@@ -23,7 +23,8 @@
 lanes = 128
 window_rows = 24
 group_size = 8
-plane_group = 2
+cell_group = 2
+plane_group = 4
 fixed_arrays = 7
 
 
@@ -228,14 +229,14 @@
     return total[0:1, :]
 
 
-def place_partners(sizes, cells, pairs_ref, atoms_ref, partner_ref, chosen_clusters):
+def place_partners(sizes, cells, pairs_ref, atoms_ref, partner_ref):
     count_x, count_y = sizes
     cells_x, cells_y = cells
     place_x, place_y = (lax.axis_index("gx"), lax.axis_index("gy"))
     clusters, listed = pairs_ref.shape[2:]
     size = atoms_ref.shape[2] // clusters
-    for slot, c in enumerate(chosen_clusters):
-        for n in range(listed):
+    for c in range(clusters):
+        for n in range(1, listed):
             chosen = pairs_ref[0, 0, c, n]
             beside = lax.div(chosen, clusters)
             which = chosen - beside * clusters
@@ -256,43 +257,37 @@
                 row = part[axis : axis + 1, :]
                 if axis < 2:
                     row = row + shifts[axis]
-                partner_ref[slot, axis, :, n * size : (n + 1) * size] = jnp.broadcast_to(
+                partner_ref[c, axis, :, (n - 1) * size : n * size] = jnp.broadcast_to(
                     row, (8, size)
                 )
 
 
-def place_columns(me, atoms_ref, column_ref, start):
-    for axis in range(3):
-        for chunk in range(column_ref.shape[1] // lanes):
-            at = start + chunk * lanes
-            row = atoms_ref[me, axis : axis + 1, at : at + lanes]
-            column_ref[axis, chunk * lanes : (chunk + 1) * lanes, :] = jnp.broadcast_to(
-                row, (lanes, lanes)
-            ).T
-
-
-def pair_sums(slot, size, column_ref, partner_ref, sum_ref, out_ref, out_start):
-    @pl.loop(0, size // 16)
-    def _(step):
-        for half in range(2):
-            own_rows = pl.ds(pl.multiple_of(slot * size + step * 16 + half * 8, 8), 8)
-            own = [column_ref[axis, own_rows, :] for axis in range(3)]
-            sums = [jnp.zeros((8, lanes), jnp.float32) for _ in range(3)]
-            for tile in range(partner_ref.shape[3] // lanes):
-                span = slice(tile * lanes, (tile + 1) * lanes)
-                offsets = [own[axis] - partner_ref[slot, axis, :, span] for axis in range(3)]
-                square = sum(offset * offset for offset in offsets)
-                weight = pair_weight(square) * partner_ref[slot, 3, :, span]
-                sums = [total + weight * offset for total, offset in zip(sums, offsets)]
-            rows = pl.ds(pl.multiple_of(step * 16 + half * 8, 8), 8)
-            for axis in range(3):
-                sum_ref[axis, rows, :] = sums[axis]
-
-    for axis in range(3):
-        out_ref[axis : axis + 1, out_start : out_start + size] = row_sums(sum_ref[axis])
-
-
-def share_kernel(sizes, cells, early, count_ref, pairs_ref, position_ref, charge_ref, raw_ref, sorted_ref, bounds_ref, rank_ref, pair_ref, key_ref, split_ref, column_ref, partner_ref, sum_ref, raw_send, raw_recv, sort_send, sort_recv, mark_send, mark_recv):
+def pair_sums(clusters, size, height, column_ref, partner_ref, before_ref, sum_ref):
+    @pl.loop(0, clusters)
+    def _(c):
+        @pl.loop(0, size // height)
+        def _(step):
+            for part in range(height // 8):
+                start = c * size + step * height + part * 8
+                rows = pl.ds(pl.multiple_of(start, 8), 8)
+                own = [column_ref[axis, rows, :] for axis in range(3)]
+                sums = [
+                    jnp.zeros((8, lanes), jnp.float32)
+                    if before_ref is None
+                    else before_ref[axis, rows, :]
+                    for axis in range(3)
+                ]
+                for tile in range(partner_ref.shape[3] // lanes):
+                    span = slice(tile * lanes, (tile + 1) * lanes)
+                    offsets = [own[axis] - partner_ref[c, axis, :, span] for axis in range(3)]
+                    square = sum(offset * offset for offset in offsets)
+                    weight = pair_weight(square) * partner_ref[c, 3, :, span]
+                    sums = [total + weight * offset for total, offset in zip(sums, offsets)]
+                for axis in range(3):
+                    sum_ref[axis, rows, :] = sums[axis]
+
+
+def share_kernel(sizes, cells, clusters, count_ref, position_ref, charge_ref, raw_ref, sorted_ref, bounds_ref, rank_ref, column_ref, sum_ref, key_ref, split_ref, partner_ref, raw_send, raw_recv, sort_send, sort_recv, mark_send, mark_recv):
     count_x, count_y = sizes
     cells_x, _ = cells
     place_x, place_y = (lax.axis_index("gx"), lax.axis_index("gy"))
@@ -372,22 +367,6 @@
     totals = lax.fori_loop(0, atom_total // 64, count_group, (zero,) * tiles)
     for tile, total in enumerate(totals):
         rank_ref[:, tile * lanes : (tile + 1) * lanes] = jnp.sum(total, axis=0, keepdims=True)
-
-    pl.semaphore_wait(barrier, len(peers))
-    beside = sorted(
-        {
-            step_x % count_x * count_y + step_y % count_y
-            for step_x in (-1, 0, 1)
-            for step_y in (-1, 0, 1)
-        }
-        - {0}
-    )
-    copies = [
-        sent(raw_ref, me, peers[order - 1], raw_send, raw_recv, order - 1, order - 1)
-        for order in beside
-    ]
-    for copy in copies:
-        copy.start()
 
     split_ref[...] = jnp.zeros_like(split_ref)
     rest = raw_ref[me]
@@ -428,69 +407,78 @@
     marks = jnp.sum(marks, axis=0, keepdims=True)
     bounds_ref[me] = marks.astype(jnp.int32)
 
-    others = [(step, at(step, 0, False)) for step in range(1, count_x)]
-    for _, peer in others:
-        passes(me, peer)
-    for step in range(1, chips):
-        passes(me, at(0, step, False))
-    passes(me, at(0, 0, True))
-    place_columns(me, raw_ref, column_ref, 0)
+    near = sorted(
+        (min(step, count_x - step) + min(chip, chips - chip), step, chip)
+        for step in range(count_x)
+        for chip in range(chips)
+    )[1:]
+    mate = at(0, 0, True)
+    pl.semaphore_wait(barrier, len(peers))
+    for _, step, chip in reversed(near):
+        passes(me, at(step, chip, False))
+    passes(me, mate)
+    beside = sorted(
+        {
+            step_x % count_x * count_y + step_y % count_y
+            for step_x in (-1, 0, 1)
+            for step_y in (-1, 0, 1)
+        }
+        - {0}
+    )
+    copies = [
+        sent(raw_ref, me, peers[order - 1], raw_send, raw_recv, order - 1, order - 1)
+        for order in beside
+    ]
     for copy in copies:
-        copy.wait_recv()
-    place_partners(sizes, cells, pairs_ref, raw_ref, partner_ref, range(early))
-    size = atom_total // pairs_ref.shape[2]
-    stops = [[] for _ in range(max(early, 2))]
-    stops[0] = [(step, 0) for step in range(1, count_x)]
-    stops[1] = [(step, chip) for chip in range(1, chips) for step in range(count_x)]
-    for stage, stop in enumerate(stops):
-        if stage < early:
-            pair_sums(stage, size, column_ref, partner_ref, sum_ref, pair_ref, stage * size)
-        for step, chip in stop:
-            owner_x, owner_y = at(step, chip, False)
-            owner = owner_x * count_y + owner_y
-            arrives(owner, at(step, 0, False) if chip == 0 else at(0, chip, False))
-            if chip == 0:
-                for far in range(1, chips):
-                    passes(owner, at(0, far, False))
-            passes(owner, at(0, 0, True))
-    for step in range(count_x):
-        for chip in range(chips):
-            owner_x, owner_y = at(step, chip, True)
-            arrives(owner_x * count_y + owner_y, at(0, 0, True))
+        copy.start()
+
+    for axis in range(3):
+        for tile in range(tiles):
+            span = slice(tile * lanes, (tile + 1) * lanes)
+            column_ref[axis, span, :] = jnp.broadcast_to(rows[axis][:, span], (lanes, lanes)).T
+    size = atom_total // clusters
+    for c in range(clusters):
+        for axis in range(4):
+            row = rows[axis][:, c * size : (c + 1) * size]
+            partner_ref[c, axis] = jnp.broadcast_to(row, (8, size))
+    pair_sums(clusters, size, 64, column_ref, partner_ref, None, sum_ref)
+    for _, step, chip in near:
+        owner_x, owner_y = at(step, chip, False)
+        arrives(owner_x * count_y + owner_y, (owner_x, owner_y))
+        passes(owner_x * count_y + owner_y, mate)
+    for _, step, chip in [(0, 0, 0), *near]:
+        owner_x, owner_y = at(step, chip, True)
+        arrives(owner_x * count_y + owner_y, mate)
     for copy in copies:
-        copy.wait_send()
+        copy.wait()
     for pair in passed:
         for copy in pair:
             copy.wait_send()
 
 
-def shared(positions, charges, pair_lists, atom_counts, count_x, count_y, cells_x, cells_y):
+def shared(positions, charges, atom_counts, clusters, count_x, count_y, cells_x, cells_y):
     devices = count_x * count_y
     atom_total = charges.shape[2]
-    clusters, listed = pair_lists.shape[2:]
-    size = atom_total // clusters
-    early = clusters // 2
     vmem = pl.BlockSpec(memory_space=pltpu.VMEM)
     smem = pl.BlockSpec(memory_space=pltpu.SMEM)
     fewer = pltpu.SemaphoreType.DMA((devices - 1,))
     flags = pltpu.SemaphoreType.DMA((devices,))
     return pl.pallas_call(
-        functools.partial(share_kernel, (count_x, count_y), (cells_x, cells_y), early),
-        in_specs=[smem, smem, vmem, vmem],
-        out_specs=[vmem] * 5,
+        functools.partial(share_kernel, (count_x, count_y), (cells_x, cells_y), clusters),
+        in_specs=[smem, vmem, vmem],
+        out_specs=[vmem] * 6,
         out_shape=[
             jax.ShapeDtypeStruct((devices, 4, atom_total), jnp.float32),
             jax.ShapeDtypeStruct((devices, 4, atom_total // lanes, lanes), jnp.float32),
             jax.ShapeDtypeStruct((devices, 1, lanes), jnp.int32),
             jax.ShapeDtypeStruct((1, atom_total), jnp.float32),
-            jax.ShapeDtypeStruct((3, early * size), jnp.float32),
+            jax.ShapeDtypeStruct((3, atom_total, lanes), jnp.float32),
+            jax.ShapeDtypeStruct((3, atom_total, lanes), jnp.float32),
         ],
         scratch_shapes=[
             pltpu.VMEM((atom_total, lanes), jnp.float32),
             pltpu.VMEM((16, atom_total), jnp.float32),
-            pltpu.VMEM((3, early * size, lanes), jnp.float32),
-            pltpu.VMEM((early, 4, 8, listed * size), jnp.float32),
-            pltpu.VMEM((3, size, lanes), jnp.float32),
+            pltpu.VMEM((clusters, 4, 8, atom_total // clusters), jnp.float32),
             fewer,
             fewer,
         ]
@@ -501,10 +489,7 @@
         name="share",
     )(
         atom_counts,
-        *[
-            pltpu.with_memory_space_constraint(value, pltpu.HBM)
-            for value in (pair_lists, positions, charges)
-        ],
+        *[pltpu.with_memory_space_constraint(value, pltpu.HBM) for value in (positions, charges)],
     )
 
 
@@ -556,10 +541,8 @@
     window = 2 * cells_y
     windows = GRID_Y // window
     extra = 8
-    mesh_ref[...] = jnp.zeros_like(mesh_ref)
     stack_ref[:, GRID_X:, :] = jnp.zeros_like(stack_ref[:, GRID_X:, :])
     out_ref[...] = jnp.zeros_like(out_ref)
-    wy_ref[...] = jnp.zeros_like(wy_ref)
     copies[-1].wait()
     table = table_ref[pl.ds(pl.multiple_of(place * depth, 8), depth), :]
 
@@ -569,12 +552,15 @@
     def prep_row(kind, spot):
         return prep_ref[pl.ds(kind * devices * tiles + spot, 8, stride=0), :]
 
-    def prepare(cell, total):
+    def listed_work(cell, total):
         for tile in range(tiles):
             for step in range(most):
                 work_ref[total + step] = (cell * tiles + tile) * most + step
             total = total + bounds_ref[cell, 0, tiles + tile]
 
+        return total
+
+    def keep_splines(cell):
         def keep(kind, value):
             rows = pl.ds(pl.multiple_of((kind * devices + cell) * tiles, 8), tiles)
             prep_ref[rows, :] = value
@@ -595,6 +581,8 @@
             keep(19 + term, values[term])
             keep(23 + term, slopes[term])
         keep(27, atoms_ref[cell, 3])
+
+    def keep_modes(cell):
         for tile in range(tiles):
             spot = cell * tiles + tile
             height = prep_row(18, spot)
@@ -603,9 +591,23 @@
             rows = pl.ds(pl.multiple_of(spot * depth, 8), depth)
             deep_ref[rows, :] = deep
             steep_ref[rows, :] = steep
+
+    def prepare_some(turn, total):
+        for inner in range(cell_group):
+            cell = turn * cell_group + inner
+            mesh_ref[lax.div(cell, depth), lax.rem(cell, depth)] = jnp.zeros(
+                mesh_ref.shape[2:], jnp.float32
+            )
+            total = listed_work(cell, total)
+        for inner in range(cell_group):
+            keep_splines(turn * cell_group + inner)
+        for inner in range(cell_group):
+            keep_modes(turn * cell_group + inner)
+        place = turn * group_size // (devices // cell_group)
+        wy_ref[place] = jnp.zeros(wy_ref.shape[1:], wy_ref.dtype)
         return total
 
-    total = lax.fori_loop(0, devices, prepare, jnp.int32(0))
+    total = lax.fori_loop(0, devices // cell_group, prepare_some, jnp.int32(0))
     rounds = lax.div(total + group_size - 1, group_size)
 
     row_index = lax.broadcasted_iota(jnp.int32, (8, lanes), 0).astype(jnp.float32)
@@ -698,24 +700,25 @@
         return dot(high, yh_ref[...]) + dot(high, yl_ref[...]) + dot(low, yh_ref[...])
 
     plane_lane = lax.broadcasted_iota(jnp.int32, (GRID_X, window), 1)
-
     for copy in copies[:-1]:
         copy.wait()
     shape = (GRID_X, GRID_Y)
     square_ref[...] = jnp.broadcast_to(column_ref[:, 0:1], shape) + row_ref[0:1, :]
     scale_ref[...] = jnp.broadcast_to(column_ref[:, 1:2], shape) * row_ref[1:2, :]
 
-    def one_plane(k):
+    def charge_of(k):
         charge = mesh_ref[0, k, :GRID_X, :] + pltpu.roll(mesh_ref[1, k, :GRID_X, :], cells_y, 1)
         over = slice(GRID_X, GRID_X + extra)
         beyond = mesh_ref[0, k, over, :] + pltpu.roll(mesh_ref[1, k, over, :], cells_y, 1)
-        charge = jnp.concatenate([charge[:extra] + beyond, charge[extra:]], axis=0)
-        waves = along(across(charge))
+        return jnp.concatenate([charge[:extra] + beyond, charge[extra:]], axis=0)
+
+    def green_of(k):
         mode = pl.ds(place * depth + k, 1)
         square = square_ref[...] + table_ref[mode, 9:10]
         scale = scale_ref[...] * table_ref[mode, 10:11]
-        green = jnp.where(square > 0.0, scale / square, 0.0)
-        plane = across(along(waves * green))
+        return jnp.where(square > 0.0, scale / square, 0.0)
+
+    def place_plane(k, plane):
         for odd in range(2):
             if odd:
                 plane = pltpu.roll(plane, GRID_Y - cells_y, 1)
@@ -738,8 +741,13 @@
 
     @pl.loop(0, depth // plane_group)
     def _(pair):
-        for inner in range(plane_group):
-            one_plane(pair * plane_group + inner)
+        spots = [pair * plane_group + inner for inner in range(plane_group)]
+        values = [across(charge_of(k)) for k in spots]
+        values = [along(value) for value in values]
+        values = [along(value * green_of(k)) for k, value in zip(spots, values)]
+        values = [across(value) for value in values]
+        for k, value in zip(spots, values):
+            place_plane(k, value)
 
     @pl.loop(0, rounds)
     def _(turn):
@@ -793,7 +801,7 @@
                 )
 
 
-def finish_kernel(sizes, cells, early, pairs_ref, partial_ref, atoms_ref, rank_ref, pair_ref, short_ref, long_ref, land_ref, column_ref, partner_ref, sum_ref, late_ref, order_ref, force_ref, send_sem, recv_sem):
+def finish_kernel(sizes, cells, pairs_ref, partial_ref, atoms_ref, rank_ref, column_ref, before_ref, short_ref, long_ref, land_ref, partner_ref, sum_ref, order_ref, force_ref, send_sem, recv_sem):
     count_x, count_y = sizes
     place_x, place_y = (lax.axis_index("gx"), lax.axis_index("gy"))
     me = place_x * count_y + place_y
@@ -809,8 +817,7 @@
     clusters = pairs_ref.shape[2]
     atom_total = atoms_ref.shape[2]
     size = atom_total // clusters
-    place_columns(me, atoms_ref, column_ref, early * size)
-    place_partners(sizes, cells, pairs_ref, atoms_ref, partner_ref, range(early, clusters))
+    place_partners(sizes, cells, pairs_ref, atoms_ref, partner_ref)
     pl.semaphore_wait(barrier, len(peers))
     copies = []
     for order, (peer_x, peer_y) in enumerate(peers):
@@ -824,15 +831,13 @@
         )
         copy.start()
         copies.append(copy)
-    for slot in range(clusters - early):
-        pair_sums(slot, size, column_ref, partner_ref, sum_ref, late_ref, slot * size)
+    pair_sums(clusters, size, 32, column_ref, partner_ref, before_ref, sum_ref)
     own_charge = atoms_ref[me, 3:4, :]
     for axis in range(3):
-        for half, source in enumerate((pair_ref, late_ref)):
-            span = slice(0, early * size) if half == 0 else slice(early * size, atom_total)
-            short_ref[axis, 0, :, span] = source[axis : axis + 1, :] * (
-                own_charge[:, span] * spacing
-            )
+        for c in range(clusters):
+            span = slice(c * size, (c + 1) * size)
+            summed = row_sums(sum_ref[axis, span, :])
+            short_ref[axis, 0, :, span] = summed * (own_charge[:, span] * spacing)
     rank = rank_ref[...]
 
     @pl.loop(0, atom_total // size)
@@ -862,25 +867,21 @@
         long_ref[axis, 0, :, :] = placed[axis : axis + 1, :] * (own_charge * (-1.0 / spacing))
 
 
-def finished(pair_lists, partial, raw, rank, pair_part, count_x, count_y, cells_x, cells_y):
+def finished(pair_lists, partial, raw, rank, columns, before, count_x, count_y, cells_x, cells_y):
     devices, _, atom_total = raw.shape
     clusters, listed = pair_lists.shape[2:]
     size = atom_total // clusters
-    early = clusters // 2
-    late = clusters - early
     vmem = pl.BlockSpec(memory_space=pltpu.VMEM)
     flags = pltpu.SemaphoreType.DMA((devices - 1,))
     return pl.pallas_call(
-        functools.partial(finish_kernel, (count_x, count_y), (cells_x, cells_y), early),
-        in_specs=[pl.BlockSpec(memory_space=pltpu.SMEM), vmem, vmem, vmem, vmem],
+        functools.partial(finish_kernel, (count_x, count_y), (cells_x, cells_y)),
+        in_specs=[pl.BlockSpec(memory_space=pltpu.SMEM)] + [vmem] * 5,
         out_specs=[vmem, vmem],
         out_shape=[jax.ShapeDtypeStruct((3, 1, 1, atom_total), jnp.float32)] * 2,
         scratch_shapes=[
             pltpu.VMEM((devices - 1, *partial.shape[1:]), jnp.float32),
-            pltpu.VMEM((3, late * size, lanes), jnp.float32),
-            pltpu.VMEM((late, 4, 8, listed * size), jnp.float32),
-            pltpu.VMEM((3, size, lanes), jnp.float32),
-            pltpu.VMEM((3, late * size), jnp.float32),
+            pltpu.VMEM((clusters, 4, 8, (listed - 1) * size), jnp.float32),
+            pltpu.VMEM((3, atom_total, lanes), jnp.float32),
             pltpu.VMEM((atom_total, atom_total), jnp.bfloat16),
             pltpu.VMEM((16, atom_total), jnp.float32),
             flags,
@@ -890,7 +891,14 @@
             collective_id=1, has_side_effects=True, vmem_limit_bytes=16 << 20
         ),
         name="finish",
-    )(pair_lists, partial, raw, rank, pair_part)
+    )(
+        pltpu.with_memory_space_constraint(pair_lists, pltpu.HBM),
+        partial,
+        raw,
+        rank,
+        columns,
+        before,
+    )
 
 
 def green_table(period):
@@ -1090,17 +1098,16 @@
         and cells_x % 8 == 0
         and cells_x <= 64
         and count_y % 2 == 0
-        and clusters % 2 == 0
         and atom_total == 8 * lanes
         and cluster_size % lanes == 0
     )
     if by_planes:
         sizes = (count_x, count_y, cells_x, cells_y)
-        raw, atoms, bounds, rank, pair_part = shared(
-            positions, charges, pair_lists, atom_counts, *sizes
+        raw, atoms, bounds, rank, columns, before = shared(
+            positions, charges, atom_counts, clusters, *sizes
         )
         partial = far_by_planes(bounds, atoms, *sizes)
-        return tuple(finished(pair_lists, partial, raw, rank, pair_part, *sizes))
+        return tuple(finished(pair_lists, partial, raw, rank, columns, before, *sizes))
     living = jnp.arange(atom_total, dtype=jnp.int32) < atom_counts[0, 0]
     charge = jnp.where(living, charges[0, 0], 0.0)
     packed = jnp.concatenate([positions, charge[None, None, None, :]], axis=0)

time: 59.6 us -> 51.8 us (0.87); the launches traced: 58.8 us -> 52.5 us
  Pallas kernels: 56.3 us -> 50 us
    pallas_call x1, Pallas kernels: 18.1 us -> 13.8 us  [shared(): pl.pallas_call(functools.partial(share_kernel, (count_x, count_y), (cells...]
    pallas_call x1, Pallas kernels: 28.5 us -> 25.4 us  [far_by_planes(): pl.pallas_call(functools.partial(mesh_kernel, (count_x, count_y), (cells_...]
    pallas_call x1, Pallas kernels: 9.69 us -> 10.7 us  [finished(): pl.pallas_call(functools.partial(finish_kernel, (count_x, count_y), (cell...]
    unnamed x4 -> x2, local copies, waits for them, and re-layouts: 1.21 us -> 1.2 us
where the time goes in v5:
time: 51.8 us; the launch traced here: 52.5 us
  Pallas kernels  50 us (97%)
  between operations  1.3 us (3%)
  local copies, waits for them, and re-layouts  1.2 us (2%)
    pallas_call x1, Pallas kernels, far_by_planes(): pl.pallas_call(functools.partial(mesh_kernel, (count_x, count_y), (cells_...  25.4 us
    pallas_call x1, Pallas kernels, shared(): pl.pallas_call(functools.partial(share_kernel, (count_x, count_y), (cells...  13.8 us
    pallas_call x1, Pallas kernels, finished(): pl.pallas_call(functools.partial(finish_kernel, (count_x, count_y), (cell...  10.7 us
    unnamed x2, local copies, waits for them, and re-layouts  1.2 us

profile of v5, /device:TPU:0, one launch (start us, length us, event | category | flops | bytes accessed | tf_op | source)
XLA Modules:
  0.0 52.5 jit_solution(13262278410561370101)
XLA Ops:
  1.3 13.8 %share.1 = (f32[16,4,1024]{2,1,0:T(4,128)S(1)}, f32[16,4,8,128]{3,2,1,0:T(8,128)S(1)}, s32[16,1,128]{2,1,0:T(1,128)S(1)}, f32[1,1024]{1,0:T(1,128)S(1)}, f32[3,1...) custom-call(s32[1,1]{1,0:T(1,128)S(6)} %copy.13.count_ref, f32[3,1,1,1024]{3,2,1,0:T(1,128)} %position_ref.1, ...), custom_call_target="tpu_custom_call" | custom-call | tf_op jit(solution)/shard_map/share/pallas_call | solution.py:466
  15.1 25.4 %mesh.1.partial_ref = f32[16,3,8,128]{3,2,1,0:T(8,128)S(1)} custom-call(s32[16,1,128]{2,1,0:T(1,128)S(1)} %get-tuple-element.8.bounds_ref, f32[16,4,8,128]{3,2,1,0:T(8,128)S(1)} %get-tuple-element.9.atoms_ref, bf16[256,256]{1,0:T(8,128)(2,1)} %constant.16.refs_0_.refs_2_, bf16[256,256]{1,0:T(8,128)(2,1)} %constant.19.refs_1_.refs_3_, ...), custom_call_target="tpu_custom_call" | custom-call | tf_op jit(solution)/shard_map/mesh/pallas_call | solution.py:970
  40.6 10.7 %finish.1 = (f32[3,1,1,1024]{3,2,1,0:T(1,128)S(1)}, f32[3,1,1,1024]{3,2,1,0:T(1,128)S(1)}) custom-call(s32[1,1,4,4]{3,2,1,0:T(4,128)} %pairs_ref.1, f32[16,3,8,128]{3,2,1,0:T(8,128)S(1)} %mesh.1.partial_ref, f32[16,4,1024]{2,1,0:T(4,128)S(1)} %get-tuple-element.10.atoms_ref, f32[1,1024]{1,0:T(1,128)S(1)} %get-tuple-element.11.rank_ref, ...), custom_call_target="tpu_custom_call" | custom-call | tf_op jit(solution)/shard_map/finish/pallas_call | solution.py:876
  51.3 0.6 %copy.14 = f32[3,1,1,1024]{3,2,1,0:T(1,128)} copy(f32[3,1,1,1024]{3,2,1,0:T(1,128)S(1)} %get-tuple-element.16) | data formatting | bytes 24576
  51.9 0.6 %copy.15 = f32[3,1,1,1024]{3,2,1,0:T(1,128)} copy(f32[3,1,1,1024]{3,2,1,0:T(1,128)S(1)} %get-tuple-element.17) | data formatting | bytes 24576

commit v6 on v5

--- a/solution.py
+++ b/solution.py
@@ -22,10 +22,11 @@
 rows_group = 8
 lanes = 128
 window_rows = 24
-group_size = 8
+group_size = 16
+gather_size = 8
 cell_group = 2
 plane_group = 4
-fixed_arrays = 7
+fixed_arrays = 8
 
 
 def moved(value, step_x, step_y):
@@ -493,26 +494,11 @@
     )
 
 
-def depth_rows(table, height, terms):
+def depth_rows(table, circle, height, terms):
     turns = height * table[:, 0:1]
-    quarter = GRID_Z // 4
-    nearest = jnp.floor(turns * (1.0 / quarter) + 0.5)
-    angle = (turns - nearest * quarter) * (2.0 * math.pi / GRID_Z)
-    quadrant = nearest - 4.0 * jnp.floor(nearest * 0.25)
-    square = angle * angle
-    near_cos = 1.0 + square * (
-        -0.5 + square * (1.0 / 24.0 + square * (-1.0 / 720.0 + square * (1.0 / 40320.0)))
-    )
-    near_sin = angle * (
-        1.0
-        + square
-        * (-1.0 / 6.0 + square * (1.0 / 120.0 + square * (-1.0 / 5040.0 + square / 362880.0)))
-    )
-    odd_turn = (quadrant == 1.0) | (quadrant == 3.0)
-    cosine = jnp.where(odd_turn, near_sin, near_cos)
-    cosine = jnp.where((quadrant == 1.0) | (quadrant == 2.0), -cosine, cosine)
-    sine = jnp.where(odd_turn, near_cos, near_sin)
-    sine = jnp.where(quadrant >= 2.0, -sine, sine)
+    turns = turns - GRID_Z * jnp.floor(turns * (1.0 / GRID_Z))
+    index = turns.astype(jnp.int32)
+    cosine, sine = [jnp.take_along_axis(part, index, axis=1) for part in circle]
     results = []
     for weights in terms:
         even = sum(table[:, 1 + t : 2 + t] * weights[t] for t in range(4))
@@ -530,7 +516,7 @@
     ]
     for copy in copies:
         copy.start()
-    xh_ref, xl_ref, yh_ref, yl_ref, column_ref, row_ref, table_ref = held
+    xh_ref, xl_ref, yh_ref, yl_ref, column_ref, row_ref, circle_ref, table_ref = held
     mesh_ref, stack_ref, prep_ref, deep_ref, steep_ref, near_ref, wy_ref, side_ref, level_ref, square_ref, scale_ref, work_ref = scratch[: -fixed_arrays - 1]
     count_x, count_y = sizes
     cells_x, cells_y = cells
@@ -541,9 +527,12 @@
     window = 2 * cells_y
     windows = GRID_Y // window
     extra = 8
+    share = -(-group_size * cell_group // devices)
     stack_ref[:, GRID_X:, :] = jnp.zeros_like(stack_ref[:, GRID_X:, :])
     out_ref[...] = jnp.zeros_like(out_ref)
+    copies[-2].wait()
     copies[-1].wait()
+    circle = [circle_ref[:8, :], circle_ref[8:, :]]
     table = table_ref[pl.ds(pl.multiple_of(place * depth, 8), depth), :]
 
     steps_x = window_rows // 8
@@ -573,6 +562,9 @@
             for term in range(4):
                 keep(9 * axis + 1 + term, values[term])
                 keep(9 * axis + 5 + term, slopes[term])
+                if axis == 1:
+                    for kind, whole in ((28, values[term]), (32, slopes[term])):
+                        keep(kind + term, whole - whole.astype(jnp.bfloat16).astype(jnp.float32))
         value = atoms_ref[cell, 2]
         height = jnp.floor(value)
         values, slopes = spline_weights(value - height)
@@ -587,7 +579,7 @@
             spot = cell * tiles + tile
             height = prep_row(18, spot)
             terms = [[prep_row(19 + 4 * s + term, spot) for term in range(4)] for s in range(2)]
-            deep, steep = depth_rows(table, height, terms)
+            deep, steep = depth_rows(table, circle, height, terms)
             rows = pl.ds(pl.multiple_of(spot * depth, 8), depth)
             deep_ref[rows, :] = deep
             steep_ref[rows, :] = steep
@@ -603,8 +595,9 @@
             keep_splines(turn * cell_group + inner)
         for inner in range(cell_group):
             keep_modes(turn * cell_group + inner)
-        place = turn * group_size // (devices // cell_group)
-        wy_ref[place] = jnp.zeros(wy_ref.shape[1:], wy_ref.dtype)
+        for inner in range(share):
+            place = jnp.minimum(turn * share + inner, group_size - 1)
+            wy_ref[place] = jnp.zeros(wy_ref.shape[1:], wy_ref.dtype)
         return total
 
     total = lax.fori_loop(0, devices // cell_group, prepare_some, jnp.int32(0))
@@ -639,23 +632,31 @@
         rows = pl.ds(pl.multiple_of(i * cells_x + begin, 8), window_rows)
         return (spot, cell, chunk, cell - i * count_y, rows, base)
 
-    def y_table(spot, kind):
-        lowest = prep_row(9, spot)
-        terms = kinds(kind, spot)
+    packed_index = jnp.concatenate([row_index, row_index + 8.0], axis=0).astype(jnp.bfloat16)
+
+    def packed_row(kind, spot):
+        row = prep_row(kind, spot)
+        return jnp.concatenate([row, row], axis=0).astype(jnp.bfloat16)
+
+    def y_table(spot, kind, low_kind):
+        lowest = packed_row(9, spot)
+        highs = [packed_row(kind + term, spot) for term in range(4)]
+        lows = [packed_row(low_kind + term, spot) for term in range(4)]
+        starts = [lowest + jnp.bfloat16(term) for term in range(4)]
         for group in range(stride // 16):
-            pieces = [
-                looked_up(row_index + float(group * 16 + half * 8), lowest, [terms])[0]
-                if group * 16 + half * 8 < pad_y
-                else jnp.zeros_like(row_index)
-                for half in range(2)
-            ]
-            yield (slice(group * 16, group * 16 + 16), *halves(jnp.concatenate(pieces, axis=0)))
+            points = packed_index + jnp.bfloat16(group * 16)
+            high = low = jnp.zeros_like(points)
+            for term in range(4):
+                hit = points == starts[term]
+                high = jnp.where(hit, highs[term], high)
+                low = jnp.where(hit, lows[term], low)
+            yield (slice(group * 16, group * 16 + 16), high, low)
 
     @pl.loop(0, rounds)
     def _(turn):
         tasks = [task(turn * group_size + place) for place in range(group_size)]
         for place, (spot, _, _, _, _, base) in enumerate(tasks):
-            for rows, high, low in y_table(spot, 10):
+            for rows, high, low in y_table(spot, 10, 28):
                 after = slice(window + rows.start, window + rows.stop)
                 later = slice(stride + rows.start, stride + rows.stop)
                 wy_ref[place, rows, :lanes] = high
@@ -700,7 +701,7 @@
         return dot(high, yh_ref[...]) + dot(high, yl_ref[...]) + dot(low, yh_ref[...])
 
     plane_lane = lax.broadcasted_iota(jnp.int32, (GRID_X, window), 1)
-    for copy in copies[:-1]:
+    for copy in copies[:-2]:
         copy.wait()
     shape = (GRID_X, GRID_Y)
     square_ref[...] = jnp.broadcast_to(column_ref[:, 0:1], shape) + row_ref[0:1, :]
@@ -749,14 +750,14 @@
         for k, value in zip(spots, values):
             place_plane(k, value)
 
-    @pl.loop(0, rounds)
+    @pl.loop(0, lax.div(total + gather_size - 1, gather_size))
     def _(turn):
-        tasks = [task(turn * group_size + place) for place in range(group_size)]
+        tasks = [task(turn * gather_size + place) for place in range(gather_size)]
         blank = jnp.zeros((2 * window - 3 * stride, lanes), jnp.bfloat16)
         for place, (spot, _, _, j, rows, _) in enumerate(tasks):
             near = near_ref[spot]
             highs, lows = [], []
-            for _, high, low in y_table(spot, 14):
+            for _, high, low in y_table(spot, 14, 32):
                 highs.append(high)
                 lows.append(low)
             columns = jnp.concatenate(
@@ -832,12 +833,11 @@
         copy.start()
         copies.append(copy)
     pair_sums(clusters, size, 32, column_ref, partner_ref, before_ref, sum_ref)
-    own_charge = atoms_ref[me, 3:4, :]
     for axis in range(3):
         for c in range(clusters):
             span = slice(c * size, (c + 1) * size)
             summed = row_sums(sum_ref[axis, span, :])
-            short_ref[axis, 0, :, span] = summed * (own_charge[:, span] * spacing)
+            short_ref[axis, 0, :, span] = summed
     rank = rank_ref[...]
 
     @pl.loop(0, atom_total // size)
@@ -864,7 +864,7 @@
     placed = dot(force_ref[...].astype(jnp.bfloat16), order_ref[...])
     placed = (placed[0:4] + placed[4:8]) + placed[8:12]
     for axis in range(3):
-        long_ref[axis, 0, :, :] = placed[axis : axis + 1, :] * (own_charge * (-1.0 / spacing))
+        long_ref[axis, 0, :, :] = placed[axis : axis + 1, :]
 
 
 def finished(pair_lists, partial, raw, rank, columns, before, count_x, count_y, cells_x, cells_y):
@@ -965,7 +965,9 @@
     vmem = pl.BlockSpec(memory_space=pltpu.VMEM)
     rows = GRID_X + window_rows
     batch = depth * window_rows
-    constants = (*turn_x, *turn_y, column, row, jnp.asarray(table))
+    angle = every_k * (2.0 * np.pi / GRID_Z)
+    circle = np.repeat(np.stack([np.cos(angle), np.sin(angle)]), 8, axis=0).astype(np.float32)
+    constants = (*turn_x, *turn_y, column, row, jnp.asarray(circle), jnp.asarray(table))
     fixed = pl.BlockSpec(memory_space=pltpu.HBM)
     return pl.pallas_call(
         functools.partial(mesh_kernel, (count_x, count_y), (cells_x, cells_y), pad_y),
@@ -975,13 +977,13 @@
         scratch_shapes=[
             pltpu.VMEM((2, depth, rows, GRID_Y), jnp.float32),
             pltpu.VMEM((depth, rows, 4 * GRID_Y), jnp.float32),
-            pltpu.VMEM((28 * devices * tiles, lanes), jnp.float32),
+            pltpu.VMEM((36 * devices * tiles, lanes), jnp.float32),
             pltpu.VMEM((devices * tiles * depth, lanes), jnp.float32),
             pltpu.VMEM((devices * tiles * depth, lanes), jnp.float32),
             pltpu.VMEM((devices * tiles, 2 * stride, lanes), jnp.bfloat16),
             pltpu.VMEM((group_size, 2 * window, 2 * lanes), jnp.bfloat16),
             pltpu.VMEM((group_size, batch, 2 * lanes), jnp.bfloat16),
-            pltpu.VMEM((group_size, batch, 2 * lanes), jnp.float32),
+            pltpu.VMEM((gather_size, batch, 2 * lanes), jnp.float32),
             pltpu.VMEM((GRID_X, GRID_Y), jnp.float32),
             pltpu.VMEM((GRID_X, GRID_Y), jnp.float32),
             pltpu.SMEM((4 * devices * tiles,), jnp.int32),
@@ -1094,6 +1096,7 @@
     cells_z = GRID_Z // count_y
     by_planes = (
         GRID_Z == 8 * devices
+        and GRID_Z == lanes
         and cells_y == 64
         and cells_x % 8 == 0
         and cells_x <= 64
@@ -1107,7 +1110,12 @@
             positions, charges, atom_counts, clusters, *sizes
         )
         partial = far_by_planes(bounds, atoms, *sizes)
-        return tuple(finished(pair_lists, partial, raw, rank, columns, before, *sizes))
+        short_sums, long_sums = finished(
+            pair_lists, partial, raw, rank, columns, before, *sizes
+        )
+        living = jnp.arange(atom_total, dtype=jnp.int32) < atom_counts[0, 0]
+        charge = jnp.where(living, charges[0, 0], 0.0)
+        return (short_sums * (charge * spacing), long_sums * (charge * (-1.0 / spacing)))
     living = jnp.arange(atom_total, dtype=jnp.int32) < atom_counts[0, 0]
     charge = jnp.where(living, charges[0, 0], 0.0)
     packed = jnp.concatenate([positions, charge[None, None, None, :]], axis=0)

time: 51.8 us -> 50.3 us (0.971); the launches traced: 52.5 us -> 50 us
  Pallas kernels: 50 us -> 48 us
  local copies, waits for them, and re-layouts: 1.2 us -> 0.01 us
  other arithmetic: 0 us -> 0.63 us
    pallas_call x1, Pallas kernels: 25.4 us -> 23.5 us  [far_by_planes(): pl.pallas_call(functools.partial(mesh_kernel, (count_x, count_y), (cells_...]
    unnamed x2, local copies, waits for them, and re-layouts: 1.2 us -> 0.01 us
    mul x0 -> x2, other arithmetic: none -> 0.63 us  [the longest x1 0.63 us: local(): long_sums * (charge * (-1.0 / spacing))]
where the time goes in v6:
time: 50.3 us; the launch traced here: 50 us
  Pallas kernels  48 us (95%)
  between operations  1.32 us (3%)
  other arithmetic  0.63 us (1%)
    pallas_call x1, Pallas kernels, far_by_planes(): pl.pallas_call(functools.partial(mesh_kernel, (count_x, count_y), (cells_...  23.5 us
    pallas_call x1, Pallas kernels, shared(): pl.pallas_call(functools.partial(share_kernel, (count_x, count_y), (cells...  13.8 us
    pallas_call x1, Pallas kernels, finished(): pl.pallas_call(functools.partial(finish_kernel, (count_x, count_y), (cell...  10.7 us

profile of v6, /device:TPU:0, one launch (start us, length us, event | category | flops | bytes accessed | tf_op | source)
XLA Modules:
  0.0 50.0 jit_solution(11684219014562955595)
XLA Ops:
  1.3 13.8 %share.1 = (f32[16,4,1024]{2,1,0:T(4,128)S(1)}, f32[16,4,8,128]{3,2,1,0:T(8,128)S(1)}, s32[16,1,128]{2,1,0:T(1,128)S(1)}, f32[1,1024]{1,0:T(1,128)S(1)}, f32[3,1...) custom-call(s32[1,1]{1,0:T(1,128)} %copy.12.count_ref, f32[3,1,1,1024]{3,2,1,0:T(1,128)} %position_ref.1, ...), custom_call_target="tpu_custom_call" | custom-call | tf_op jit(solution)/shard_map/share/pallas_call | solution.py:467
  15.1 23.5 %mesh.1.partial_ref = f32[16,3,8,128]{3,2,1,0:T(8,128)S(1)} custom-call(s32[16,1,128]{2,1,0:T(1,128)S(1)} %get-tuple-element.10.bounds_ref, f32[16,4,8,128]{3,2,1,0:T(8,128)S(1)} %get-tuple-element.11.atoms_ref, bf16[256,256]{1,0:T(8,128)(2,1)} %constant.25.refs_0_.refs_2_, bf16[256,256]{1,0:T(8,128)(2,1)} %constant.28.refs_1_.refs_3_, ...), custom_call_target="tpu_custom_call" | custom-call | tf_op jit(solution)/shard_map/mesh/pallas_call | solution.py:972
  38.6 0.0 copy-start
  38.6 10.7 %finish.1 = (f32[3,1,1,1024]{3,2,1,0:T(1,128)S(1)}, f32[3,1,1,1024]{3,2,1,0:T(1,128)S(1)}) custom-call(s32[1,1,4,4]{3,2,1,0:T(4,128)} %pairs_ref.1, f32[16,3,8,128]{3,2,1,0:T(8,128)S(1)} %mesh.1.partial_ref, f32[16,4,1024]{2,1,0:T(4,128)S(1)} %get-tuple-element.12.atoms_ref, f32[1,1024]{1,0:T(1,128)S(1)} %get-tuple-element.13.rank_ref, ...), custom_call_target="tpu_custom_call" | custom-call | tf_op jit(solution)/shard_map/finish/pallas_call | solution.py:876
  49.3 0.0 copy-done
  49.4 0.6 %broadcast_multiply_fusion = (f32[3,1,1,1024]{3,2,1,0:T(1,128)}, f32[3,1,1,1024]{3,2,1,0:T(1,128)}) fusion(f32[3,1,1,1024]{3,2,1,0:T(1,128)S(1)} %get-tuple-element.17, f32[1024]{0:T(1024)S(1)} %get-tuple-element.18, f32[3,1,1,1024]{3,2,1,0:T(1,128)S(1)} %get-tuple-element.16, f32[1024]{0:T(1024)S(1)} %get-tuple-element.19), kind=kLoop, calls=%fused_computation | loop fusion | flops 6144 | bytes 57344 | tf_op jit(solution)/shard_map/mul | solution.py:1118
  (1 shorter events, 0.0 us)
Async XLA Ops:
  38.6 10.7 %copy-start = (f32[1,1,1024]{2,1,0:T(1,128)S(1)}, f32[1,1,1024]{2,1,0:T(1,128)}, u32[]{:S(2)}) copy-start(f32[1,1,1024]{2,1,0:T(1,128)} %charge_ref.1) | copy-start | bytes 12292

commit v7 on v6

--- a/solution.py
+++ b/solution.py
@@ -24,8 +24,8 @@
 window_rows = 24
 group_size = 16
 gather_size = 8
-cell_group = 2
-plane_group = 4
+cell_group = 4
+plane_group = 8
 fixed_arrays = 8
 
 
@@ -743,12 +743,18 @@
     @pl.loop(0, depth // plane_group)
     def _(pair):
         spots = [pair * plane_group + inner for inner in range(plane_group)]
-        values = [across(charge_of(k)) for k in spots]
-        values = [along(value) for value in values]
-        values = [along(value * green_of(k)) for k, value in zip(spots, values)]
-        values = [across(value) for value in values]
-        for k, value in zip(spots, values):
-            place_plane(k, value)
+        stages = [
+            lambda k, _: across(charge_of(k)),
+            lambda k, value: along(value),
+            lambda k, value: along(value * green_of(k)),
+            lambda k, value: across(value),
+            lambda k, value: place_plane(k, value),
+        ]
+        values = [None] * plane_group
+        for wave in range(plane_group + len(stages) - 1):
+            for inner in range(plane_group):
+                if 0 <= wave - inner < len(stages):
+                    values[inner] = stages[wave - inner](spots[inner], values[inner])
 
     @pl.loop(0, lax.div(total + gather_size - 1, gather_size))
     def _(turn):

time: 50.3 us -> 48.7 us (0.968)
  Pallas kernels: 48 us -> 46.3 us
    pallas_call x1, Pallas kernels: 23.5 us -> 21.8 us  [far_by_planes(): pl.pallas_call(functools.partial(mesh_kernel, (count_x, count_y), (cells_...]
where the time goes in v7:
time: 48.7 us; the launch traced here: 48.3 us
  Pallas kernels  46.3 us (95%)
  between operations  1.32 us (3%)
  other arithmetic  0.63 us (1%)
    pallas_call x1, Pallas kernels, far_by_planes(): pl.pallas_call(functools.partial(mesh_kernel, (count_x, count_y), (cells_...  21.8 us
    pallas_call x1, Pallas kernels, shared(): pl.pallas_call(functools.partial(share_kernel, (count_x, count_y), (cells...  13.8 us
    pallas_call x1, Pallas kernels, finished(): pl.pallas_call(functools.partial(finish_kernel, (count_x, count_y), (cell...  10.7 us

profile of v7, /device:TPU:0, one launch (start us, length us, event | category | flops | bytes accessed | tf_op | source)
XLA Modules:
  0.0 48.3 jit_solution(8300961026898691807)
XLA Ops:
  1.3 13.8 %share.1 = (f32[16,4,1024]{2,1,0:T(4,128)S(1)}, f32[16,4,8,128]{3,2,1,0:T(8,128)S(1)}, s32[16,1,128]{2,1,0:T(1,128)S(1)}, f32[1,1024]{1,0:T(1,128)S(1)}, f32[3,1...) custom-call(s32[1,1]{1,0:T(1,128)} %copy.12.count_ref, f32[3,1,1,1024]{3,2,1,0:T(1,128)} %position_ref.1, ...), custom_call_target="tpu_custom_call" | custom-call | tf_op jit(solution)/shard_map/share/pallas_call | solution.py:467
  15.1 21.8 %mesh.1.partial_ref = f32[16,3,8,128]{3,2,1,0:T(8,128)S(1)} custom-call(s32[16,1,128]{2,1,0:T(1,128)S(1)} %get-tuple-element.10.bounds_ref, f32[16,4,8,128]{3,2,1,0:T(8,128)S(1)} %get-tuple-element.11.atoms_ref, bf16[256,256]{1,0:T(8,128)(2,1)} %constant.25.refs_0_.refs_2_, bf16[256,256]{1,0:T(8,128)(2,1)} %constant.28.refs_1_.refs_3_, ...), custom_call_target="tpu_custom_call" | custom-call | tf_op jit(solution)/shard_map/mesh/pallas_call | solution.py:978
  36.9 0.0 copy-start
  36.9 10.7 %finish.1 = (f32[3,1,1,1024]{3,2,1,0:T(1,128)S(1)}, f32[3,1,1,1024]{3,2,1,0:T(1,128)S(1)}) custom-call(s32[1,1,4,4]{3,2,1,0:T(4,128)} %pairs_ref.1, f32[16,3,8,128]{3,2,1,0:T(8,128)S(1)} %mesh.1.partial_ref, f32[16,4,1024]{2,1,0:T(4,128)S(1)} %get-tuple-element.12.atoms_ref, f32[1,1024]{1,0:T(1,128)S(1)} %get-tuple-element.13.rank_ref, ...), custom_call_target="tpu_custom_call" | custom-call | tf_op jit(solution)/shard_map/finish/pallas_call | solution.py:882
  47.6 0.0 copy-done
  47.7 0.6 %broadcast_multiply_fusion = (f32[3,1,1,1024]{3,2,1,0:T(1,128)}, f32[3,1,1,1024]{3,2,1,0:T(1,128)}) fusion(f32[3,1,1,1024]{3,2,1,0:T(1,128)S(1)} %get-tuple-element.17, f32[1024]{0:T(1024)S(1)} %get-tuple-element.18, f32[3,1,1,1024]{3,2,1,0:T(1,128)S(1)} %get-tuple-element.16, f32[1024]{0:T(1024)S(1)} %get-tuple-element.19), kind=kLoop, calls=%fused_computation | loop fusion | flops 6144 | bytes 57344 | tf_op jit(solution)/shard_map/mul | solution.py:1124
  (1 shorter events, 0.0 us)
Async XLA Ops:
  36.9 10.7 %copy-start = (f32[1,1,1024]{2,1,0:T(1,128)S(1)}, f32[1,1,1024]{2,1,0:T(1,128)}, u32[]{:S(2)}) copy-start(f32[1,1,1024]{2,1,0:T(1,128)} %charge_ref.1) | copy-start | bytes 12292

commit v8 on v7

--- a/solution.py
+++ b/solution.py
@@ -530,10 +530,6 @@
     share = -(-group_size * cell_group // devices)
     stack_ref[:, GRID_X:, :] = jnp.zeros_like(stack_ref[:, GRID_X:, :])
     out_ref[...] = jnp.zeros_like(out_ref)
-    copies[-2].wait()
-    copies[-1].wait()
-    circle = [circle_ref[:8, :], circle_ref[8:, :]]
-    table = table_ref[pl.ds(pl.multiple_of(place * depth, 8), depth), :]
 
     steps_x = window_rows // 8
     most = (cells_x + 2) // 8 // steps_x + 1
@@ -593,14 +589,22 @@
             total = listed_work(cell, total)
         for inner in range(cell_group):
             keep_splines(turn * cell_group + inner)
-        for inner in range(cell_group):
-            keep_modes(turn * cell_group + inner)
         for inner in range(share):
             place = jnp.minimum(turn * share + inner, group_size - 1)
             wy_ref[place] = jnp.zeros(wy_ref.shape[1:], wy_ref.dtype)
         return total
 
     total = lax.fori_loop(0, devices // cell_group, prepare_some, jnp.int32(0))
+    copies[-2].wait()
+    copies[-1].wait()
+    circle = [circle_ref[:8, :], circle_ref[8:, :]]
+    table = table_ref[pl.ds(pl.multiple_of(place * depth, 8), depth), :]
+
+    @pl.loop(0, devices // cell_group)
+    def _(turn):
+        for inner in range(cell_group):
+            keep_modes(turn * cell_group + inner)
+
     rounds = lax.div(total + group_size - 1, group_size)
 
     row_index = lax.broadcasted_iota(jnp.int32, (8, lanes), 0).astype(jnp.float32)
@@ -983,9 +987,9 @@
         scratch_shapes=[
             pltpu.VMEM((2, depth, rows, GRID_Y), jnp.float32),
             pltpu.VMEM((depth, rows, 4 * GRID_Y), jnp.float32),
-            pltpu.VMEM((36 * devices * tiles, lanes), jnp.float32),
-            pltpu.VMEM((devices * tiles * depth, lanes), jnp.float32),
-            pltpu.VMEM((devices * tiles * depth, lanes), jnp.float32),
+            pltpu.VMEM((36 * devices * tiles + 8, lanes), jnp.float32),
+            pltpu.VMEM((devices * tiles * depth + 8, lanes), jnp.float32),
+            pltpu.VMEM((devices * tiles * depth + 8, lanes), jnp.float32),
             pltpu.VMEM((devices * tiles, 2 * stride, lanes), jnp.bfloat16),
             pltpu.VMEM((group_size, 2 * window, 2 * lanes), jnp.bfloat16),
             pltpu.VMEM((group_size, batch, 2 * lanes), jnp.bfloat16),

time: 48.7 us -> 48.4 us (level); the launches traced: 48.3 us -> 47.5 us
  Pallas kernels: 46.3 us -> 45.5 us
    pallas_call x1, Pallas kernels: 21.8 us -> 21 us  [far_by_planes(): pl.pallas_call(functools.partial(mesh_kernel, (count_x, count_y), (cells_...]
where the time goes in v8:
time: 48.4 us; the launch traced here: 47.5 us
  Pallas kernels  45.5 us (94%)
  between operations  1.32 us (3%)
  other arithmetic  0.63 us (1%)
    pallas_call x1, Pallas kernels, far_by_planes(): pl.pallas_call(functools.partial(mesh_kernel, (count_x, count_y), (cells_...  21 us
    pallas_call x1, Pallas kernels, shared(): pl.pallas_call(functools.partial(share_kernel, (count_x, count_y), (cells...  13.8 us
    pallas_call x1, Pallas kernels, finished(): pl.pallas_call(functools.partial(finish_kernel, (count_x, count_y), (cell...  10.7 us

profile of v8, /device:TPU:0, one launch (start us, length us, event | category | flops | bytes accessed | tf_op | source)
XLA Modules:
  0.0 47.5 jit_solution(16645454376188217297)
XLA Ops:
  1.3 13.8 %share.1 = (f32[16,4,1024]{2,1,0:T(4,128)S(1)}, f32[16,4,8,128]{3,2,1,0:T(8,128)S(1)}, s32[16,1,128]{2,1,0:T(1,128)S(1)}, f32[1,1024]{1,0:T(1,128)S(1)}, f32[3,1...) custom-call(s32[1,1]{1,0:T(1,128)} %copy.12.count_ref, f32[3,1,1,1024]{3,2,1,0:T(1,128)} %position_ref.1, ...), custom_call_target="tpu_custom_call" | custom-call | tf_op jit(solution)/shard_map/share/pallas_call | solution.py:467
  15.1 21.0 %mesh.1.partial_ref = f32[16,3,8,128]{3,2,1,0:T(8,128)S(1)} custom-call(s32[16,1,128]{2,1,0:T(1,128)S(1)} %get-tuple-element.10.bounds_ref, f32[16,4,8,128]{3,2,1,0:T(8,128)S(1)} %get-tuple-element.11.atoms_ref, bf16[256,256]{1,0:T(8,128)(2,1)} %constant.25.refs_0_.refs_2_, bf16[256,256]{1,0:T(8,128)(2,1)} %constant.28.refs_1_.refs_3_, ...), custom_call_target="tpu_custom_call" | custom-call | tf_op jit(solution)/shard_map/mesh/pallas_call | solution.py:982
  36.1 0.0 copy-start
  36.1 10.7 %finish.1 = (f32[3,1,1,1024]{3,2,1,0:T(1,128)S(1)}, f32[3,1,1,1024]{3,2,1,0:T(1,128)S(1)}) custom-call(s32[1,1,4,4]{3,2,1,0:T(4,128)} %pairs_ref.1, f32[16,3,8,128]{3,2,1,0:T(8,128)S(1)} %mesh.1.partial_ref, f32[16,4,1024]{2,1,0:T(4,128)S(1)} %get-tuple-element.12.atoms_ref, f32[1,1024]{1,0:T(1,128)S(1)} %get-tuple-element.13.rank_ref, ...), custom_call_target="tpu_custom_call" | custom-call | tf_op jit(solution)/shard_map/finish/pallas_call | solution.py:886
  46.9 0.0 copy-done
  46.9 0.6 %broadcast_multiply_fusion = (f32[3,1,1,1024]{3,2,1,0:T(1,128)}, f32[3,1,1,1024]{3,2,1,0:T(1,128)}) fusion(f32[3,1,1,1024]{3,2,1,0:T(1,128)S(1)} %get-tuple-element.17, f32[1024]{0:T(1024)S(1)} %get-tuple-element.18, f32[3,1,1,1024]{3,2,1,0:T(1,128)S(1)} %get-tuple-element.16, f32[1024]{0:T(1024)S(1)} %get-tuple-element.19), kind=kLoop, calls=%fused_computation | loop fusion | flops 6144 | bytes 57344 | tf_op jit(solution)/shard_map/mul | solution.py:1128
  (1 shorter events, 0.0 us)
Async XLA Ops:
  36.1 10.7 %copy-start = (f32[1,1,1024]{2,1,0:T(1,128)S(1)}, f32[1,1,1024]{2,1,0:T(1,128)}, u32[]{:S(2)}) copy-start(f32[1,1,1024]{2,1,0:T(1,128)} %charge_ref.1) | copy-start | bytes 12292

commit v9 on v8

--- a/solution.py
+++ b/solution.py
@@ -23,7 +23,7 @@
 lanes = 128
 window_rows = 24
 group_size = 16
-gather_size = 8
+gather_size = 12
 cell_group = 4
 plane_group = 8
 fixed_arrays = 8

time: 48.4 us -> 48.2 us (level); the launches traced: 47.5 us -> 47.9 us
  Pallas kernels: 45.5 us -> 46 us
where the time goes in v9:
time: 48.2 us; the launch traced here: 47.9 us
  Pallas kernels  46 us (95%)
  between operations  1.32 us (3%)
  other arithmetic  0.63 us (1%)
    pallas_call x1, Pallas kernels, far_by_planes(): pl.pallas_call(functools.partial(mesh_kernel, (count_x, count_y), (cells_...  21.4 us
    pallas_call x1, Pallas kernels, shared(): pl.pallas_call(functools.partial(share_kernel, (count_x, count_y), (cells...  13.8 us
    pallas_call x1, Pallas kernels, finished(): pl.pallas_call(functools.partial(finish_kernel, (count_x, count_y), (cell...  10.7 us

profile of v9, /device:TPU:0, one launch (start us, length us, event | category | flops | bytes accessed | tf_op | source)
XLA Modules:
  0.0 47.9 jit_solution(8266274513565231065)
XLA Ops:
  1.3 13.8 %share.1 = (f32[16,4,1024]{2,1,0:T(4,128)S(1)}, f32[16,4,8,128]{3,2,1,0:T(8,128)S(1)}, s32[16,1,128]{2,1,0:T(1,128)S(1)}, f32[1,1024]{1,0:T(1,128)S(1)}, f32[3,1...) custom-call(s32[1,1]{1,0:T(1,128)} %copy.12.count_ref, f32[3,1,1,1024]{3,2,1,0:T(1,128)} %position_ref.1, ...), custom_call_target="tpu_custom_call" | custom-call | tf_op jit(solution)/shard_map/share/pallas_call | solution.py:467
  15.1 21.4 %mesh.1.partial_ref = f32[16,3,8,128]{3,2,1,0:T(8,128)S(1)} custom-call(s32[16,1,128]{2,1,0:T(1,128)S(1)} %get-tuple-element.10.bounds_ref, f32[16,4,8,128]{3,2,1,0:T(8,128)S(1)} %get-tuple-element.11.atoms_ref, bf16[256,256]{1,0:T(8,128)(2,1)} %constant.25.refs_0_.refs_2_, bf16[256,256]{1,0:T(8,128)(2,1)} %constant.28.refs_1_.refs_3_, ...), custom_call_target="tpu_custom_call" | custom-call | tf_op jit(solution)/shard_map/mesh/pallas_call | solution.py:982
  36.6 0.0 copy-start
  36.6 10.7 %finish.1 = (f32[3,1,1,1024]{3,2,1,0:T(1,128)S(1)}, f32[3,1,1,1024]{3,2,1,0:T(1,128)S(1)}) custom-call(s32[1,1,4,4]{3,2,1,0:T(4,128)} %pairs_ref.1, f32[16,3,8,128]{3,2,1,0:T(8,128)S(1)} %mesh.1.partial_ref, f32[16,4,1024]{2,1,0:T(4,128)S(1)} %get-tuple-element.12.atoms_ref, f32[1,1024]{1,0:T(1,128)S(1)} %get-tuple-element.13.rank_ref, ...), custom_call_target="tpu_custom_call" | custom-call | tf_op jit(solution)/shard_map/finish/pallas_call | solution.py:886
  47.3 0.0 copy-done
  47.3 0.6 %broadcast_multiply_fusion = (f32[3,1,1,1024]{3,2,1,0:T(1,128)}, f32[3,1,1,1024]{3,2,1,0:T(1,128)}) fusion(f32[3,1,1,1024]{3,2,1,0:T(1,128)S(1)} %get-tuple-element.17, f32[1024]{0:T(1024)S(1)} %get-tuple-element.18, f32[3,1,1,1024]{3,2,1,0:T(1,128)S(1)} %get-tuple-element.16, f32[1024]{0:T(1024)S(1)} %get-tuple-element.19), kind=kLoop, calls=%fused_computation | loop fusion | flops 6144 | bytes 57344 | tf_op jit(solution)/shard_map/mul | solution.py:1128
  (1 shorter events, 0.0 us)
Async XLA Ops:
  36.6 10.7 %copy-start = (f32[1,1,1024]{2,1,0:T(1,128)S(1)}, f32[1,1,1024]{2,1,0:T(1,128)}, u32[]{:S(2)}) copy-start(f32[1,1,1024]{2,1,0:T(1,128)} %charge_ref.1) | copy-start | bytes 12292

commit v10 on v8

--- a/solution.py
+++ b/solution.py
@@ -22,7 +22,7 @@
 rows_group = 8
 lanes = 128
 window_rows = 24
-group_size = 16
+group_size = 12
 gather_size = 8
 cell_group = 4
 plane_group = 8

time: 48.4 us -> 48.7 us (level); the launches traced: 47.5 us -> 48.8 us
  Pallas kernels: 45.5 us -> 46.8 us
    pallas_call x1, Pallas kernels: 21 us -> 22.3 us  [far_by_planes(): pl.pallas_call(functools.partial(mesh_kernel, (count_x, count_y), (cells_...]
where the time goes in v10:
time: 48.7 us; the launch traced here: 48.8 us
  Pallas kernels  46.8 us (96%)
  between operations  1.32 us (3%)
  other arithmetic  0.63 us (1%)
    pallas_call x1, Pallas kernels, far_by_planes(): pl.pallas_call(functools.partial(mesh_kernel, (count_x, count_y), (cells_...  22.3 us
    pallas_call x1, Pallas kernels, shared(): pl.pallas_call(functools.partial(share_kernel, (count_x, count_y), (cells...  13.8 us
    pallas_call x1, Pallas kernels, finished(): pl.pallas_call(functools.partial(finish_kernel, (count_x, count_y), (cell...  10.7 us

profile of v10, /device:TPU:0, one launch (start us, length us, event | category | flops | bytes accessed | tf_op | source)
XLA Modules:
  0.0 48.8 jit_solution(66745858107910137)
XLA Ops:
  1.3 13.8 %share.1 = (f32[16,4,1024]{2,1,0:T(4,128)S(1)}, f32[16,4,8,128]{3,2,1,0:T(8,128)S(1)}, s32[16,1,128]{2,1,0:T(1,128)S(1)}, f32[1,1024]{1,0:T(1,128)S(1)}, f32[3,1...) custom-call(s32[1,1]{1,0:T(1,128)} %copy.12.count_ref, f32[3,1,1,1024]{3,2,1,0:T(1,128)} %position_ref.1, ...), custom_call_target="tpu_custom_call" | custom-call | tf_op jit(solution)/shard_map/share/pallas_call | solution.py:467
  15.1 22.3 %mesh.1.partial_ref = f32[16,3,8,128]{3,2,1,0:T(8,128)S(1)} custom-call(s32[16,1,128]{2,1,0:T(1,128)S(1)} %get-tuple-element.10.bounds_ref, f32[16,4,8,128]{3,2,1,0:T(8,128)S(1)} %get-tuple-element.11.atoms_ref, bf16[256,256]{1,0:T(8,128)(2,1)} %constant.25.refs_0_.refs_2_, bf16[256,256]{1,0:T(8,128)(2,1)} %constant.28.refs_1_.refs_3_, ...), custom_call_target="tpu_custom_call" | custom-call | tf_op jit(solution)/shard_map/mesh/pallas_call | solution.py:982
  37.4 0.0 copy-start
  37.4 10.7 %finish.1 = (f32[3,1,1,1024]{3,2,1,0:T(1,128)S(1)}, f32[3,1,1,1024]{3,2,1,0:T(1,128)S(1)}) custom-call(s32[1,1,4,4]{3,2,1,0:T(4,128)} %pairs_ref.1, f32[16,3,8,128]{3,2,1,0:T(8,128)S(1)} %mesh.1.partial_ref, f32[16,4,1024]{2,1,0:T(4,128)S(1)} %get-tuple-element.12.atoms_ref, f32[1,1024]{1,0:T(1,128)S(1)} %get-tuple-element.13.rank_ref, ...), custom_call_target="tpu_custom_call" | custom-call | tf_op jit(solution)/shard_map/finish/pallas_call | solution.py:886
  48.1 0.0 copy-done
  48.2 0.6 %broadcast_multiply_fusion = (f32[3,1,1,1024]{3,2,1,0:T(1,128)}, f32[3,1,1,1024]{3,2,1,0:T(1,128)}) fusion(f32[3,1,1,1024]{3,2,1,0:T(1,128)S(1)} %get-tuple-element.17, f32[1024]{0:T(1024)S(1)} %get-tuple-element.18, f32[3,1,1,1024]{3,2,1,0:T(1,128)S(1)} %get-tuple-element.16, f32[1024]{0:T(1024)S(1)} %get-tuple-element.19), kind=kLoop, calls=%fused_computation | loop fusion | flops 6144 | bytes 57344 | tf_op jit(solution)/shard_map/mul | solution.py:1128
  (1 shorter events, 0.0 us)
Async XLA Ops:
  37.4 10.7 %copy-start = (f32[1,1,1024]{2,1,0:T(1,128)S(1)}, f32[1,1,1024]{2,1,0:T(1,128)}, u32[]{:S(2)}) copy-start(f32[1,1,1024]{2,1,0:T(1,128)} %charge_ref.1) | copy-start | bytes 12292
